TPU v7x, 32 devices: a whole 2x2x4 slice. The times are simulated.
32 devices in a mesh: seq: 4 (over y, x), ctx: 8 (over z, core).
Axes of the slice: x: 2, y: 2, z: 4, core: 2. Of those that a mesh axis runs over, the one named last changes fastest.
Arguments:
- block_in: bfloat16 [4, 1024, 1024], P('seq', 'ctx'), may hold values from -6 to 6
- cotangent: bfloat16 [4, 1024, 1024], P('seq', 'ctx'), may hold values from -6 to 6
- segments: int32 [4, 1024], P('seq', 'ctx'), may hold values from 0 to 3, never falling along the last dimension, each value on 1 to 512 neighbouring positions
- ln_gain: bfloat16 [1024], P(('seq', 'ctx')), may hold values from 0.5 to 1.5
- ln_bias: bfloat16 [1024], P(('seq', 'ctx')), may hold values from -3 to 3
- w_qkv: bfloat16 [1024, 3072], P(('seq', 'ctx')), as said below
- b_qkv: bfloat16 [3072], P(('seq', 'ctx')), may hold values from -3 to 3
- w_out: bfloat16 [1024, 1024], P(('seq', 'ctx')), may hold values from -0.75 to 0.75
- b_out: bfloat16 [1024], P(('seq', 'ctx')), may hold values from -3 to 3
- w_fc1: bfloat16 [1024, 4096], P(('seq', 'ctx')), may hold values from -0.1875 to 0.1875
- b_fc1: bfloat16 [4096], P(('seq', 'ctx')), may hold values from -3 to 3
- w_fc2: bfloat16 [1024, 4096], P(('seq', 'ctx')), may hold values from -0.09375 to 0.09375
- b_fc2: bfloat16 [1024], P(('seq', 'ctx')), may hold values from -3 to 3
Outputs:
- block_out: bfloat16 [4, 1024, 1024], P('seq', 'ctx')
- in_grad: float32 [4, 1024, 1024], P('seq', 'ctx')
- grad_ln_gain: float32 [1024], P(('seq', 'ctx'))
- grad_ln_bias: float32 [1024], P(('seq', 'ctx'))
- grad_w_qkv: float32 [1024, 3072], P(('seq', 'ctx'))
- grad_b_qkv: float32 [3072], P(('seq', 'ctx'))
- grad_w_out: float32 [1024, 1024], P(('seq', 'ctx'))
- grad_b_out: float32 [1024], P(('seq', 'ctx'))
- grad_w_fc1: float32 [1024, 4096], P(('seq', 'ctx'))
- grad_b_fc1: float32 [4096], P(('seq', 'ctx'))
- grad_w_fc2: float32 [1024, 4096], P(('seq', 'ctx'))
- grad_b_fc2: float32 [1024], P(('seq', 'ctx'))
Inputs may be any that keep to these rules, and one draw needn't show every extreme that they name: `segments`: segment ids never fall along a sequence, start at 0 and name 4 documents, each one contiguous run. `w_qkv`: columns are queries, keys, values in that order, each 16 heads of 64 features in a row.
All inputs are finite; a program needn't handle non-finite values.
Results may differ from a plain program's by a relative error of at most 0.0094.
Values may be sent and summed in bfloat16 or wider, within the bound.
No kernel may reach another device: no remote copies, remote signals or barrier semaphores. Data moves between devices by JAX's collectives and lax.ppermute only.
A program may use at most 192 MiB of HBM per device.

v0:
```python
import jax
import jax.numpy as jnp
from jax import lax
from jax.experimental import pallas as pl
from jax.experimental.pallas import tpu as pltpu
from jax.sharding import PartitionSpec as P

HEADS = 16
HEAD_DIM = 64
ROT = 16
HALF = ROT // 2
SMALL = 128

norm_eps = 1e-05
big_negative = -1e30
f32 = jnp.float32
bf16 = jnp.bfloat16


def dot(left, right):
    return lax.dot_general(left, right, (((1,), (0,)), ((), ())), preferred_element_type=f32)


def rows_dot(left, right):
    return lax.dot_general(left, right, (((0,), (0,)), ((), ())), preferred_element_type=f32)


def cols_dot(left, right):
    return lax.dot_general(left, right, (((1,), (1,)), ((), ())), preferred_element_type=f32)


def shape(dims, kind=bf16):
    return jax.ShapeDtypeStruct(dims, kind)


def call(kernel, outs, scratch, scalars, operands, after=(), cost=None):
    vmem = pl.BlockSpec(memory_space=pltpu.VMEM)
    in_specs = (
        [pl.BlockSpec(memory_space=pltpu.SMEM)]
        + [vmem] * len(operands)
        + [pl.BlockSpec(memory_space=pl.ANY)] * len(after)
    )
    count = len(operands)

    def wrapped(*refs):
        kernel(refs[0], *refs[1 : 1 + count], *refs[1 + count + len(after) :])

    flops, moved = cost or (0, 0)
    moved = moved or sum(a.size * a.dtype.itemsize for a in operands)
    results = pl.pallas_call(
        wrapped,
        in_specs=in_specs,
        out_specs=[vmem] * len(outs),
        out_shape=outs,
        scratch_shapes=scratch,
        cost_estimate=pl.CostEstimate(flops=flops, bytes_accessed=moved, transcendentals=0),
    )(scalars, *operands, *after)
    return list(results)


def rows_at(index, count):
    return pl.ds(pl.multiple_of(index * count, count), count)


def roll_lanes(x, shift):
    width = x.shape[1]
    shift = shift % width
    if width % 128 == 0:
        return pltpu.roll(x, shift, 1)
    return jnp.concatenate([x[:, width - shift :], x[:, : width - shift]], axis=1)


CORE, Z, S, SUB, _ = range(5)


def head_lanes(to, part, i, heads, group, lanes, width):
    return part * width + (((to % group) * heads + i) * lanes + to // group) * HEAD_DIM


def pack_call(scalars, group, heads, lanes, w_qkv, w_fc1, w_fc2, vectors, seg):
    share, hidden = w_fc1.shape
    count = group * lanes
    cut = hidden // count
    total = 3 * heads * HEAD_DIM
    width = w_qkv.shape[1] // 3

    def kernel(_, qkv_ref, fc1_ref, fc2_ref, *refs):
        *small_refs, seg_ref, out_ref, small = refs
        small[...] = jnp.zeros_like(small)
        for at, ref in enumerate(small_refs):
            small[at : at + 1, : ref.shape[0]] = ref[...].astype(f32).reshape(1, -1)
        at = len(small_refs)
        small[at : at + 1, : seg_ref.shape[1]] = seg_ref[...].astype(f32)
        rounded = small[...].astype(bf16)
        for to in range(count):
            for part in range(3):
                for i in range(heads):
                    begin = head_lanes(to, part, i, heads, group, lanes, width)
                    put = (part * heads + i) * HEAD_DIM
                    out_ref[to, :, put : put + HEAD_DIM] = qkv_ref[:, begin : begin + HEAD_DIM]
            base = total + SMALL
            out_ref[to, :, total:base] = rounded
            out_ref[to, :, base : base + cut] = fc1_ref[:, to * cut : (to + 1) * cut]
            out_ref[to, :, base + cut :] = fc2_ref[:, to * cut : (to + 1) * cut]

    return call(
        kernel,
        [shape((count, share, total + SMALL + 2 * cut))],
        [pltpu.VMEM((share, SMALL), f32)],
        scalars,
        (w_qkv, w_fc1, w_fc2, *vectors, seg),
    )[0]


def spread_out_call(scalars, pieces, rows, share, width, group, heads):
    seqs = len(pieces)
    lanes = pieces[0].shape[1]
    chunks = -(-width // lanes)

    def kernel(at, *refs):
        in_refs, small_ref, part_refs, stage = refs[:seqs], refs[seqs], refs[seqs + 1 : -1], refs[-1]
        for k, ref in enumerate(in_refs):
            slot = lax.rem(at[S] + k, seqs)
            small_ref[rows_at(slot, rows), :] = ref[:rows, lanes - SMALL :]
            for j in range(chunks):
                upto = min(width - j * lanes, lanes)
                begin = rows + j * share
                stage[slot, :, j * lanes : j * lanes + upto] = ref[begin : begin + share, :upto]
        for k, ref in enumerate(part_refs):
            for i in range(heads):
                ref[i] = stage[(at[SUB] ^ k) * heads + i]

    return call(
        kernel,
        [shape((seqs * rows, SMALL))] + [shape((heads, share, width))] * group,
        [pltpu.VMEM((seqs, share, width), bf16)],
        scalars,
        pieces,
    )


def rope(x, cos_full, low_sin, high_sin, sign):
    return x * cos_full + sign * (
        roll_lanes(x, HALF) * high_sin - roll_lanes(x, -HALF) * low_sin
    )


def scores_of(keys, queries_t, first, begin, here, limit):
    raw = dot(keys[:limit], queries_t[:, begin : begin + here])
    key_at = lax.broadcasted_iota(jnp.int32, raw.shape, 0)
    query_at = lax.broadcasted_iota(jnp.int32, raw.shape, 1) + begin
    allowed = (key_at <= query_at) & (key_at >= first[:, begin : begin + here])
    return jnp.where(allowed, raw, big_negative)


def slots(at, refs):
    count = len(refs) // 2
    for k in range(count):
        here = 2 * lax.rem(at[Z] + k, count)
        yield refs[k], here + at[CORE]
        yield refs[count + k], here + 1 - at[CORE]


def attend_call(scalars, block, heads, rows, pieces, gain, shift, weights, bias, tables, first):
    piece, width = pieces[0].shape
    seq_len = piece * len(pieces)
    seqs = len(weights)
    total = 3 * heads * HEAD_DIM
    own = heads * HEAD_DIM
    tile = min(256, seq_len)

    def kernel(at, *refs):
        n = len(pieces)
        x_refs, (gain_ref, shift_ref), w_refs = refs[:n], refs[n : n + 2], refs[n + 2 : n + 2 + seqs]
        bias_ref, cos_ref, low_ref, high_ref, first_ref = refs[n + 2 + seqs : n + 7 + seqs]
        h_ref, xhat_ref, out_ref, lse_ref, kept_ref, w_ref, x_all, qkv, out_t = refs[n + 7 + seqs :]
        for ref, slot in slots(at, x_refs):
            x_all[rows_at(slot, piece), :] = ref[...]
        for k, ref in enumerate(w_refs):
            w_ref[rows_at(lax.rem(at[S] + k, seqs), rows), :] = ref[:rows, :total]

        def norm_tile(t, carry):
            here = rows_at(t, tile)
            x = x_all[here, :].astype(f32)
            centred = x - jnp.mean(x, axis=1, keepdims=True)
            rstd = lax.rsqrt(jnp.mean(centred * centred, axis=1, keepdims=True) + norm_eps)
            xhat = centred * rstd
            xhat_ref[here, :] = xhat.astype(bf16)
            h = (xhat * gain_ref[...] + shift_ref[...]).astype(bf16)
            h_ref[here, :] = h
            qkv[here, :] = dot(h, w_ref[...]) + bias_ref[...]
            return carry

        lax.fori_loop(0, seq_len // tile, norm_tile, 0)
        cos_full, low_sin, high_sin = cos_ref[...], low_ref[...], high_ref[...]
        q = rope(qkv[:, :own], cos_full, low_sin, high_sin, 1.0) * 0.125
        k = rope(qkv[:, own : 2 * own], cos_full, low_sin, high_sin, 1.0)
        v = qkv[:, 2 * own :]
        kb = k.astype(bf16)
        kept_ref[:, :own] = q.astype(bf16)
        kept_ref[:, own : 2 * own] = kb
        kept_ref[:, 2 * own :] = v.astype(bf16)
        q_t = q.T.astype(bf16)
        v_t = v.T.astype(bf16)
        begins = first_ref[...]
        for head in range(heads):
            lanes = slice(head * HEAD_DIM, (head + 1) * HEAD_DIM)
            keys, queries_t, values_t = kb[:, lanes], q_t[lanes], v_t[lanes]
            for begin in range(0, seq_len, block):
                limit = begin + block
                scores = scores_of(keys, queries_t, begins, begin, block, limit)
                top = jnp.max(scores, axis=0, keepdims=True)
                expd = jnp.exp(scores - top)
                sums = jnp.sum(expd, axis=0, keepdims=True)
                probs = (expd * (1.0 / sums)).astype(bf16)
                out_t[lanes, begin:limit] = dot(values_t[:, :limit], probs)
                lse_ref[head : head + 1, begin:limit] = top + jnp.log(sums)
        out_ref[...] = out_t[...].T.astype(bf16)

    return call(
        kernel,
        [
            shape((seq_len, width)),
            shape((seq_len, width)),
            shape((seq_len, own)),
            shape((heads, seq_len), f32),
            shape((seq_len, total)),
            shape((width, total)),
        ],
        [
            pltpu.VMEM((seq_len, width), bf16),
            pltpu.VMEM((seq_len, total), f32),
            pltpu.VMEM((own, seq_len), f32),
        ],
        scalars,
        (*pieces, gain, shift, *weights, bias, *tables, first),
        cost=(4 * seq_len * width * total, 0),
    )


def attend_back_call(scalars, block, heads, kept, grad, lse, tables, first, after):
    seq_len, total = kept.shape
    own = total // 3

    def kernel(
        at, kept_ref, grad_ref, lse_ref, cos_ref, low_ref, high_ref, first_ref, out_ref, sum_ref, dq_t, dk, dv
    ):
        q = kept_ref[:, :own]
        k = kept_ref[:, own : 2 * own]
        v = kept_ref[:, 2 * own :]
        grad = grad_ref[...]
        q_t = q.astype(f32).T.astype(bf16)
        k_t = k.astype(f32).T.astype(bf16)
        grad_t = grad.astype(f32).T.astype(bf16)
        begins = first_ref[...]
        for head in range(heads):
            lanes = slice(head * HEAD_DIM, (head + 1) * HEAD_DIM)
            q_h, k_h, v_h, grad_h = q[:, lanes], k[:, lanes], v[:, lanes], grad[:, lanes]
            for begin in reversed(range(0, seq_len, block)):
                limit = begin + block
                scores = scores_of(k_h, q_t[lanes], begins, begin, block, limit)
                probs = jnp.exp(scores - lse_ref[head : head + 1, begin:limit])
                grad_p = dot(v_h[:limit], grad_t[lanes, begin:limit])
                delta = jnp.sum(probs * grad_p, axis=0, keepdims=True)
                grad_s = (probs * (grad_p - delta)).astype(bf16)
                dk_here = dot(grad_s, q_h[begin:limit])
                dv_here = dot(probs.astype(bf16), grad_h[begin:limit])
                if limit == seq_len:
                    dk[head] = dk_here
                    dv[head] = dv_here
                else:
                    dk[head, :limit] += dk_here
                    dv[head, :limit] += dv_here
                dq_t[lanes, begin:limit] = dot(k_t[lanes, :limit], grad_s)
        cos_full, low_sin, high_sin = cos_ref[...], low_ref[...], high_ref[...]
        dk_all = jnp.concatenate([dk[head] for head in range(heads)], axis=1)
        dv_all = jnp.concatenate([dv[head] for head in range(heads)], axis=1)
        for part, value in (
            (0, rope(dq_t[...].T * 0.125, cos_full, low_sin, high_sin, -1.0)),
            (1, rope(dk_all, cos_full, low_sin, high_sin, -1.0)),
            (2, dv_all),
        ):
            rounded = value.astype(bf16)
            cols = slice(part * own, (part + 1) * own)
            out_ref[:, cols] = rounded
            sum_ref[:, cols] = jnp.sum(rounded.astype(f32), axis=0, keepdims=True)

    return call(
        kernel,
        [shape((seq_len, total)), shape((1, total), f32)],
        [
            pltpu.VMEM((own, seq_len), f32),
            pltpu.VMEM((heads, seq_len, HEAD_DIM), f32),
            pltpu.VMEM((heads, seq_len, HEAD_DIM), f32),
        ],
        scalars,
        (kept, grad, lse, *tables, first),
        after,
        cost=(10 * seq_len * seq_len * own, 0),
    )


ROOT = 0.7978845608028654
CUBIC = 0.044715


def split_rows(at, z, piece, value, stage, mine_ref, theirs_ref):
    stage[...] = value.astype(bf16)
    mine_ref[rows_at(z, piece), :] = stage[rows_at(at[CORE], piece), :]
    theirs_ref[rows_at(z, piece), :] = stage[rows_at(1 - at[CORE], piece), :]


def forward_call(scalars, rows, piece, h, weights, bias, attn, w_out):
    seq_len, width = h.shape
    cut = weights[0].shape[1] // 2
    seqs = len(weights)
    tile = 2 * piece
    half = seq_len // 2

    def kernel(at, h_ref, *refs):
        w_refs, (bias_ref, attn_ref, w_out_ref) = refs[:seqs], refs[seqs : seqs + 3]
        w_ref, fc_ref, act_ref, mine_ref, theirs_ref, stage = refs[seqs + 3 :]
        for k, ref in enumerate(w_refs):
            w_ref[rows_at(lax.rem(at[S] + k, seqs), rows), :] = ref[...]

        def step(t, carry):
            here = rows_at(t, tile)
            v = dot(h_ref[here, :], w_ref[:, :cut]) + bias_ref[...]
            fc_ref[here, :] = v
            act = (0.5 * v * (1.0 + jnp.tanh(ROOT * (v + CUBIC * (v * v * v))))).astype(bf16)
            act_ref[here, :] = act
            out = dot(attn_ref[here, :], w_out_ref[...]) + cols_dot(act, w_ref[:, cut:])
            split_rows(at, t, piece, out, stage, mine_ref, theirs_ref)
            return carry

        lax.fori_loop(0, seq_len // tile, step, 0)

    return call(
        kernel,
        [
            shape((width, 2 * cut)),
            shape((seq_len, cut), f32),
            shape((seq_len, cut)),
            shape((half, width)),
            shape((half, width)),
        ],
        [pltpu.VMEM((tile, width), bf16)],
        scalars,
        (h, *weights, bias, attn, w_out),
        cost=(4 * seq_len * width * cut, 0),
    )


def middle_call(scalars, piece, mine, theirs):
    half, width = mine.shape
    count = half // piece

    def kernel(at, mine_ref, theirs_ref, keep_ref, *sends):
        for k in range(count):
            here = rows_at(lax.rem(at[Z] + count - k, count), piece)
            value = mine_ref[here, :].astype(f32) + theirs_ref[here, :].astype(f32)
            if k == 0:
                keep_ref[...] = value
            else:
                sends[k - 1][...] = value.astype(bf16)

    return call(
        kernel,
        [shape((piece, width), f32)] + [shape((piece, width))] * (count - 1),
        [],
        scalars,
        (mine, theirs),
    )


def backward_call(scalars, pieces, weight, w_out, fc):
    piece, width = pieces[0].shape
    seq_len, cut = fc.shape
    own = w_out.shape[0]
    tile = min(256, seq_len)

    def kernel(at, *refs):
        n = len(pieces)
        dy_refs, (w_ref, w_out_ref, fc_ref), (dy_ref, dfc_ref, dattn_ref, sum_ref) = (
            refs[:n],
            refs[n : n + 3],
            refs[n + 3 :],
        )
        for ref, slot in slots(at, dy_refs):
            dy_ref[rows_at(slot, piece), :] = ref[...]
        sum_ref[...] = jnp.zeros_like(sum_ref)

        def step(t, carry):
            here = rows_at(t, tile)
            dy = dy_ref[here, :]
            v = fc_ref[here, :]
            square = v * v
            t_v = jnp.tanh(ROOT * (v + CUBIC * (square * v)))
            slope = 0.5 * (1.0 + t_v) + 0.5 * v * (1.0 - t_v * t_v) * (
                ROOT * (1.0 + (3.0 * CUBIC) * square)
            )
            dfc = (dot(dy, w_ref[:, cut:]) * slope).astype(bf16)
            dfc_ref[here, :] = dfc
            sum_ref[...] += jnp.sum(dfc.astype(f32), axis=0, keepdims=True)
            dattn_ref[here, :] = cols_dot(dy, w_out_ref[...]).astype(bf16)
            return carry

        lax.fori_loop(0, seq_len // tile, step, 0)

    return call(
        kernel,
        [shape((seq_len, width)), shape((seq_len, cut)), shape((seq_len, own)), shape((1, cut), f32)],
        [],
        scalars,
        (*pieces, weight, w_out, fc),
        cost=(2 * seq_len * width * cut, 0),
    )


def input_grad_call(scalars, piece, dfc, weight, dqkv, w_qkv, xhat):
    seq_len, cut = dfc.shape
    width = weight.shape[0]
    tile = 2 * piece
    half = seq_len // 2

    def kernel(at, dfc_ref, w_ref, dqkv_ref, w_qkv_ref, xhat_ref, mine_ref, theirs_ref, gain_ref, shift_ref, stage):
        gain_ref[...] = jnp.zeros_like(gain_ref)
        shift_ref[...] = jnp.zeros_like(shift_ref)

        def step(t, carry):
            here = rows_at(t, tile)
            value = cols_dot(dfc_ref[here, :], w_ref[:, :cut]) + cols_dot(
                dqkv_ref[here, :], w_qkv_ref[...]
            )
            gain_ref[...] += jnp.sum(value * xhat_ref[here, :].astype(f32), axis=0, keepdims=True)
            shift_ref[...] += jnp.sum(value, axis=0, keepdims=True)
            split_rows(at, t, piece, value, stage, mine_ref, theirs_ref)
            return carry

        lax.fori_loop(0, seq_len // tile, step, 0)

    return call(
        kernel,
        [shape((half, width)), shape((half, width)), shape((1, width), f32), shape((1, width), f32)],
        [pltpu.VMEM((tile, width), bf16)],
        scalars,
        (dfc, weight, dqkv, w_qkv, xhat),
        cost=(2 * seq_len * width * cut, 0),
    )


def split_fc_call(scalars, seqs, grad_fc1, grad_fc2):
    width, cut = grad_fc1.shape
    rows = width // seqs

    def kernel(at, one_ref, two_ref, *outs):
        for k, ref in enumerate(outs):
            here = rows_at(lax.rem(at[S] + seqs - k, seqs), rows)
            ref[:, :cut] = one_ref[here, :]
            ref[:, cut:] = two_ref[here, :]

    return call(kernel, [shape((rows, 2 * cut))] * seqs, [], scalars, (grad_fc1, grad_fc2))


def small_rows(share):
    return 5, (2 if share >= 10 else 1)


def put_small(block_ref, base, share, lane0, values):
    kinds, parts = small_rows(share)
    for kind, value in enumerate(values):
        high = value.astype(bf16)
        block_ref[base + kind : base + kind + 1, lane0 : lane0 + value.shape[1]] = high.astype(f32)
        if parts == 2:
            row = base + kinds + kind
            block_ref[row : row + 1, lane0 : lane0 + value.shape[1]] = value - high.astype(f32)


def split_qkv_call(scalars, seqs, share, group, heads, grad_qkv, grad_out, halves, vectors):
    width, total = grad_qkv.shape
    rows = width // seqs
    lanes = total + SMALL
    chunks = -(-width // lanes)
    out_rows = rows + chunks * share
    ctxs = rows // share

    def kernel(at, qkv_ref, out_grad_ref, *refs):
        half_refs, refs = refs[: group - 1], refs[group - 1 :]
        vector_refs, outs, stage, small = refs[:5], refs[5 : 5 + seqs], refs[-2], refs[-1]

        def put_out(slot, value):
            for j in range(chunks):
                upto = min(width - j * lanes, lanes)
                begin = rows + j * share
                stage[slot, begin : begin + share, :upto] = value[:, j * lanes : j * lanes + upto]

        for k in range(group):
            for i in range(heads):
                slot = (at[SUB] ^ k) * heads + i
                if k:
                    put_out(slot, half_refs[k - 1][i])
                else:
                    here = pl.ds(pl.multiple_of(i * HEAD_DIM + at[SUB] * share, share), share)
                    put_out(slot, out_grad_ref[here, :])
        small[...] = jnp.zeros_like(small)
        sizes = [ref.shape[1] // (seqs * ctxs) for ref in vector_refs]
        for seq in range(seqs):
            for ctx in range(ctxs):
                owner = seq * ctxs + ctx
                values = [
                    ref[:, owner * n : (owner + 1) * n] for ref, n in zip(vector_refs, sizes)
                ]
                put_small(small, ctx * share, share, 0, values)
            stage[seq, :rows, :total] = qkv_ref[seq * rows : (seq + 1) * rows, :]
            stage[seq, :rows, total:] = small[...].astype(bf16)
        for k, ref in enumerate(outs):
            ref[...] = stage[lax.rem(at[S] + seqs - k, seqs)]

    return call(
        kernel,
        [shape((out_rows, lanes))] * seqs,
        [pltpu.VMEM((seqs, out_rows, lanes), bf16), pltpu.VMEM((rows, SMALL), f32)],
        scalars,
        (grad_qkv, grad_out, *halves, *vectors),
    )


def sum_qkv_call(scalars, share, width, rows, pieces):
    lanes = pieces[0].shape[1]
    chunks = -(-width // lanes)
    kinds, parts = small_rows(share)
    ctxs = rows // share

    def kernel(at, *refs):
        in_refs, out_ref, w_out_ref, sums = refs[: len(pieces)], refs[-3], refs[-2], refs[-1]
        sums[...] = sum(ref[...].astype(f32) for ref in in_refs)
        for j in range(chunks):
            upto = min(width - j * lanes, lanes)
            begin = rows + j * share
            w_out_ref[:, j * lanes : j * lanes + upto] = sums[begin : begin + share, :upto]
        if parts == 2:
            for ctx in range(ctxs):
                base = ctx * share
                here = sums[base : base + kinds, lanes - SMALL :]
                left = sums[base + kinds : base + 2 * kinds, lanes - SMALL :]
                value = here + left
                high = value.astype(bf16).astype(f32)
                sums[base : base + kinds, lanes - SMALL :] = high
                sums[base + kinds : base + 2 * kinds, lanes - SMALL :] = value - high
        out_ref[...] = sums[:rows, :].astype(bf16)

    return call(
        kernel,
        [shape((rows, lanes)), shape((share, width), f32)],
        [pltpu.VMEM(pieces[0].shape, f32)],
        scalars,
        pieces,
    )


def home_fc_call(scalars, got):
    ctxs, share, double = got.shape
    cut = double // 2

    def kernel(at, got_ref, one_ref, two_ref):
        for ctx in range(ctxs):
            cols = slice(ctx * cut, (ctx + 1) * cut)
            one_ref[:, cols] = got_ref[ctx, :, :cut].astype(f32)
            two_ref[:, cols] = got_ref[ctx, :, cut:].astype(f32)

    return call(kernel, [shape((share, ctxs * cut), f32)] * 2, [], scalars, (got,))


def home_qkv_call(scalars, group, heads, lanes, width, got):
    ctxs, share, _ = got.shape
    total = 3 * heads * HEAD_DIM
    kinds, parts = small_rows(share)
    sizes = (share, share, share, 3 * share, 4 * share)

    def kernel(at, got_ref, out_ref, *small_refs):
        for ctx in range(ctxs):
            for part in range(3):
                for i in range(heads):
                    put = head_lanes(ctx, part, i, heads, group, lanes, width)
                    take = (part * heads + i) * HEAD_DIM
                    out_ref[:, put : put + HEAD_DIM] = got_ref[
                        ctx, :, take : take + HEAD_DIM
                    ].astype(f32)
        sums = sum(got_ref[ctx, :, total:].astype(f32) for ctx in range(ctxs))
        for kind, ref in enumerate(small_refs):
            value = sums[kind : kind + 1, :]
            if parts == 2:
                value = value + sums[kinds + kind : kinds + kind + 1, :]
            ref[...] = value[:, : sizes[kind]]

    return call(
        kernel,
        [shape((share, 3 * width), f32)] + [shape((1, n), f32) for n in sizes],
        [],
        scalars,
        (got,),
    )


def finish_call(scalars, x, dy, gain, keep, parts):
    def kernel(at, x_ref, dy_ref, gain_ref, keep_ref, *refs):
        *part_refs, out_ref = refs
        dh = keep_ref[...] + sum(ref[...].astype(f32) for ref in part_refs)
        here = x_ref[...].astype(f32)
        centred = here - jnp.mean(here, axis=1, keepdims=True)
        rstd = lax.rsqrt(jnp.mean(centred * centred, axis=1, keepdims=True) + norm_eps)
        xhat = centred * rstd
        scaled = dh * gain_ref[...]
        out_ref[...] = dy_ref[...].astype(f32) + rstd * (
            scaled
            - jnp.mean(scaled, axis=1, keepdims=True)
            - xhat * jnp.mean(scaled * xhat, axis=1, keepdims=True)
        )

    return call(kernel, [shape(x.shape, f32)], [], scalars, (x, dy, gain, keep, *parts))[0]


def body(
    block_in,
    cotangent,
    segments,
    ln_gain,
    ln_bias,
    w_qkv,
    b_qkv,
    w_out,
    b_out,
    w_fc1,
    b_fc1,
    w_fc2,
    b_fc2,
):
    seqs, ctxs = lax.axis_size("seq"), lax.axis_size("ctx")
    s, c = lax.axis_index("seq"), lax.axis_index("ctx")
    _, piece, width = block_in.shape
    seq_len = piece * ctxs
    share = w_qkv.shape[0]
    hidden = w_fc1.shape[1]
    cut = hidden // ctxs
    heads = HEADS // ctxs
    group = HEAD_DIM // share
    lanes = ctxs // group
    rows = ctxs * share
    zs = ctxs // 2
    sub, lane = c % group, c // group
    scalars = jnp.stack([c % 2, c // 2, s, sub, lane]).astype(jnp.int32)
    total = 3 * heads * HEAD_DIM
    x_here, dy_here = block_in[0], cotangent[0]

    def from_z(k):
        return [(i, ((i // 2 - k) % zs) * 2 + i % 2) for i in range(ctxs)]

    def from_s(k):
        return [(i, (i - k) % seqs) for i in range(seqs)]

    def partner(k):
        return [(i, i ^ k) for i in range(ctxs)]

    def along(axis, parts, pairs):
        return [lax.ppermute(part, axis, pair) for part, pair in zip(parts, pairs)]

    hops_z = [from_z(k) for k in range(1, zs)]
    hops_s = [from_s(k) for k in range(1, seqs)]
    hops_g = [partner(k) for k in range(1, group)]

    def spread_ctx(local):
        mine = [local] + along("ctx", [local] * (zs - 1), hops_z)
        return mine + along("ctx", mine, [partner(1)] * zs)

    def swap_ctx(blocks):
        return lax.all_to_all(blocks, "ctx", split_axis=0, concat_axis=0, tiled=True)

    packed = pack_call(
        scalars,
        group,
        heads,
        lanes,
        w_qkv,
        w_fc1,
        w_fc2,
        (ln_gain, ln_bias, b_out, b_fc2, b_qkv, b_fc1),
        segments,
    )
    got = swap_ctx(packed)
    wide = total + SMALL
    chunks = -(-width // wide)
    padded = jnp.pad(w_out, ((0, 0), (0, chunks * wide - width)))
    joint = jnp.concatenate(
        [got[:, :, :wide].reshape(rows, wide)]
        + [padded[:, j * wide : (j + 1) * wide] for j in range(chunks)]
    )
    joint = [joint] + along("seq", [joint] * (seqs - 1), hops_s)
    fc_here = got[:, :, wide:].reshape(rows, 2 * cut)
    w_fc = [fc_here] + along("seq", [fc_here] * (seqs - 1), hops_s)
    x_all = spread_ctx(x_here)
    dy_all = spread_ctx(dy_here)

    seg = got[:, 6, total : total + piece].reshape(1, seq_len)
    first = jnp.zeros((1, seq_len), jnp.int32)
    for name in range(1, 4):
        begin = jnp.sum((seg < name).astype(jnp.int32))
        first = jnp.where(seg >= name, begin, first)
    pos = lax.broadcasted_iota(jnp.int32, (1, seq_len), 1) - first
    freq = jnp.power(f32(10000.0), -2.0 * jnp.arange(HALF, dtype=f32) / ROT)
    angle = (pos.astype(f32) * freq[:, None]).T
    cos_t, sin_t = jnp.cos(angle), jnp.sin(angle)
    ones = jnp.ones((seq_len, HEAD_DIM - ROT), f32)
    zero = jnp.zeros((seq_len, HEAD_DIM - ROT), f32)
    empty = jnp.zeros((seq_len, HALF), f32)
    tables = (
        jnp.concatenate([cos_t, cos_t, ones] * heads, axis=1),
        jnp.concatenate([sin_t, empty, zero] * heads, axis=1),
        jnp.concatenate([empty, sin_t, zero] * heads, axis=1),
    )

    smalls, *out_parts = spread_out_call(scalars, joint, rows, share, width, group, heads)
    out_parts = out_parts[:1] + along("ctx", out_parts[1:], hops_g)
    smalls = smalls.reshape(seqs * ctxs, share, SMALL)

    def small_part(at, count):
        return smalls[:, at, : count * share].reshape(-1)

    gain = small_part(0, 1).astype(f32).reshape(1, width)
    shift = small_part(1, 1).astype(f32).reshape(1, width)
    bias_out = small_part(2, 1).astype(f32) + small_part(3, 1).astype(f32)
    bias_qkv = small_part(4, 3).reshape(3, group, heads, lanes, HEAD_DIM)
    bias_qkv = lax.dynamic_slice(bias_qkv, (0, sub, 0, lane, 0), (3, 1, heads, 1, HEAD_DIM))
    bias_qkv = bias_qkv.reshape(1, total).astype(f32)
    bias_fc1 = lax.dynamic_slice_in_dim(small_part(5, 4), c * cut, cut, 0)
    bias_fc1 = bias_fc1.astype(f32).reshape(1, cut)
    ordered = jnp.stack(out_parts)[jnp.stack([sub ^ k for k in range(group)])]
    w_out_c = ordered.transpose(1, 0, 2, 3).reshape(heads * HEAD_DIM, width)

    block = min(256, seq_len)
    h, xhat, attn, lse, kept, w_qkv_c = attend_call(
        scalars, block, heads, rows, x_all, gain, shift, joint, bias_qkv, tables, first
    )
    w_fc_c, fc, act, out_mine, out_theirs = forward_call(
        scalars, rows, piece, h, w_fc, bias_fc1, attn, w_out_c
    )
    out_theirs = along("ctx", [out_theirs], [partner(1)])[0]
    out_keep, *out_sends = middle_call(scalars, piece, out_mine, out_theirs)
    out_parts = along("ctx", out_sends, hops_z)
    block_out = x_here.astype(f32) + out_keep + bias_out
    for part in out_parts:
        block_out = block_out + part.astype(f32)
    block_out = block_out.astype(bf16)

    dy, dfc, dattn, sum_fc1 = backward_call(scalars, dy_all, w_fc_c, w_out_c, fc)
    grad_fc1 = rows_dot(h, dfc).astype(bf16)
    grad_fc2 = rows_dot(dy, act).astype(bf16)
    fc_parts = split_fc_call(scalars, seqs, grad_fc1, grad_fc2)
    fc_parts = fc_parts[:1] + along("seq", fc_parts[1:], hops_s)
    grad_out = rows_dot(attn, dy).astype(bf16)
    blocks = grad_out.reshape(heads, group, share, width)
    halves = [lax.dynamic_index_in_dim(blocks, sub ^ k, 1, keepdims=False) for k in range(1, group)]
    halves = along("ctx", halves, hops_g)
    dqkv, sum_qkv = attend_back_call(
        scalars, block, heads, kept, dattn, lse, tables, first, (fc_parts[0],)
    )
    dh_mine, dh_theirs, sum_gain, sum_shift = input_grad_call(
        scalars, piece, dfc, w_fc_c, dqkv, w_qkv_c, xhat
    )
    dh_theirs = along("ctx", [dh_theirs], [partner(1)])[0]
    grad_qkv = rows_dot(h, dqkv).astype(bf16)
    full_qkv = lax.dynamic_update_slice(
        jnp.zeros((3, group, heads, lanes, HEAD_DIM), f32),
        sum_qkv.reshape(3, 1, heads, 1, HEAD_DIM),
        (0, sub, 0, lane, 0),
    ).reshape(1, 3 * width)
    full_fc1 = lax.dynamic_update_slice(
        jnp.zeros((1, hidden), f32), sum_fc1, (0, c * cut)
    )
    sum_y = jnp.sum(dy_here.astype(f32), axis=0, keepdims=True)
    qkv_parts = split_qkv_call(
        scalars,
        seqs,
        share,
        group,
        heads,
        grad_qkv,
        grad_out,
        halves,
        (sum_gain, sum_shift, sum_y, full_qkv, full_fc1),
    )
    qkv_parts = qkv_parts[:1] + along("seq", qkv_parts[1:], hops_s)
    dh_keep, *dh_sends = middle_call(scalars, piece, dh_mine, dh_theirs)
    dh_parts = along("ctx", dh_sends, hops_z)

    fc_sum = sum(part.astype(f32) for part in fc_parts).astype(bf16)
    fc_home = swap_ctx(fc_sum.reshape(ctxs, share, 2 * cut))
    qkv_sum, out_wout = sum_qkv_call(scalars, share, width, rows, qkv_parts)
    qkv_home = swap_ctx(qkv_sum.reshape(ctxs, share, wide))
    grad_in = finish_call(scalars, x_here, dy_here, gain, dh_keep, dh_parts)
    out_wfc1, out_wfc2 = home_fc_call(scalars, fc_home)
    out_wqkv, *small = home_qkv_call(scalars, group, heads, lanes, width, qkv_home)
    small = [value.reshape(-1) for value in small]
    return (
        block_out[None],
        grad_in[None],
        small[0],
        small[1],
        out_wqkv,
        small[3],
        out_wout,
        small[2],
        out_wfc1,
        small[4],
        out_wfc2,
        small[2],
    )


def solution(mesh):
    both = ("seq", "ctx")
    tokens, flat, matrix = P("seq", "ctx", None), P(both), P(both, None)
    in_specs = (tokens, tokens, P("seq", "ctx"), flat, flat) + (matrix, flat) * 4
    out_specs = (tokens, tokens, flat, flat) + (matrix, flat) * 4
    return jax.shard_map(body, mesh=mesh, in_specs=in_specs, out_specs=out_specs, check_vma=False)
```

profile of v0, /device:TPU:0, one launch (start us, length us, event | category | flops | bytes accessed | tf_op | source)
XLA Modules:
  0.0 269.9 jit_solution(4610405656940144302)
XLA Ops:
  1.3 2.3 shard_map.220
  3.6 6.4 %all-to-all-start = ((bf16[8,32,1536]{2,1,0:T(8,128)(2,1)}), bf16[8,32,1536]{2,1,0:T(8,128)(2,1)S(1)}, u32[]{:S(2)}, u32[]{:S(2)}) async-start(bf16[8,32,1536]{2,1,0:T(8,128)(2,1)} %shard_map.220), calls=%async_computation | async-start | bytes 1572864 | tf_op jit(solution)/shard_map/all_to_all | solution.py:676
  9.9 3.8 %collective-permute-start = (bf16[128,1024]{1,0:T(8,128)(2,1)}, bf16[128,1024]{1,0:T(8,128)(2,1)}, u32[]{:S(2)}, u32[]{:S(2)}) collective-permute-start(bf16[128,1024]{1,0:T(8,128)(2,1)} %bitcast.refs_1_), channel_id=1, source_target_pairs={{0,6},{1,7},{2,0},{3,1},{4,2},{5,3},{6,4},{7,5},{8,14},{9,15},{10,... | collective-permute-start | bytes 786440 | tf_op jit(solution)/shard_map/ppermute | solution.py:665
  14.5 17.0 %all-to-all-done = bf16[8,32,1536]{2,1,0:T(8,128)(2,1)S(1)} async-done(((bf16[8,32,1536]{2,1,0:T(8,128)(2,1)}), bf16[8,32,1536]{2,1,0:T(8,128)(2,1)S(1)}, u32[]{:S(2)}, u32[]{:S(2)}) %all-to-all-start) | async-done | bytes 786464 | tf_op jit(solution)/shard_map/all_to_all | solution.py:676
  31.6 2.5 collective-permute-start.7
  35.8 2.0 compare_select_fusion.2
  37.8 9.3 %collective-permute-start.2 = (bf16[128,1024]{1,0:T(8,128)(2,1)}, bf16[128,1024]{1,0:T(8,128)(2,1)}, u32[]{:S(2)}, u32[]{:S(2)}) collective-permute-start(bf16[128,1024]{1,0:T(8,128)(2,1)} %bitcast.refs_1_), channel_id=1, source_target_pairs={{0,2},{1,3},{2,4},{3,5},{4,6},{5,7},{6,0},{7,1},{8,10},{9,11},{10,... | collective-permute-start | bytes 786440 | tf_op jit(solution)/shard_map/ppermute | solution.py:665
  47.8 6.4 %collective-permute-start.18 = (bf16[128,1024]{1,0:T(8,128)(2,1)S(1)}, bf16[128,1024]{1,0:T(8,128)(2,1)}, u32[]{:S(2)}, u32[]{:S(2)}) collective-permute-start(bf16[128,1024]{1,0:T(8,128)(2,1)S(1)} %bitcast.58), channel_id=1, source_target_pairs={{0,6},{1,7},{2,0},{3,1},{4,2},{5,3},{6,4},{7,5},{8,14},{9,15},{10,... | collective-permute-start | bytes 786440 | tf_op jit(solution)/shard_map/ppermute | solution.py:665
  54.9 1.9 multiply_sine_fusion
  56.9 2.6 fusion.17.refs_19_.refs_7_
  59.6 1.7 concatenate.33.refs_17_.refs_5_
  61.3 1.7 concatenate.34.refs_18_.refs_6_
  63.1 1.7 concatenate.32.refs_16_.refs_4_
  64.9 2.3 shard_map.221
  67.8 3.4 %collective-permute-start.10 = (bf16[256,1024]{1,0:T(8,128)(2,1)S(1)}, bf16[256,1024]{1,0:T(8,128)(2,1)S(1)}, u32[]{:S(2)}, u32[]{:S(2)}) collective-permute-start(bf16[256,1024]{1,0:T(8,128)(2,1)S(1)} %bitcast.67), channel_id=1, source_target_pairs={{0,24},{8,0},{16,8},{24,16},{1,25},{9,1},{17,9},{25,17},{2,26},{10... | collective-permute-start | bytes 1572872 | tf_op jit(solution)/shard_map/ppermute | solution.py:665
  75.7 1.7 collective-permute-start.12
  79.5 3.6 %collective-permute-start.20 = (bf16[128,1024]{1,0:T(8,128)(2,1)S(1)}, bf16[128,1024]{1,0:T(8,128)(2,1)S(1)}, u32[]{:S(2)}, u32[]{:S(2)}) collective-permute-start(bf16[128,1024]{1,0:T(8,128)(2,1)S(1)} %bitcast.60), channel_id=1, source_target_pairs={{0,2},{1,3},{2,4},{3,5},{4,6},{5,7},{6,0},{7,1},{8,10},{9,11},{10,... | collective-permute-start | bytes 786440 | tf_op jit(solution)/shard_map/ppermute | solution.py:665
  83.8 11.2 %shard_map.222 = (bf16[1024,1024]{1,0:T(8,128)(2,1)}, bf16[1024,1024]{1,0:T(8,128)(2,1)}, bf16[1024,128]{1,0:T(8,128)(2,1)}, f32[2,1024]{1,0:T(2,128)}, bf16[102...) custom-call(s32[5]{0:T(128)} %stack.35.refs_0_, bf16[128,1024]{1,0:T(8,128)(2,1)} %bitcast.refs_1_, ...), custom_call_target="tpu_custom_call" | custom-call | flops 1610612736 | bytes 4994560 | tf_op jit(solution)/shard_map/pallas_call | solution.py:50
  99.1 8.6 %shard_map.223 = (bf16[1024,1024]{1,0:T(8,128)(2,1)}, f32[1024,512]{1,0:T(8,128)}, bf16[1024,512]{1,0:T(8,128)(2,1)}, bf16[512,1024]{1,0:T(8,128)(2,1)}, bf16[512,1024]{1,0:T(8,128)(2,1)}) custom-call(s32[5]{0:T(128)} %stack.35.refs_0_, bf16[1024,1024]{1,0:T(8,128)(2,1)} %get-tuple-element.63.refs_1_, bf16[256,1024]{1,0:T(8,128)(2,1)} %bitcast.70, ...), custom_call_target="tpu_custom_call" | custom-call | flops 2147483648 | bytes 4720640 | tf_op jit(solution)/shard_map/pallas_call | solution.py:50
  108.7 7.0 %shard_map.225 = (bf16[1024,1024]{1,0:T(8,128)(2,1)}, bf16[1024,512]{1,0:T(8,128)(2,1)}, bf16[1024,128]{1,0:T(8,128)(2,1)}, f32[1,512]{1,0:T(1,128)}) custom-call(s32[5]{0:T(128)} %stack.35.refs_0_, bf16[128,1024]{1,0:T(8,128)(2,1)} %bitcast.56, bf16[128,1024]{1,0:T(8,128)(2,1)} %collective-permute-done.18.refs_2_, ...), custom_call_target="tpu_custom_call" | custom-call | flops 1073741824 | bytes 6553600 | tf_op jit(solution)/shard_map/pallas_call | solution.py:50
  115.8 4.3 %convolution_convert_fusion.1.refs_1_ = bf16[1024,512]{1,0:T(8,128)(2,1)} fusion(bf16[1024,1024]{1,0:T(8,128)(2,1)} %get-tuple-element.63.refs_1_, bf16[1024,512]{1,0:T(8,128)(2,1)} %get-tuple-element.75.refs_1_), kind=kOutput, calls=%fused_computation.2 | convolution fusion | flops 1074266112 | bytes 4194304 | tf_op jit(solution)/shard_map/dot_general | solution.py:25
  121.3 2.3 convolution_convert_fusion.refs_2_
  123.6 3.0 %shard_map.226 = (bf16[256,1024]{1,0:T(8,128)(2,1)}, bf16[256,1024]{1,0:T(8,128)(2,1)}, bf16[256,1024]{1,0:T(8,128)(2,1)}, bf16[256,1024]{1,0:T(8,128)(2,1)}) custom-call(s32[5]{0:T(128)} %stack.35.refs_0_, bf16[1024,512]{1,0:T(8,128)(2,1)} %convolution_convert_fusion.1.refs_1_, bf16[1024,512]{1,0:T(8,128)(2,1)} %convolution_convert_fusion.refs_2_), custom_call_target="tpu_custom_call" | custom-call | bytes 2097152 | tf_op jit(solution)/shard_map/pallas_call | solution.py:50
  126.7 8.6 %shard_map.227 = (bf16[1024,384]{1,0:T(8,128)(2,1)}, f32[1,384]{1,0:T(1,128)}) custom-call(s32[5]{0:T(128)} %stack.35.refs_0_, bf16[1024,384]{1,0:T(8,128)(2,1)} %get-tuple-element.76.refs_1_, bf16[1024,128]{1,0:T(8,128)(2,1)} %get-tuple-element.77.refs_2_, f32[2,1024]{1,0:T(2,128)} %get-tuple-element.78.refs_3_, f32[1024,128]{1,0:T(8,128)} %concatenate.32.refs_16_.refs_4_, ...), custom_call_target="tpu_custom_call" | custom-call | flops 1342177280 | bytes 2633728 | tf_op jit(solution)/shard_map/pallas_call | solution.py:50
  135.3 3.3 %convolution_convert_fusion.2.refs_1_ = bf16[1024,384]{1,0:T(8,128)(2,1)} fusion(bf16[1024,1024]{1,0:T(8,128)(2,1)S(1)} %copy-done.40, bf16[1024,384]{1,0:T(8,128)(2,1)} %get-tuple-element.82.refs_3_), kind=kOutput, calls=%fused_computation.3 | convolution fusion | flops 805699584 | bytes 3670016 | tf_op jit(solution)/shard_map/dot_general | solution.py:25
  139.2 7.7 %shard_map.228 = (bf16[512,1024]{1,0:T(8,128)(2,1)}, bf16[512,1024]{1,0:T(8,128)(2,1)}, f32[1,1024]{1,0:T(1,128)}, f32[1,1024]{1,0:T(1,128)}) custom-call(s32[5]{0:T(128)} %stack.35.refs_0_, bf16[1024,512]{1,0:T(8,128)(2,1)} %get-tuple-element.75.refs_1_, bf16[1024,1024]{1,0:T(8,128)(2,1)} %get-tuple-element.73.refs_9_.refs_2_, ...), custom_call_target="tpu_custom_call" | custom-call | flops 1073741824 | bytes 6815744 | tf_op jit(solution)/shard_map/pallas_call | solution.py:50
  148.4 2.7 shard_map.231
  151.9 1.5 collective-permute-start.31
  155.4 6.5 %collective-permute-done.30.refs_2_ = bf16[320,512]{1,0:T(8,128)(2,1)S(1)} collective-permute-done((bf16[320,512]{1,0:T(8,128)(2,1)}, bf16[320,512]{1,0:T(8,128)(2,1)S(1)}, u32[]{:S(2)}, u32[]{:S(2)}) %collective-permute-start.30) | collective-permute-done | bytes 327712 | tf_op jit(solution)/shard_map/ppermute | solution.py:665
  163.1 17.1 %collective-permute-done.31.refs_3_ = bf16[320,512]{1,0:T(8,128)(2,1)S(1)} collective-permute-done((bf16[320,512]{1,0:T(8,128)(2,1)}, bf16[320,512]{1,0:T(8,128)(2,1)S(1)}, u32[]{:S(2)}, u32[]{:S(2)}) %collective-permute-start.31) | collective-permute-done | bytes 327712 | tf_op jit(solution)/shard_map/ppermute | solution.py:665
  181.7 2.3 shard_map.232
  184.0 7.2 %all-to-all-start.1 = ((bf16[8,32,512]{2,1,0:T(8,128)(2,1)}), bf16[8,32,512]{2,1,0:T(8,128)(2,1)S(1)}, u32[]{:S(2)}, u32[]{:S(2)}) async-start(bf16[8,32,512]{2,1,0:T(8,128)(2,1)} %bitcast.72), calls=%async_computation.1 | async-start | bytes 524288 | tf_op jit(solution)/shard_map/all_to_all | solution.py:676
  191.5 2.4 add_convert_fusion
  193.9 7.0 %all-to-all-done.1.refs_1_ = bf16[8,32,512]{2,1,0:T(8,128)(2,1)S(1)} async-done(((bf16[8,32,512]{2,1,0:T(8,128)(2,1)}), bf16[8,32,512]{2,1,0:T(8,128)(2,1)S(1)}, u32[]{:S(2)}, u32[]{:S(2)}) %all-to-all-start.1) | async-done | bytes 262176 | tf_op jit(solution)/shard_map/all_to_all | solution.py:676
  200.9 3.5 %all-to-all-start.2 = ((bf16[8,32,1024]{2,1,0:T(8,128)(2,1)}), bf16[8,32,1024]{2,1,0:T(8,128)(2,1)S(1)}, u32[]{:S(2)}, u32[]{:S(2)}) async-start(bf16[8,32,1024]{2,1,0:T(8,128)(2,1)} %bitcast.30), calls=%async_computation.2 | async-start | bytes 1048576 | tf_op jit(solution)/shard_map/all_to_all | solution.py:676
  205.4 2.8 %shard_map.229 = (f32[128,1024]{1,0:T(8,128)}, bf16[128,1024]{1,0:T(8,128)(2,1)}, bf16[128,1024]{1,0:T(8,128)(2,1)}, bf16[128,1024]{1,0:T(8,128)(2,1)}) custom-call(s32[5]{0:T(128)} %stack.35.refs_0_, bf16[512,1024]{1,0:T(8,128)(2,1)} %get-tuple-element.85.refs_1_, bf16[512,1024]{1,0:T(8,128)(2,1)} %copy-done.5), custom_call_target="tpu_custom_call" | custom-call | bytes 2097152 | tf_op jit(solution)/shard_map/pallas_call | solution.py:50
  208.1 3.7 %collective-permute-start.26 = (bf16[128,1024]{1,0:T(8,128)(2,1)}, bf16[128,1024]{1,0:T(8,128)(2,1)S(1)}, u32[]{:S(2)}, u32[]{:S(2)}) collective-permute-start(bf16[128,1024]{1,0:T(8,128)(2,1)} %get-tuple-element.88), channel_id=1, source_target_pairs={{0,6},{1,7},{2,0},{3,1},{4,2},{5,3},{6,4},{7,5},{8,14},{9,15},{10,... | collective-permute-start | bytes 786440 | tf_op jit(solution)/shard_map/ppermute | solution.py:665
  212.9 2.8 %shard_map.224 = (f32[128,1024]{1,0:T(8,128)}, bf16[128,1024]{1,0:T(8,128)(2,1)}, bf16[128,1024]{1,0:T(8,128)(2,1)}, bf16[128,1024]{1,0:T(8,128)(2,1)}) custom-call(s32[5]{0:T(128)} %stack.35.refs_0_, bf16[512,1024]{1,0:T(8,128)(2,1)} %get-tuple-element.67.refs_1_, bf16[512,1024]{1,0:T(8,128)(2,1)} %copy-done.6), custom_call_target="tpu_custom_call" | custom-call | bytes 2097152 | tf_op jit(solution)/shard_map/pallas_call | solution.py:50
  216.8 3.3 %collective-permute-start.28 = (bf16[128,1024]{1,0:T(8,128)(2,1)S(1)}, bf16[128,1024]{1,0:T(8,128)(2,1)S(1)}, u32[]{:S(2)}, u32[]{:S(2)}) collective-permute-start(bf16[128,1024]{1,0:T(8,128)(2,1)S(1)} %copy-done.37), channel_id=1, source_target_pairs={{0,2},{1,3},{2,4},{3,5},{4,6},{5,7},{6,0},{7,1},{8,10},{9,11},{10,... | collective-permute-start | bytes 786440 | tf_op jit(solution)/shard_map/ppermute | solution.py:665
  220.2 1.7 collective-permute-done.26.refs_5_
  221.8 2.2 collective-permute-start.15
  225.1 1.9 shard_map.233
  226.9 27.1 %collective-permute-done.27.refs_6_ = bf16[128,1024]{1,0:T(8,128)(2,1)S(1)} collective-permute-done((bf16[128,1024]{1,0:T(8,128)(2,1)S(1)}, bf16[128,1024]{1,0:T(8,128)(2,1)S(1)}, u32[]{:S(2)}, u32[]{:S(2)}) %collective-permute-start.27) | collective-permute-done | bytes 262176 | tf_op jit(solution)/shard_map/ppermute | solution.py:665
  254.8 2.7 %shard_map.230 = f32[128,1024]{1,0:T(8,128)} custom-call(s32[5]{0:T(128)} %stack.35.refs_0_, bf16[128,1024]{1,0:T(8,128)(2,1)} %bitcast.refs_1_, bf16[128,1024]{1,0:T(8,128)(2,1)} %bitcast.57, f32[1,1024]{1,0:T(1,128)} %reshape.334.refs_9_.refs_3_, f32[128,1024]{1,0:T(8,128)} %get-tuple-element.87.refs_4_, bf16[128,1024]{1,0:T(8,128)(2,1)} %copy-done.18, ...), custom_call_target="tpu_custom_call" | custom-call | bytes 1839104 | tf_op jit(solution)/shard_map/pallas_call | solution.py:50
  257.6 2.0 collective-permute-done.16
  259.6 5.0 %collective-permute-done.15 = bf16[128,1024]{1,0:T(8,128)(2,1)S(1)} collective-permute-done((bf16[128,1024]{1,0:T(8,128)(2,1)}, bf16[128,1024]{1,0:T(8,128)(2,1)S(1)}, u32[]{:S(2)}, u32[]{:S(2)}) %collective-permute-start.15) | collective-permute-done | bytes 262176 | tf_op jit(solution)/shard_map/ppermute | solution.py:665
  264.6 1.9 fusion
  267.3 2.1 shard_map.234
  (181 shorter events, 33.1 us)
Async XLA Ops:
  3.6 27.9 %all-to-all-start = ((bf16[8,32,1536]{2,1,0:T(8,128)(2,1)}), bf16[8,32,1536]{2,1,0:T(8,128)(2,1)S(1)}, u32[]{:S(2)}, u32[]{:S(2)}) async-start(bf16[8,32,1536]{2,1,0:T(8,128)(2,1)} %shard_map.220), calls=%async_computation | async-start | bytes 1572864 | tf_op jit(solution)/shard_map/all_to_all | solution.py:676
  9.9 27.9 %collective-permute-start = (bf16[128,1024]{1,0:T(8,128)(2,1)}, bf16[128,1024]{1,0:T(8,128)(2,1)}, u32[]{:S(2)}, u32[]{:S(2)}) collective-permute-start(bf16[128,1024]{1,0:T(8,128)(2,1)} %bitcast.refs_1_), channel_id=1, source_target_pairs={{0,6},{1,7},{2,0},{3,1},{4,2},{5,3},{6,4},{7,5},{8,14},{9,15},{10,... | collective-permute-start | bytes 786440 | tf_op jit(solution)/shard_map/ppermute | solution.py:665
  13.8 34.0 %collective-permute-start.1 = (bf16[128,1024]{1,0:T(8,128)(2,1)}, bf16[128,1024]{1,0:T(8,128)(2,1)S(1)}, u32[]{:S(2)}, u32[]{:S(2)}) collective-permute-start(bf16[128,1024]{1,0:T(8,128)(2,1)} %bitcast.refs_1_), channel_id=1, source_target_pairs={{0,4},{1,5},{2,6},{3,7},{4,0},{5,1},{6,2},{7,3},{8,12},{9,13},{10,... | collective-permute-start | bytes 786440 | tf_op jit(solution)/shard_map/ppermute | solution.py:665
  31.6 29.8 %copy-start.4 = (bf16[320,512]{1,0:T(8,128)(2,1)}, bf16[320,512]{1,0:T(8,128)(2,1)S(1)}, u32[]{:S(2)}) copy-start(bf16[320,512]{1,0:T(8,128)(2,1)S(1)} %pad_maximum_fusion.refs_1_.refs_11_) | copy-start | bytes 983044
  31.6 16.2 %collective-permute-start.7 = (bf16[320,512]{1,0:T(8,128)(2,1)S(1)}, bf16[320,512]{1,0:T(8,128)(2,1)S(1)}, u32[]{:S(2)}, u32[]{:S(2)}) collective-permute-start(bf16[320,512]{1,0:T(8,128)(2,1)S(1)} %pad_maximum_fusion.refs_1_.refs_11_), channel_id=1, source_target_pairs={{0,24},{8,0},{16,8},{24,16},{1,25},{9,1},{17,9},{25,17},{2,26},{10... | collective-permute-start | bytes 983048 | tf_op jit(solution)/shard_map/ppermute | solution.py:665
  34.1 20.1 %collective-permute-start.8 = (bf16[320,512]{1,0:T(8,128)(2,1)S(1)}, bf16[320,512]{1,0:T(8,128)(2,1)S(1)}, u32[]{:S(2)}, u32[]{:S(2)}) collective-permute-start(bf16[320,512]{1,0:T(8,128)(2,1)S(1)} %pad_maximum_fusion.refs_1_.refs_11_), channel_id=1, source_target_pairs={{0,16},{8,24},{16,0},{24,8},{1,17},{9,25},{17,1},{25,9},{2,18},{10... | collective-permute-start | bytes 983048 | tf_op jit(solution)/shard_map/ppermute | solution.py:665
  34.6 22.2 %collective-permute-start.9 = (bf16[320,512]{1,0:T(8,128)(2,1)S(1)}, bf16[320,512]{1,0:T(8,128)(2,1)S(1)}, u32[]{:S(2)}, u32[]{:S(2)}) collective-permute-start(bf16[320,512]{1,0:T(8,128)(2,1)S(1)} %pad_maximum_fusion.refs_1_.refs_11_), channel_id=1, source_target_pairs={{0,8},{8,16},{16,24},{24,0},{1,9},{9,17},{17,25},{25,1},{2,10},{10... | collective-permute-start | bytes 983048 | tf_op jit(solution)/shard_map/ppermute | solution.py:665
  37.8 29.4 %collective-permute-start.2 = (bf16[128,1024]{1,0:T(8,128)(2,1)}, bf16[128,1024]{1,0:T(8,128)(2,1)}, u32[]{:S(2)}, u32[]{:S(2)}) collective-permute-start(bf16[128,1024]{1,0:T(8,128)(2,1)} %bitcast.refs_1_), channel_id=1, source_target_pairs={{0,2},{1,3},{2,4},{3,5},{4,6},{5,7},{6,0},{7,1},{8,10},{9,11},{10,... | collective-permute-start | bytes 786440 | tf_op jit(solution)/shard_map/ppermute | solution.py:665
  47.8 20.0 %collective-permute-start.3 = (bf16[128,1024]{1,0:T(8,128)(2,1)}, bf16[128,1024]{1,0:T(8,128)(2,1)}, u32[]{:S(2)}, u32[]{:S(2)}) collective-permute-start(bf16[128,1024]{1,0:T(8,128)(2,1)} %bitcast.refs_1_), channel_id=1, source_target_pairs={{0,1},{1,0},{2,3},{3,2},{4,5},{5,4},{6,7},{7,6},{8,9},{9,8},{10,11... | collective-permute-start | bytes 786440 | tf_op jit(solution)/shard_map/ppermute | solution.py:665
  47.8 20.0 %collective-permute-start.18 = (bf16[128,1024]{1,0:T(8,128)(2,1)S(1)}, bf16[128,1024]{1,0:T(8,128)(2,1)}, u32[]{:S(2)}, u32[]{:S(2)}) collective-permute-start(bf16[128,1024]{1,0:T(8,128)(2,1)S(1)} %bitcast.58), channel_id=1, source_target_pairs={{0,6},{1,7},{2,0},{3,1},{4,2},{5,3},{6,4},{7,5},{8,14},{9,15},{10,... | collective-permute-start | bytes 786440 | tf_op jit(solution)/shard_map/ppermute | solution.py:665
  54.9 17.7 %collective-permute-start.19 = (bf16[128,1024]{1,0:T(8,128)(2,1)S(1)}, bf16[128,1024]{1,0:T(8,128)(2,1)}, u32[]{:S(2)}, u32[]{:S(2)}) collective-permute-start(bf16[128,1024]{1,0:T(8,128)(2,1)S(1)} %bitcast.59), channel_id=1, source_target_pairs={{0,4},{1,5},{2,6},{3,7},{4,0},{5,1},{6,2},{7,3},{8,12},{9,13},{10,... | collective-permute-start | bytes 786440 | tf_op jit(solution)/shard_map/ppermute | solution.py:665
  56.8 18.8 %collective-permute-start.4 = (bf16[128,1024]{1,0:T(8,128)(2,1)}, bf16[128,1024]{1,0:T(8,128)(2,1)}, u32[]{:S(2)}, u32[]{:S(2)}) collective-permute-start(bf16[128,1024]{1,0:T(8,128)(2,1)} %collective-permute-done.refs_2_), channel_id=1, source_target_pairs={{0,1},{1,0},{2,3},{3,2},{4,5},{5,4},{6,7},{7,6},{8,9},{9,8},{10,11... | collective-permute-start | bytes 786440 | tf_op jit(solution)/shard_map/ppermute | solution.py:665
  64.9 30.1 %copy-start.10 = (bf16[8,32,1024]{2,1,0:T(8,128)(2,1)}, bf16[8,32,1024]{2,1,0:T(8,128)(2,1)S(1)}, u32[]{:S(2)}) copy-start(bf16[8,32,1024]{2,1,0:T(8,128)(2,1)S(1)} %slice.51) | copy-start | bytes 1572868
  67.2 12.3 %collective-permute-start.5 = (bf16[128,1024]{1,0:T(8,128)(2,1)S(1)}, bf16[128,1024]{1,0:T(8,128)(2,1)S(1)}, u32[]{:S(2)}, u32[]{:S(2)}) collective-permute-start(bf16[128,1024]{1,0:T(8,128)(2,1)S(1)} %copy-done.34), channel_id=1, source_target_pairs={{0,1},{1,0},{2,3},{3,2},{4,5},{5,4},{6,7},{7,6},{8,9},{9,8},{10,11... | collective-permute-start | bytes 786440 | tf_op jit(solution)/shard_map/ppermute | solution.py:665
  67.8 15.4 %collective-permute-start.6 = (bf16[128,1024]{1,0:T(8,128)(2,1)}, bf16[128,1024]{1,0:T(8,128)(2,1)S(1)}, u32[]{:S(2)}, u32[]{:S(2)}) collective-permute-start(bf16[128,1024]{1,0:T(8,128)(2,1)} %collective-permute-done.2.refs_4_), channel_id=1, source_target_pairs={{0,1},{1,0},{2,3},{3,2},{4,5},{5,4},{6,7},{7,6},{8,9},{9,8},{10,11... | collective-permute-start | bytes 786440 | tf_op jit(solution)/shard_map/ppermute | solution.py:665
  67.8 29.2 %collective-permute-start.10 = (bf16[256,1024]{1,0:T(8,128)(2,1)S(1)}, bf16[256,1024]{1,0:T(8,128)(2,1)S(1)}, u32[]{:S(2)}, u32[]{:S(2)}) collective-permute-start(bf16[256,1024]{1,0:T(8,128)(2,1)S(1)} %bitcast.67), channel_id=1, source_target_pairs={{0,24},{8,0},{16,8},{24,16},{1,25},{9,1},{17,9},{25,17},{2,26},{10... | collective-permute-start | bytes 1572872 | tf_op jit(solution)/shard_map/ppermute | solution.py:665
  72.7 25.1 %collective-permute-start.11 = (bf16[256,1024]{1,0:T(8,128)(2,1)S(1)}, bf16[256,1024]{1,0:T(8,128)(2,1)}, u32[]{:S(2)}, u32[]{:S(2)}) collective-permute-start(bf16[256,1024]{1,0:T(8,128)(2,1)S(1)} %bitcast.68), channel_id=1, source_target_pairs={{0,16},{8,24},{16,0},{24,8},{1,17},{9,25},{17,1},{25,9},{2,18},{10... | collective-permute-start | bytes 1572872 | tf_op jit(solution)/shard_map/ppermute | solution.py:665
  75.7 23.4 %collective-permute-start.12 = (bf16[256,1024]{1,0:T(8,128)(2,1)S(1)}, bf16[256,1024]{1,0:T(8,128)(2,1)}, u32[]{:S(2)}, u32[]{:S(2)}) collective-permute-start(bf16[256,1024]{1,0:T(8,128)(2,1)S(1)} %bitcast.69), channel_id=1, source_target_pairs={{0,8},{8,16},{16,24},{24,0},{1,9},{9,17},{17,25},{25,1},{2,10},{10... | collective-permute-start | bytes 1572872 | tf_op jit(solution)/shard_map/ppermute | solution.py:665
  79.5 17.0 %collective-permute-start.20 = (bf16[128,1024]{1,0:T(8,128)(2,1)S(1)}, bf16[128,1024]{1,0:T(8,128)(2,1)S(1)}, u32[]{:S(2)}, u32[]{:S(2)}) collective-permute-start(bf16[128,1024]{1,0:T(8,128)(2,1)S(1)} %bitcast.60), channel_id=1, source_target_pairs={{0,2},{1,3},{2,4},{3,5},{4,6},{5,7},{6,0},{7,1},{8,10},{9,11},{10,... | collective-permute-start | bytes 786440 | tf_op jit(solution)/shard_map/ppermute | solution.py:665
  83.1 14.6 %copy-start.27 = (bf16[2,32,1024]{2,1,0:T(8,128)(2,1)S(1)}, bf16[2,32,1024]{2,1,0:T(8,128)(2,1)}, u32[]{:S(2)}) copy-start(bf16[2,32,1024]{2,1,0:T(8,128)(2,1)} %get-tuple-element.65) | copy-start | bytes 393220
  83.1 13.4 %collective-permute-start.13 = (bf16[2,32,1024]{2,1,0:T(8,128)(2,1)}, bf16[2,32,1024]{2,1,0:T(8,128)(2,1)S(1)}, u32[]{:S(2)}, u32[]{:S(2)}) collective-permute-start(bf16[2,32,1024]{2,1,0:T(8,128)(2,1)} %get-tuple-element.66), channel_id=1, source_target_pairs={{0,1},{1,0},{2,3},{3,2},{4,5},{5,4},{6,7},{7,6},{8,9},{9,8},{10,11... | collective-permute-start | bytes 393224 | tf_op jit(solution)/shard_map/ppermute | solution.py:665
  96.6 11.2 %collective-permute-start.21 = (bf16[128,1024]{1,0:T(8,128)(2,1)S(1)}, bf16[128,1024]{1,0:T(8,128)(2,1)S(1)}, u32[]{:S(2)}, u32[]{:S(2)}) collective-permute-start(bf16[128,1024]{1,0:T(8,128)(2,1)S(1)} %bitcast.61), channel_id=1, source_target_pairs={{0,1},{1,0},{2,3},{3,2},{4,5},{5,4},{6,7},{7,6},{8,9},{9,8},{10,11... | collective-permute-start | bytes 786440 | tf_op jit(solution)/shard_map/ppermute | solution.py:665
  96.6 11.2 %collective-permute-start.22 = (bf16[128,1024]{1,0:T(8,128)(2,1)}, bf16[128,1024]{1,0:T(8,128)(2,1)S(1)}, u32[]{:S(2)}, u32[]{:S(2)}) collective-permute-start(bf16[128,1024]{1,0:T(8,128)(2,1)} %collective-permute-done.18.refs_2_), channel_id=1, source_target_pairs={{0,1},{1,0},{2,3},{3,2},{4,5},{5,4},{6,7},{7,6},{8,9},{9,8},{10,11... | collective-permute-start | bytes 786440 | tf_op jit(solution)/shard_map/ppermute | solution.py:665
  97.1 10.7 %collective-permute-start.23 = (bf16[128,1024]{1,0:T(8,128)(2,1)}, bf16[128,1024]{1,0:T(8,128)(2,1)S(1)}, u32[]{:S(2)}, u32[]{:S(2)}) collective-permute-start(bf16[128,1024]{1,0:T(8,128)(2,1)} %collective-permute-done.19.refs_3_), channel_id=1, source_target_pairs={{0,1},{1,0},{2,3},{3,2},{4,5},{5,4},{6,7},{7,6},{8,9},{9,8},{10,11... | collective-permute-start | bytes 786440 | tf_op jit(solution)/shard_map/ppermute | solution.py:665
  97.8 10.0 %collective-permute-start.24 = (bf16[128,1024]{1,0:T(8,128)(2,1)S(1)}, bf16[128,1024]{1,0:T(8,128)(2,1)S(1)}, u32[]{:S(2)}, u32[]{:S(2)}) collective-permute-start(bf16[128,1024]{1,0:T(8,128)(2,1)S(1)} %collective-permute-done.20.refs_4_), channel_id=1, source_target_pairs={{0,1},{1,0},{2,3},{3,2},{4,5},{5,4},{6,7},{7,6},{8,9},{9,8},{10,11... | collective-permute-start | bytes 786440 | tf_op jit(solution)/shard_map/ppermute | solution.py:665
  120.6 18.0 %copy-start.3 = (bf16[128,1024]{1,0:T(8,128)(2,1)}, bf16[128,1024]{1,0:T(8,128)(2,1)S(1)}, u32[]{:S(2)}) copy-start(bf16[128,1024]{1,0:T(8,128)(2,1)S(1)} %convolution_convert_fusion.3.refs_2_) | copy-start | bytes 786436
  138.6 9.2 %collective-permute-start.29 = (bf16[2,32,1024]{2,1,0:T(8,128)(2,1)S(1)}, bf16[2,32,1024]{2,1,0:T(8,128)(2,1)S(1)}, u32[]{:S(2)}, u32[]{:S(2)}) collective-permute-start(bf16[2,32,1024]{2,1,0:T(8,128)(2,1)S(1)} %dynamic-slice_bitcast_fusion), channel_id=1, source_target_pairs={{0,1},{1,0},{2,3},{3,2},{4,5},{5,4},{6,7},{7,6},{8,9},{9,8},{10,11... | collective-permute-start | bytes 393224 | tf_op jit(solution)/shard_map/ppermute | solution.py:665
  146.8 44.7 %copy-start.8 = (bf16[256,1024]{1,0:T(8,128)(2,1)S(1)}, bf16[256,1024]{1,0:T(8,128)(2,1)}, u32[]{:S(2)}) copy-start(bf16[256,1024]{1,0:T(8,128)(2,1)} %get-tuple-element.81.refs_8_) | copy-start | bytes 1572868
  151.1 10.8 %collective-permute-start.30 = (bf16[320,512]{1,0:T(8,128)(2,1)}, bf16[320,512]{1,0:T(8,128)(2,1)S(1)}, u32[]{:S(2)}, u32[]{:S(2)}) collective-permute-start(bf16[320,512]{1,0:T(8,128)(2,1)} %get-tuple-element.96), channel_id=1, source_target_pairs={{0,24},{8,0},{16,8},{24,16},{1,25},{9,1},{17,9},{25,17},{2,26},{10... | collective-permute-start | bytes 983048 | tf_op jit(solution)/shard_map/ppermute | solution.py:665
  151.9 28.3 %collective-permute-start.31 = (bf16[320,512]{1,0:T(8,128)(2,1)}, bf16[320,512]{1,0:T(8,128)(2,1)S(1)}, u32[]{:S(2)}, u32[]{:S(2)}) collective-permute-start(bf16[320,512]{1,0:T(8,128)(2,1)} %get-tuple-element.97), channel_id=1, source_target_pairs={{0,16},{8,24},{16,0},{24,8},{1,17},{9,25},{17,1},{25,9},{2,18},{10... | collective-permute-start | bytes 983048 | tf_op jit(solution)/shard_map/ppermute | solution.py:665
  153.4 26.8 %collective-permute-start.32 = (bf16[320,512]{1,0:T(8,128)(2,1)}, bf16[320,512]{1,0:T(8,128)(2,1)S(1)}, u32[]{:S(2)}, u32[]{:S(2)}) collective-permute-start(bf16[320,512]{1,0:T(8,128)(2,1)} %get-tuple-element.98), channel_id=1, source_target_pairs={{0,8},{8,16},{16,24},{24,0},{1,9},{9,17},{17,25},{25,1},{2,10},{10... | collective-permute-start | bytes 983048 | tf_op jit(solution)/shard_map/ppermute | solution.py:665
  154.3 50.0 %collective-permute-start.25 = (bf16[512,1024]{1,0:T(8,128)(2,1)}, bf16[512,1024]{1,0:T(8,128)(2,1)S(1)}, u32[]{:S(2)}, u32[]{:S(2)}) collective-permute-start(bf16[512,1024]{1,0:T(8,128)(2,1)} %get-tuple-element.86), channel_id=1, source_target_pairs={{0,1},{1,0},{2,3},{3,2},{4,5},{5,4},{6,7},{7,6},{8,9},{9,8},{10,11... | collective-permute-start | bytes 3145736 | tf_op jit(solution)/shard_map/ppermute | solution.py:665
  154.3 36.8 %collective-permute-start.35 = (bf16[256,1024]{1,0:T(8,128)(2,1)}, bf16[256,1024]{1,0:T(8,128)(2,1)S(1)}, u32[]{:S(2)}, u32[]{:S(2)}) collective-permute-start(bf16[256,1024]{1,0:T(8,128)(2,1)} %get-tuple-element.108), channel_id=1, source_target_pairs={{0,8},{8,16},{16,24},{24,0},{1,9},{9,17},{17,25},{25,1},{2,10},{10... | collective-permute-start | bytes 1572872 | tf_op jit(solution)/shard_map/ppermute | solution.py:665
  161.9 18.4 %copy-start.14 = (bf16[320,512]{1,0:T(8,128)(2,1)}, bf16[320,512]{1,0:T(8,128)(2,1)S(1)}, u32[]{:S(2)}) copy-start(bf16[320,512]{1,0:T(8,128)(2,1)S(1)} %collective-permute-done.30.refs_2_) | copy-start | bytes 983044
  161.9 29.6 %collective-permute-start.34 = (bf16[256,1024]{1,0:T(8,128)(2,1)}, bf16[256,1024]{1,0:T(8,128)(2,1)}, u32[]{:S(2)}, u32[]{:S(2)}) collective-permute-start(bf16[256,1024]{1,0:T(8,128)(2,1)} %get-tuple-element.107), channel_id=1, source_target_pairs={{0,16},{8,24},{16,0},{24,8},{1,17},{9,25},{17,1},{25,9},{2,18},{10... | collective-permute-start | bytes 1572872 | tf_op jit(solution)/shard_map/ppermute | solution.py:665
  180.2 11.2 %collective-permute-start.33 = (bf16[256,1024]{1,0:T(8,128)(2,1)}, bf16[256,1024]{1,0:T(8,128)(2,1)}, u32[]{:S(2)}, u32[]{:S(2)}) collective-permute-start(bf16[256,1024]{1,0:T(8,128)(2,1)} %get-tuple-element.106), channel_id=1, source_target_pairs={{0,24},{8,0},{16,8},{24,16},{1,25},{9,1},{17,9},{25,17},{2,26},{10... | collective-permute-start | bytes 1572872 | tf_op jit(solution)/shard_map/ppermute | solution.py:665
  181.7 30.2 %collective-permute-start.14 = (bf16[512,1024]{1,0:T(8,128)(2,1)}, bf16[512,1024]{1,0:T(8,128)(2,1)S(1)}, u32[]{:S(2)}, u32[]{:S(2)}) collective-permute-start(bf16[512,1024]{1,0:T(8,128)(2,1)} %get-tuple-element.68), channel_id=1, source_target_pairs={{0,1},{1,0},{2,3},{3,2},{4,5},{5,4},{6,7},{7,6},{8,9},{9,8},{10,11... | collective-permute-start | bytes 3145736 | tf_op jit(solution)/shard_map/ppermute | solution.py:665
  184.0 16.9 %all-to-all-start.1 = ((bf16[8,32,512]{2,1,0:T(8,128)(2,1)}), bf16[8,32,512]{2,1,0:T(8,128)(2,1)S(1)}, u32[]{:S(2)}, u32[]{:S(2)}) async-start(bf16[8,32,512]{2,1,0:T(8,128)(2,1)} %bitcast.72), calls=%async_computation.1 | async-start | bytes 524288 | tf_op jit(solution)/shard_map/all_to_all | solution.py:676
  200.9 14.8 %copy-start.7 = (bf16[8,32,512]{2,1,0:T(8,128)(2,1)}, bf16[8,32,512]{2,1,0:T(8,128)(2,1)S(1)}, u32[]{:S(2)}) copy-start(bf16[8,32,512]{2,1,0:T(8,128)(2,1)S(1)} %all-to-all-done.1.refs_1_) | copy-start | bytes 786436
  200.9 65.6 %all-to-all-start.2 = ((bf16[8,32,1024]{2,1,0:T(8,128)(2,1)}), bf16[8,32,1024]{2,1,0:T(8,128)(2,1)S(1)}, u32[]{:S(2)}, u32[]{:S(2)}) async-start(bf16[8,32,1024]{2,1,0:T(8,128)(2,1)} %bitcast.30), calls=%async_computation.2 | async-start | bytes 1048576 | tf_op jit(solution)/shard_map/all_to_all | solution.py:676
  208.1 13.7 %collective-permute-start.26 = (bf16[128,1024]{1,0:T(8,128)(2,1)}, bf16[128,1024]{1,0:T(8,128)(2,1)S(1)}, u32[]{:S(2)}, u32[]{:S(2)}) collective-permute-start(bf16[128,1024]{1,0:T(8,128)(2,1)} %get-tuple-element.88), channel_id=1, source_target_pairs={{0,6},{1,7},{2,0},{3,1},{4,2},{5,3},{6,4},{7,5},{8,14},{9,15},{10,... | collective-permute-start | bytes 786440 | tf_op jit(solution)/shard_map/ppermute | solution.py:665
  215.7 48.9 %copy-start.9 = (f32[128,1024]{1,0:T(8,128)S(1)}, f32[128,1024]{1,0:T(8,128)}, u32[]{:S(2)}) copy-start(f32[128,1024]{1,0:T(8,128)} %get-tuple-element.69) | copy-start | bytes 1572868
  215.7 41.9 %collective-permute-start.17 = (bf16[128,1024]{1,0:T(8,128)(2,1)}, bf16[128,1024]{1,0:T(8,128)(2,1)S(1)}, u32[]{:S(2)}, u32[]{:S(2)}) collective-permute-start(bf16[128,1024]{1,0:T(8,128)(2,1)} %get-tuple-element.72), channel_id=1, source_target_pairs={{0,2},{1,3},{2,4},{3,5},{4,6},{5,7},{6,0},{7,1},{8,10},{9,11},{10,... | collective-permute-start | bytes 786440 | tf_op jit(solution)/shard_map/ppermute | solution.py:665
  215.7 38.3 %collective-permute-start.27 = (bf16[128,1024]{1,0:T(8,128)(2,1)S(1)}, bf16[128,1024]{1,0:T(8,128)(2,1)S(1)}, u32[]{:S(2)}, u32[]{:S(2)}) collective-permute-start(bf16[128,1024]{1,0:T(8,128)(2,1)S(1)} %copy-done.38), channel_id=1, source_target_pairs={{0,4},{1,5},{2,6},{3,7},{4,0},{5,1},{6,2},{7,3},{8,12},{9,13},{10,... | collective-permute-start | bytes 786440 | tf_op jit(solution)/shard_map/ppermute | solution.py:665
  216.8 37.2 %collective-permute-start.28 = (bf16[128,1024]{1,0:T(8,128)(2,1)S(1)}, bf16[128,1024]{1,0:T(8,128)(2,1)S(1)}, u32[]{:S(2)}, u32[]{:S(2)}) collective-permute-start(bf16[128,1024]{1,0:T(8,128)(2,1)S(1)} %copy-done.37), channel_id=1, source_target_pairs={{0,2},{1,3},{2,4},{3,5},{4,6},{5,7},{6,0},{7,1},{8,10},{9,11},{10,... | collective-permute-start | bytes 786440 | tf_op jit(solution)/shard_map/ppermute | solution.py:665
  220.1 39.5 %collective-permute-start.16 = (bf16[128,1024]{1,0:T(8,128)(2,1)}, bf16[128,1024]{1,0:T(8,128)(2,1)S(1)}, u32[]{:S(2)}, u32[]{:S(2)}) collective-permute-start(bf16[128,1024]{1,0:T(8,128)(2,1)} %get-tuple-element.71), channel_id=1, source_target_pairs={{0,4},{1,5},{2,6},{3,7},{4,0},{5,1},{6,2},{7,3},{8,12},{9,13},{10,... | collective-permute-start | bytes 786440 | tf_op jit(solution)/shard_map/ppermute | solution.py:665
  221.8 32.2 %copy-start.18 = (bf16[128,1024]{1,0:T(8,128)(2,1)}, bf16[128,1024]{1,0:T(8,128)(2,1)S(1)}, u32[]{:S(2)}) copy-start(bf16[128,1024]{1,0:T(8,128)(2,1)S(1)} %collective-permute-done.26.refs_5_) | copy-start | bytes 786436
  221.8 42.8 %collective-permute-start.15 = (bf16[128,1024]{1,0:T(8,128)(2,1)}, bf16[128,1024]{1,0:T(8,128)(2,1)S(1)}, u32[]{:S(2)}, u32[]{:S(2)}) collective-permute-start(bf16[128,1024]{1,0:T(8,128)(2,1)} %get-tuple-element.70), channel_id=1, source_target_pairs={{0,6},{1,7},{2,0},{3,1},{4,2},{5,3},{6,4},{7,5},{8,14},{9,15},{10,... | collective-permute-start | bytes 786440 | tf_op jit(solution)/shard_map/ppermute | solution.py:665
  (33 other events, 139.0 us)
where the time goes:
time: 271 us; the launch traced here: 270 us
  waiting for transfers between devices  86.5 us (32%)
  Pallas kernels  67.9 us (25%)
  starting transfers between devices  67.8 us (25%)
  local copies, waits for them, and re-layouts  22.3 us (8%)
  other arithmetic  13.8 us (5%)
  matrix products  10.4 us (4%)
    pallas_call x15, Pallas kernels, call(): pl.pallas_call(wrapped, in_specs=in_specs, out_specs=[vmem] * len(outs),...  67.9 us
    ppermute x36, waiting for transfers between devices, along(): return [lax.ppermute(part, axis, pair) for part, pair in zip(parts, pairs)]  62.5 us
    ppermute x36, starting transfers between devices, along(): return [lax.ppermute(part, axis, pair) for part, pair in zip(parts, pairs)]  50.8 us
    all_to_all x3, waiting for transfers between devices, swap_ctx(): lax.all_to_all(blocks, 'ctx', split_axis=0, concat_axis=0, tiled=True)  24 us
    all_to_all x3, starting transfers between devices, swap_ctx(): lax.all_to_all(blocks, 'ctx', split_axis=0, concat_axis=0, tiled=True)  17 us
    dot_general x4, matrix products, rows_dot(): lax.dot_general(left, right, (((0,), (0,)), ((), ())), preferred_element_...  10.4 us
    unnamed x87, local copies, waits for them, and re-layouts  9.37 us
  transfers between devices with their start and end apart: 39, of which 12 were waited for; matrix products, arithmetic and copies ran while one was open for 10% of the time, Pallas kernels for 16%

commit v1 on v0

v1 whole, which is shorter than its diff:
```python
import math

import jax
import jax.numpy as jnp
from jax import lax
from jax.experimental import pallas as pl
from jax.experimental.pallas import tpu as pltpu
from jax.sharding import PartitionSpec as P

HEADS = 16
HEAD_DIM = 64
ROT = 16
HALF = ROT // 2
SMALL = 128

norm_eps = 1e-05
big_negative = -1e30
f32 = jnp.float32
bf16 = jnp.bfloat16


def dot(left, right):
    return lax.dot_general(left, right, (((1,), (0,)), ((), ())), preferred_element_type=f32)


def rows_dot(left, right):
    return lax.dot_general(left, right, (((0,), (0,)), ((), ())), preferred_element_type=f32)


def cols_dot(left, right):
    return lax.dot_general(left, right, (((1,), (1,)), ((), ())), preferred_element_type=f32)


def shape(dims, kind=bf16):
    return jax.ShapeDtypeStruct(dims, kind)


def held(array):
    *lead, low, high = (1, 1, *array.shape)
    size = jnp.dtype(array.dtype).itemsize
    lines = 32 // size
    return math.prod(lead) * (-(-low // lines) * lines) * (-(-high // 128) * 128) * size


def call(kernel, outs, scratch, scalars, operands, far=(), far_outs=(), after=(), room=3, cost=None):
    vmem = pl.BlockSpec(memory_space=pltpu.VMEM)
    hbm = pl.BlockSpec(memory_space=pl.ANY)
    count = len(operands) + len(far)

    def wrapped(*refs):
        kernel(refs[0], *refs[1 : 1 + count], *refs[1 + count + len(after) :])

    flops, moved = cost or (0, 0)
    moved = moved or sum(held(a) for a in [*operands, *far])
    limit = None
    if room:
        limit = sum(held(a) for a in scratch if "sem" not in str(a.dtype)) + (room << 20)
    results = pl.pallas_call(
        wrapped,
        in_specs=[pl.BlockSpec(memory_space=pltpu.SMEM)]
        + [vmem] * len(operands)
        + [hbm] * len(far)
        + [pl.BlockSpec(memory_space=pl.ANY)] * len(after),
        out_specs=[vmem] * len(outs) + [hbm] * len(far_outs),
        out_shape=[*outs, *far_outs],
        scratch_shapes=scratch,
        compiler_params=pltpu.CompilerParams(vmem_limit_bytes=limit),
        cost_estimate=pl.CostEstimate(flops=flops, bytes_accessed=moved, transcendentals=0),
    )(scalars, *operands, *far, *after)
    return list(results)


def start_all(pairs, sems):
    copies = [
        pltpu.make_async_copy(source, target, sems.at[at]) for at, (source, target) in enumerate(pairs)
    ]
    for copy in copies:
        copy.start()
    return copies


def wait_all(copies):
    for copy in copies:
        copy.wait()


def sems(count):
    return pltpu.SemaphoreType.DMA((count,))


def rows_at(index, count):
    return pl.ds(pl.multiple_of(index * count, count), count)


CORE, Z, S, SUB, LANE = range(5)


def padded(total):
    return -(-total // 128) * 128


def head_lanes(to, part, i, heads, group, lanes, width):
    return part * width + (((to % group) * heads + i) * lanes + to // group) * HEAD_DIM


def pack_call(scalars, group, heads, lanes, w_qkv, w_fc1, w_fc2, vectors, seg):
    share, hidden = w_fc1.shape
    count = group * lanes
    cut = hidden // count
    total = 3 * heads * HEAD_DIM
    width = w_qkv.shape[1] // 3

    def kernel(_, qkv_ref, fc1_ref, fc2_ref, *refs):
        *small_refs, seg_ref, out_ref, small = refs
        small[...] = jnp.zeros_like(small)
        for at, ref in enumerate(small_refs):
            small[at : at + 1, : ref.shape[0]] = ref[...].astype(f32).reshape(1, -1)
        at = len(small_refs)
        small[at : at + 1, : seg_ref.shape[1]] = seg_ref[...].astype(f32)
        rounded = small[...].astype(bf16)
        for to in range(count):
            for part in range(3):
                for i in range(heads):
                    begin = head_lanes(to, part, i, heads, group, lanes, width)
                    put = (part * heads + i) * HEAD_DIM
                    out_ref[to, :, put : put + HEAD_DIM] = qkv_ref[:, begin : begin + HEAD_DIM]
            base = padded(total) + SMALL
            out_ref[to, :, base - SMALL : base] = rounded
            out_ref[to, :, base : base + cut] = fc1_ref[:, to * cut : (to + 1) * cut]
            out_ref[to, :, base + cut :] = fc2_ref[:, to * cut : (to + 1) * cut]

    return call(
        kernel,
        [shape((count, share, padded(total) + SMALL + 2 * cut))],
        [pltpu.VMEM((share, SMALL), f32)],
        scalars,
        (w_qkv, w_fc1, w_fc2, *vectors, seg),
        room=0,
    )[0]


def spread_out_call(scalars, pieces, rows, share, width, group, heads, lanes, cut):
    seqs = len(pieces)
    wide = pieces[0].shape[1]
    chunks = -(-width // wide)
    total = 3 * heads * HEAD_DIM
    ctxs = rows // share
    sizes = (share, share, share, share, 3 * share, 4 * share)

    def kernel(at, *refs):
        far_refs, refs = refs[:seqs], refs[seqs:]
        *refs, local, sem = refs
        wait_all(start_all([(ref, local.at[k]) for k, ref in enumerate(far_refs)], sem))
        in_refs = [local.at[k] for k in range(seqs)]
        gain_ref, shift_ref, out_ref, qkv_ref, fc_ref = refs[:5]
        part_refs, stage, rows_refs, full = refs[5 : 5 + group], refs[5 + group], refs[6 + group : -1], refs[-1]
        for k, ref in enumerate(in_refs):
            slot = lax.rem(at[S] + k, seqs)
            for ctx in range(ctxs):
                block = ref[ctx * share : ctx * share + len(sizes), wide - SMALL :].astype(f32)
                for kind, n in enumerate(sizes):
                    rows_refs[kind][slot, :, ctx * n : (ctx + 1) * n] = block[kind : kind + 1, :n]
            for j in range(chunks):
                upto = min(width - j * wide, wide)
                begin = rows + j * share
                stage[slot, :, j * wide : j * wide + upto] = ref[begin : begin + share, :upto]
        for seq in range(seqs):
            cols = slice(seq * rows, (seq + 1) * rows)
            gain_ref[:, cols] = rows_refs[0][seq]
            shift_ref[:, cols] = rows_refs[1][seq]
            out_ref[:, cols] = rows_refs[2][seq] + rows_refs[3][seq]
            full[:, 3 * seq * rows : 3 * (seq + 1) * rows] = rows_refs[4][seq]
        for part in range(3):
            for i in range(heads):
                head = (at[SUB] * heads + i) * lanes + at[LANE]
                pair = full[:, pl.ds(pl.multiple_of(part * width + head // 2 * 128, 128), 128)]
                put = (part * heads + i) * HEAD_DIM
                low = jnp.full((1, HEAD_DIM), lax.rem(head, 2), jnp.int32) == 0
                qkv_ref[:, put : put + HEAD_DIM] = jnp.where(
                    low, pair[:, :HEAD_DIM], pair[:, HEAD_DIM:]
                )
        per_seq = 4 * rows
        begin = (at[LANE] * group + at[SUB]) * cut
        fc_ref[...] = rows_refs[5][
            begin // per_seq, :, pl.ds(pl.multiple_of(lax.rem(begin, per_seq), 128), cut)
        ]
        for k, ref in enumerate(part_refs):
            for i in range(heads):
                ref[i] = stage[(at[SUB] ^ k) * heads + i]

    return call(
        kernel,
        [shape((1, width), f32)] * 3
        + [shape((1, total), f32), shape((1, cut), f32)]
        + [shape((heads, share, width))] * group,
        [pltpu.VMEM((seqs, share, width), bf16)]
        + [pltpu.VMEM((seqs, 1, ctxs * n), f32) for n in sizes]
        + [pltpu.VMEM((1, 3 * width), f32), pltpu.VMEM((seqs, *pieces[0].shape), bf16), sems(seqs)],
        scalars,
        (),
        far=pieces,
    )


def tables_call(scalars, joint, rows, share, piece):
    ctxs = rows // share
    seq_len = ctxs * piece
    total = joint.shape[1] - SMALL
    powers = [float(10000.0 ** (-2.0 * i / ROT)) for i in range(HALF)]

    def kernel(at, far_ref, first_ref, cos_ref, sin_ref, seg_ref, joint_ref, sem):
        wait_all(start_all([(far_ref, joint_ref)], sem))
        for ctx in range(ctxs):
            block = joint_ref[ctx * share : ctx * share + 8, total : total + piece].astype(f32)
            seg_ref[:, ctx * piece : (ctx + 1) * piece] = block[6:7]
        seg = seg_ref[...]
        first = jnp.zeros((1, seq_len), f32)
        for name in range(1, 4):
            begin = jnp.sum((seg < name).astype(f32), axis=1, keepdims=True)
            first = jnp.where(seg >= name, begin, first)
        first_ref[...] = first.astype(jnp.int32)
        pos = lax.broadcasted_iota(jnp.int32, (HALF, seq_len), 1).astype(f32) - first
        which = lax.broadcasted_iota(jnp.int32, (HALF, seq_len), 0)
        freq = jnp.full((HALF, seq_len), powers[0], f32)
        for i in range(1, HALF):
            freq = jnp.where(which == i, powers[i], freq)
        angle = pos * freq
        cos_ref[...] = jnp.cos(angle)
        sin_ref[...] = jnp.sin(angle)

    return call(
        kernel,
        [shape((1, seq_len), jnp.int32), shape((HALF, seq_len), f32), shape((HALF, seq_len), f32)],
        [pltpu.VMEM((1, seq_len), f32), pltpu.VMEM(joint.shape, bf16), sems(1)],
        scalars,
        (),
        far=(joint,),
    )


def rope_t(x_t, cos_t, sin_t):
    parts = []
    for base in range(0, x_t.shape[0], HEAD_DIM):
        one, two = x_t[base : base + HALF], x_t[base + HALF : base + ROT]
        parts += [
            one * cos_t - two * sin_t,
            two * cos_t + one * sin_t,
            x_t[base + ROT : base + HEAD_DIM],
        ]
    return jnp.concatenate(parts, axis=0)


def scores_of(keys, queries_t, first, begin, here, limit):
    raw = dot(keys[:limit], queries_t[:, begin : begin + here])
    first = first[:, begin : begin + here]
    key_at = lax.broadcasted_iota(jnp.int32, (here, here), 0)
    query_at = lax.broadcasted_iota(jnp.int32, (here, here), 1)
    causal = (key_at <= query_at) & (key_at + begin >= first)
    parts = []
    if begin:
        early = lax.broadcasted_iota(jnp.int32, (begin, here), 0) >= first
        parts.append(jnp.where(early, raw[:begin], big_negative))
    parts.append(jnp.where(causal, raw[begin:], big_negative))
    return jnp.concatenate(parts, axis=0) if begin else parts[0]


def slots(at, refs):
    count = len(refs) // 2
    for k in range(count):
        here = 2 * lax.rem(at[Z] + k, count)
        yield refs[k], here + at[CORE]
        yield refs[count + k], here + 1 - at[CORE]


def attend_call(scalars, block, heads, rows, pieces, gain, shift, weights, bias, tables):
    piece, width = pieces[0].shape
    seq_len = piece * len(pieces)
    seqs = len(weights)
    total = 3 * heads * HEAD_DIM
    own = heads * HEAD_DIM
    tile = min(256, seq_len)

    def kernel(at, *refs):
        n = len(pieces)
        gain_ref, shift_ref, bias_ref, first_ref, cos_ref, sin_ref = refs[:6]
        x_refs, w_refs = refs[6 : 6 + n], refs[6 + n : 6 + n + seqs]
        h_ref, xhat_ref, out_ref, lse_ref, kept_ref, turned_ref, w_ref = refs[
            6 + n + seqs : 13 + n + seqs
        ]
        x_all, qkv, out_t, sem = refs[13 + n + seqs :]
        pairs = [(ref, x_all.at[rows_at(slot, piece), :]) for ref, slot in slots(at, x_refs)]
        pairs += [
            (ref.at[:rows, : padded(total)], w_ref.at[rows_at(lax.rem(at[S] + k, seqs), rows), :])
            for k, ref in enumerate(w_refs)
        ]
        wait_all(start_all(pairs, sem))

        def norm_tile(t, carry):
            here = rows_at(t, tile)
            x = x_all[here, :].astype(f32)
            centred = x - jnp.mean(x, axis=1, keepdims=True)
            rstd = lax.rsqrt(jnp.mean(centred * centred, axis=1, keepdims=True) + norm_eps)
            xhat = centred * rstd
            xhat_ref[here, :] = xhat.astype(bf16)
            h = (xhat * gain_ref[...] + shift_ref[...]).astype(bf16)
            h_ref[here, :] = h
            qkv[here, :] = dot(h, w_ref[:, :total]) + bias_ref[...]
            return carry

        lax.fori_loop(0, seq_len // tile, norm_tile, 0)
        cos_t, sin_t = cos_ref[...], sin_ref[...]
        q_t = rope_t(qkv[:, :own].T, cos_t, sin_t) * 0.125
        k_t = rope_t(qkv[:, own : 2 * own].T, cos_t, sin_t)
        v = qkv[:, 2 * own :]
        kb = k_t.T.astype(bf16)
        kept_ref[:, :own] = q_t.T.astype(bf16)
        kept_ref[:, own : 2 * own] = kb
        kept_ref[:, 2 * own :] = v.astype(bf16)
        q_t = q_t.astype(bf16)
        v_t = v.T.astype(bf16)
        turned_ref[:own] = q_t
        turned_ref[own:] = k_t.astype(bf16)
        begins = first_ref[...]
        for head in range(heads):
            lanes = slice(head * HEAD_DIM, (head + 1) * HEAD_DIM)
            keys, queries_t, values_t = kb[:, lanes], q_t[lanes], v_t[lanes]
            for begin in range(0, seq_len, block):
                limit = begin + block
                scores = scores_of(keys, queries_t, begins, begin, block, limit)
                top = jnp.max(scores, axis=0, keepdims=True)
                expd = jnp.exp(scores - top)
                sums = jnp.sum(expd, axis=0, keepdims=True)
                out = dot(values_t[:, :limit], expd.astype(bf16))
                out_t[lanes, begin:limit] = out * (1.0 / sums)
                lse_ref[head : head + 1, begin:limit] = top + jnp.log(sums)
        out_ref[...] = out_t[...].T.astype(bf16)

    return call(
        kernel,
        [
            shape((seq_len, width)),
            shape((seq_len, width)),
            shape((seq_len, own)),
            shape((heads, seq_len), f32),
            shape((seq_len, total)),
            shape((2 * own, seq_len)),
            shape((width, padded(total))),
        ],
        [
            pltpu.VMEM((seq_len, width), bf16),
            pltpu.VMEM((seq_len, total), f32),
            pltpu.VMEM((own, seq_len), f32),
            sems(len(pieces) + seqs),
        ],
        scalars,
        (gain, shift, bias, *tables),
        far=(*pieces, *weights),
        room=8 * (seq_len // 1024) ** 2,
        cost=(4 * seq_len * width * total, 0),
    )


def attend_back_call(scalars, block, heads, kept, turned, grad, lse, tables, after):
    seq_len, total = kept.shape
    own = total // 3

    def kernel(
        at, kept_ref, turned_ref, grad_ref, lse_ref, first_ref, cos_ref, sin_ref, out_ref, sum_ref, dq_t, dk, dv
    ):
        q = kept_ref[:, :own]
        k = kept_ref[:, own : 2 * own]
        v = kept_ref[:, 2 * own :]
        grad = grad_ref[...]
        q_t, k_t = turned_ref[:own], turned_ref[own:]
        grad_t = grad.astype(f32).T.astype(bf16)
        begins = first_ref[...]
        for head in range(heads):
            lanes = slice(head * HEAD_DIM, (head + 1) * HEAD_DIM)
            q_h, k_h, v_h, grad_h = q[:, lanes], k[:, lanes], v[:, lanes], grad[:, lanes]
            for begin in reversed(range(0, seq_len, block)):
                limit = begin + block
                scores = scores_of(k_h, q_t[lanes], begins, begin, block, limit)
                probs = jnp.exp(scores - lse_ref[head : head + 1, begin:limit])
                grad_p = dot(v_h[:limit], grad_t[lanes, begin:limit])
                delta = jnp.sum(probs * grad_p, axis=0, keepdims=True)
                grad_s = (probs * (grad_p - delta)).astype(bf16)
                dk_here = dot(grad_s, q_h[begin:limit])
                dv_here = dot(probs.astype(bf16), grad_h[begin:limit])
                if limit == seq_len:
                    dk[head] = dk_here
                    dv[head] = dv_here
                else:
                    dk[head, :limit] += dk_here
                    dv[head, :limit] += dv_here
                dq_t[lanes, begin:limit] = dot(k_t[lanes, :limit], grad_s)
        cos_t, sin_t = cos_ref[...], -sin_ref[...]
        dk_all = jnp.concatenate([dk[head] for head in range(heads)], axis=1)
        dv_all = jnp.concatenate([dv[head] for head in range(heads)], axis=1)
        for part, value in (
            (0, rope_t(dq_t[...] * 0.125, cos_t, sin_t).T),
            (1, rope_t(dk_all.T, cos_t, sin_t).T),
            (2, dv_all),
        ):
            rounded = value.astype(bf16)
            cols = slice(part * own, (part + 1) * own)
            out_ref[:, cols] = rounded
            sum_ref[:, cols] = jnp.sum(rounded.astype(f32), axis=0, keepdims=True)

    return call(
        kernel,
        [shape((seq_len, total)), shape((1, total), f32)],
        [
            pltpu.VMEM((own, seq_len), f32),
            pltpu.VMEM((heads, seq_len, HEAD_DIM), f32),
            pltpu.VMEM((heads, seq_len, HEAD_DIM), f32),
        ],
        scalars,
        (kept, turned, grad, lse, *tables),
        after=after,
        room=8 * (seq_len // 1024) ** 2,
        cost=(10 * seq_len * seq_len * own, 0),
    )


ROOT = 0.7978845608028654
CUBIC = 0.044715


def split_rows(at, z, piece, value, stage, mine_ref, theirs_ref, sem):
    stage[z] = value.astype(bf16)
    mine_ref[rows_at(z, piece), :] = stage[z, rows_at(at[CORE], piece), :]
    out_rows(at, z, piece, stage, theirs_ref, sem).start()


def out_rows(at, z, piece, stage, theirs_ref, sem):
    return pltpu.make_async_copy(
        stage.at[z, rows_at(1 - at[CORE], piece), :], theirs_ref.at[rows_at(z, piece), :], sem.at[z]
    )


def forward_call(scalars, rows, piece, h, weights, bias, attn, out_parts):
    seq_len, width = h.shape
    cut = weights[0].shape[1] // 2
    seqs = len(weights)
    tile = 2 * piece
    half = seq_len // 2
    count = seq_len // tile

    heads, share, _ = out_parts[0].shape
    group = len(out_parts)

    def kernel(at, h_ref, bias_ref, attn_ref, *refs):
        w_refs, part_refs, refs = refs[:seqs], refs[seqs : seqs + group], refs[seqs + group :]
        w_ref, slope_ref, act_ref, mine_ref, w_out_ref, theirs_ref, stage, sem, sem_out = refs
        pairs = [
            (ref, w_ref.at[rows_at(lax.rem(at[S] + k, seqs), rows), :])
            for k, ref in enumerate(w_refs)
        ]
        for k, ref in enumerate(part_refs):
            for i in range(heads):
                begin = i * HEAD_DIM + (at[SUB] ^ k) * share
                here = pl.ds(pl.multiple_of(begin, share), share)
                pairs.append((ref.at[i], w_out_ref.at[here, :]))
        wait_all(start_all(pairs, sem))

        def step(t, carry):
            here = rows_at(t, tile)
            v = dot(h_ref[here, :], w_ref[:, :cut]) + bias_ref[...]
            square = v * v
            t_v = jnp.tanh(ROOT * (v + CUBIC * (square * v)))
            halved = 0.5 * (1.0 + t_v)
            act = (v * halved).astype(bf16)
            act_ref[here, :] = act
            slope = halved + 0.5 * v * (1.0 - t_v * t_v) * (ROOT * (1.0 + (3.0 * CUBIC) * square))
            slope_ref[here, :] = slope.astype(bf16)
            out = dot(attn_ref[here, :], w_out_ref[...]) + cols_dot(act, w_ref[:, cut:])
            split_rows(at, t, piece, out, stage, mine_ref, theirs_ref, sem_out)
            return carry

        lax.fori_loop(0, count, step, 0)
        wait_all([out_rows(at, z, piece, stage, theirs_ref, sem_out) for z in range(count)])

    return call(
        kernel,
        [
            shape((width, 2 * cut)),
            shape((seq_len, cut)),
            shape((seq_len, cut)),
            shape((half, width)),
            shape((heads * HEAD_DIM, width)),
        ],
        [pltpu.VMEM((count, tile, width), bf16), sems(seqs + group * heads), sems(count)],
        scalars,
        (h, bias, attn),
        far=(*weights, *out_parts),
        far_outs=[shape((half, width))],
        cost=(4 * seq_len * width * cut, 0),
    )


def middle_call(scalars, piece, mine, theirs):
    half, width = mine.shape
    count = half // piece

    def kernel(at, mine_ref, theirs_ref, keep_ref, *refs):
        sends, (got, made, sem, sem_out) = refs[: count - 1], refs[count - 1 :]
        here = [rows_at(lax.rem(at[Z] + count - k, count), piece) for k in range(count)]
        order = [*range(1, count), 0]
        copies = start_all([(theirs_ref.at[here[k], :], got.at[k]) for k in order], sem)
        outs = []
        for copy, k in zip(copies, order):
            copy.wait()
            value = mine_ref[here[k], :].astype(f32) + got[k].astype(f32)
            if k == 0:
                keep_ref[...] = value
            else:
                made[k - 1] = value.astype(bf16)
                out = pltpu.make_async_copy(made.at[k - 1], sends[k - 1], sem_out.at[k - 1])
                out.start()
                outs.append(out)
        wait_all(outs)

    return call(
        kernel,
        [shape((piece, width), f32)],
        [
            pltpu.VMEM((count, piece, width), bf16),
            pltpu.VMEM((count - 1, piece, width), bf16),
            sems(count),
            sems(count - 1),
        ],
        scalars,
        (mine,),
        far=(theirs,),
        far_outs=[shape((piece, width))] * (count - 1),
    )


def backward_call(scalars, pieces, weight, w_out, slope):
    piece, width = pieces[0].shape
    seq_len, cut = slope.shape
    own = w_out.shape[0]
    tile = min(256, seq_len)

    def kernel(at, *refs):
        n = len(pieces)
        (w_ref, w_out_ref, slope_ref), dy_refs = refs[:3], refs[3 : 3 + n]
        dy_ref, dfc_ref, dattn_ref, sum_ref, sem = refs[3 + n :]
        pairs = [(ref, dy_ref.at[rows_at(slot, piece), :]) for ref, slot in slots(at, dy_refs)]
        wait_all(start_all(pairs, sem))
        sum_ref[...] = jnp.zeros_like(sum_ref)

        def step(t, carry):
            here = rows_at(t, tile)
            dy = dy_ref[here, :]
            dfc = (dot(dy, w_ref[:, cut:]) * slope_ref[here, :].astype(f32)).astype(bf16)
            dfc_ref[here, :] = dfc
            sum_ref[...] += jnp.sum(dfc.astype(f32), axis=0, keepdims=True)
            dattn_ref[here, :] = cols_dot(dy, w_out_ref[...]).astype(bf16)
            return carry

        lax.fori_loop(0, seq_len // tile, step, 0)

    return call(
        kernel,
        [shape((seq_len, width)), shape((seq_len, cut)), shape((seq_len, own)), shape((1, cut), f32)],
        [sems(len(pieces))],
        scalars,
        (weight, w_out, slope),
        far=pieces,
        cost=(2 * seq_len * width * cut, 0),
    )


def input_grad_call(scalars, piece, dfc, weight, dqkv, w_qkv, xhat):
    seq_len, cut = dfc.shape
    width = weight.shape[0]
    total = dqkv.shape[1]
    tile = 2 * piece
    half = seq_len // 2
    count = seq_len // tile

    def kernel(at, dfc_ref, w_ref, dqkv_ref, w_qkv_ref, xhat_ref, mine_ref, gain_ref, shift_ref, theirs_ref, stage, sem_out):
        gain_ref[...] = jnp.zeros_like(gain_ref)
        shift_ref[...] = jnp.zeros_like(shift_ref)

        def step(t, carry):
            here = rows_at(t, tile)
            value = cols_dot(dfc_ref[here, :], w_ref[:, :cut]) + cols_dot(
                dqkv_ref[here, :], w_qkv_ref[:, :total]
            )
            gain_ref[...] += jnp.sum(value * xhat_ref[here, :].astype(f32), axis=0, keepdims=True)
            shift_ref[...] += jnp.sum(value, axis=0, keepdims=True)
            split_rows(at, t, piece, value, stage, mine_ref, theirs_ref, sem_out)
            return carry

        lax.fori_loop(0, count, step, 0)
        wait_all([out_rows(at, z, piece, stage, theirs_ref, sem_out) for z in range(count)])

    return call(
        kernel,
        [shape((half, width)), shape((1, width), f32), shape((1, width), f32)],
        [pltpu.VMEM((count, tile, width), bf16), sems(count)],
        scalars,
        (dfc, weight, dqkv, w_qkv, xhat),
        far_outs=[shape((half, width))],
        cost=(2 * seq_len * width * cut, 0),
    )


def split_fc_call(scalars, seqs, grad_fc1, grad_fc2):
    width, cut = grad_fc1.shape
    rows = width // seqs

    def kernel(at, one_ref, two_ref, *refs):
        *outs, sem = refs
        pairs = []
        for k, ref in enumerate(outs):
            here = rows_at(lax.rem(at[S] + seqs - k, seqs), rows)
            pairs += [
                (one_ref.at[here, :], ref.at[:, :cut]),
                (two_ref.at[here, :], ref.at[:, cut:]),
            ]
        wait_all(start_all(pairs, sem))

    return call(
        kernel,
        [],
        [sems(2 * seqs)],
        scalars,
        (grad_fc1, grad_fc2),
        far_outs=[shape((rows, 2 * cut))] * seqs,
    )


def sum_fc_call(scalars, pieces):
    rows, lanes = pieces[0].shape
    count = len(pieces)
    tiles = 2
    tile = rows // tiles

    def kernel(at, *refs):
        far_refs, (out_ref, got, made, sem, sem_out) = refs[:count], refs[count:]
        starts = [slice(t * tile, (t + 1) * tile) for t in range(tiles)]
        copies = start_all(
            [(ref.at[here, :], got.at[k, here, :]) for here in starts for k, ref in enumerate(far_refs)],
            sem,
        )
        outs = []
        for t, here in enumerate(starts):
            wait_all(copies[t * count : (t + 1) * count])
            made[here, :] = sum(got[k, here, :].astype(f32) for k in range(count)).astype(bf16)
            out = pltpu.make_async_copy(made.at[here, :], out_ref.at[here, :], sem_out.at[t])
            out.start()
            outs.append(out)
        wait_all(outs)

    return call(
        kernel,
        [],
        [
            pltpu.VMEM((count, rows, lanes), bf16),
            pltpu.VMEM((rows, lanes), bf16),
            sems(tiles * count),
            sems(tiles),
        ],
        scalars,
        (),
        far=pieces,
        far_outs=[shape((rows, lanes))],
    )[0]


def small_rows(share):
    return 5, (2 if share >= 10 else 1)


def put_small(block_ref, base, share, lane0, values):
    kinds, parts = small_rows(share)
    for kind, value in enumerate(values):
        high = value.astype(bf16)
        block_ref[base + kind : base + kind + 1, lane0 : lane0 + value.shape[1]] = high.astype(f32)
        if parts == 2:
            row = base + kinds + kind
            block_ref[row : row + 1, lane0 : lane0 + value.shape[1]] = value - high.astype(f32)


def split_qkv_call(scalars, seqs, share, group, heads, lanes_c, grad_qkv, grad_out, halves, vectors):
    width, total = grad_qkv.shape
    rows = width // seqs
    lanes = padded(total) + SMALL
    chunks = -(-width // lanes)
    out_rows = rows + chunks * share
    ctxs = rows // share

    def kernel(at, qkv_ref, out_grad_ref, *refs):
        half_refs, refs = refs[: group - 1], refs[group - 1 :]
        (gain_ref, shift_ref, dy_ref, sum_qkv_ref, sum_fc_ref) = refs[:5]
        outs, (stage, small, full_y, full_qkv, full_fc, sem) = refs[5 : 5 + seqs], refs[5 + seqs :]
        full_y[...] = jnp.sum(dy_ref[...].astype(f32), axis=0, keepdims=True)
        full_qkv[...] = jnp.zeros_like(full_qkv)
        full_fc[...] = jnp.zeros_like(full_fc)
        cut = sum_fc_ref.shape[1]
        begin = (at[LANE] * group + at[SUB]) * cut
        full_fc[:, pl.ds(pl.multiple_of(begin, cut), cut)] = sum_fc_ref[...]
        nothing = jnp.zeros((1, HEAD_DIM), f32)
        for part in range(3):
            for i in range(heads):
                head = (at[SUB] * heads + i) * lanes_c + at[LANE]
                take = (part * heads + i) * HEAD_DIM
                value = sum_qkv_ref[:, take : take + HEAD_DIM]
                low = jnp.full((1, 2 * HEAD_DIM), lax.rem(head, 2), jnp.int32) == 0
                put = pl.ds(pl.multiple_of(part * width + head // 2 * 128, 128), 128)
                full_qkv[:, put] = jnp.where(
                    low,
                    jnp.concatenate([value, nothing], axis=1),
                    jnp.concatenate([nothing, value], axis=1),
                )
        vector_refs = (gain_ref, shift_ref, full_y, full_qkv, full_fc)

        def put_out(slot, value):
            for j in range(chunks):
                upto = min(width - j * lanes, lanes)
                begin = rows + j * share
                stage[slot, begin : begin + share, :upto] = value[:, j * lanes : j * lanes + upto]

        for k in range(group):
            for i in range(heads):
                slot = (at[SUB] ^ k) * heads + i
                if k:
                    put_out(slot, half_refs[k - 1][i])
                else:
                    here = pl.ds(pl.multiple_of(i * HEAD_DIM + at[SUB] * share, share), share)
                    put_out(slot, out_grad_ref[here, :])
        small[...] = jnp.zeros_like(small)
        sizes = [ref.shape[1] // (seqs * ctxs) for ref in vector_refs]
        for seq in range(seqs):
            for ctx in range(ctxs):
                owner = seq * ctxs + ctx
                values = [
                    ref[:, owner * n : (owner + 1) * n] for ref, n in zip(vector_refs, sizes)
                ]
                put_small(small, ctx * share, share, 0, values)
            stage[seq, :rows, :total] = qkv_ref[seq * rows : (seq + 1) * rows, :]
            stage[seq, :rows, lanes - SMALL :] = small[...].astype(bf16)
        wait_all(
            start_all(
                [(stage.at[lax.rem(at[S] + seqs - k, seqs)], ref) for k, ref in enumerate(outs)], sem
            )
        )

    return call(
        kernel,
        [],
        [
            pltpu.VMEM((seqs, out_rows, lanes), bf16),
            pltpu.VMEM((rows, SMALL), f32),
            pltpu.VMEM((1, width), f32),
            pltpu.VMEM((1, 3 * width), f32),
            pltpu.VMEM((1, 4 * width), f32),
            sems(seqs),
        ],
        scalars,
        (grad_qkv, grad_out, *halves, *vectors),
        far_outs=[shape((out_rows, lanes))] * seqs,
    )


def sum_qkv_call(scalars, share, width, rows, pieces):
    lanes = pieces[0].shape[1]
    chunks = -(-width // lanes)
    kinds, parts = small_rows(share)
    ctxs = rows // share

    def kernel(at, *refs):
        far_refs, (w_out_ref, out_ref, sums, got, made, sem, sem_out) = (
            refs[: len(pieces)],
            refs[len(pieces) :],
        )
        wait_all(start_all([(ref, got.at[k]) for k, ref in enumerate(far_refs)], sem))
        sums[...] = sum(got[k].astype(f32) for k in range(len(pieces)))
        for j in range(chunks):
            upto = min(width - j * lanes, lanes)
            begin = rows + j * share
            w_out_ref[:, j * lanes : j * lanes + upto] = sums[begin : begin + share, :upto]
        if parts == 2:
            for ctx in range(ctxs):
                base = ctx * share
                here = sums[base : base + kinds, lanes - SMALL :]
                left = sums[base + kinds : base + 2 * kinds, lanes - SMALL :]
                value = here + left
                high = value.astype(bf16).astype(f32)
                sums[base : base + kinds, lanes - SMALL :] = high
                sums[base + kinds : base + 2 * kinds, lanes - SMALL :] = value - high
        made[...] = sums[:rows, :].astype(bf16)
        wait_all(start_all([(made, out_ref)], sem_out))

    return call(
        kernel,
        [shape((share, width), f32)],
        [
            pltpu.VMEM(pieces[0].shape, f32),
            pltpu.VMEM((len(pieces), *pieces[0].shape), bf16),
            pltpu.VMEM((rows, lanes), bf16),
            sems(len(pieces)),
            sems(1),
        ],
        scalars,
        (),
        far=pieces,
        far_outs=[shape((rows, lanes))],
    )


def home_fc_call(scalars, got):
    ctxs, share, double = got.shape
    cut = double // 2

    def kernel(at, got_ref, one_ref, two_ref):
        for ctx in range(ctxs):
            cols = slice(ctx * cut, (ctx + 1) * cut)
            one_ref[:, cols] = got_ref[ctx, :, :cut].astype(f32)
            two_ref[:, cols] = got_ref[ctx, :, cut:].astype(f32)

    return call(kernel, [shape((share, ctxs * cut), f32)] * 2, [], scalars, (got,), room=0)


def home_qkv_call(scalars, group, heads, lanes, width, got):
    ctxs, share, wide = got.shape
    kinds, parts = small_rows(share)
    sizes = (share, share, share, 3 * share, 4 * share, share)
    kind_of = (0, 1, 2, 3, 4, 2)

    def kernel(at, got_ref, out_ref, *small_refs):
        for ctx in range(ctxs):
            for part in range(3):
                for i in range(heads):
                    put = head_lanes(ctx, part, i, heads, group, lanes, width)
                    take = (part * heads + i) * HEAD_DIM
                    out_ref[:, put : put + HEAD_DIM] = got_ref[
                        ctx, :, take : take + HEAD_DIM
                    ].astype(f32)
        sums = sum(got_ref[ctx, :, wide - SMALL :].astype(f32) for ctx in range(ctxs))
        for kind, n, ref in zip(kind_of, sizes, small_refs):
            value = sums[kind : kind + 1, :]
            if parts == 2:
                value = value + sums[kinds + kind : kinds + kind + 1, :]
            ref[...] = value[:, :n]

    return call(
        kernel,
        [shape((share, 3 * width), f32)] + [shape((1, n), f32) for n in sizes],
        [],
        scalars,
        (got,),
        room=0,
    )


def finish_call(scalars, x, dy, gain, keep, parts):
    def kernel(at, x_ref, dy_ref, gain_ref, keep_ref, *refs):
        *part_refs, out_ref = refs
        dh = keep_ref[...] + sum(ref[...].astype(f32) for ref in part_refs)
        here = x_ref[...].astype(f32)
        centred = here - jnp.mean(here, axis=1, keepdims=True)
        rstd = lax.rsqrt(jnp.mean(centred * centred, axis=1, keepdims=True) + norm_eps)
        xhat = centred * rstd
        scaled = dh * gain_ref[...]
        out_ref[...] = dy_ref[...].astype(f32) + rstd * (
            scaled
            - jnp.mean(scaled, axis=1, keepdims=True)
            - xhat * jnp.mean(scaled * xhat, axis=1, keepdims=True)
        )

    return call(kernel, [shape(x.shape, f32)], [], scalars, (x, dy, gain, keep, *parts), room=0)[0]


def body(
    block_in,
    cotangent,
    segments,
    ln_gain,
    ln_bias,
    w_qkv,
    b_qkv,
    w_out,
    b_out,
    w_fc1,
    b_fc1,
    w_fc2,
    b_fc2,
):
    seqs, ctxs = lax.axis_size("seq"), lax.axis_size("ctx")
    s, c = lax.axis_index("seq"), lax.axis_index("ctx")
    _, piece, width = block_in.shape
    seq_len = piece * ctxs
    share = w_qkv.shape[0]
    hidden = w_fc1.shape[1]
    cut = hidden // ctxs
    heads = HEADS // ctxs
    group = HEAD_DIM // share
    lanes = ctxs // group
    rows = ctxs * share
    zs = ctxs // 2
    sub, lane = c % group, c // group
    scalars = jnp.stack([c % 2, c // 2, s, sub, lane]).astype(jnp.int32)
    total = 3 * heads * HEAD_DIM
    x_here, dy_here = block_in[0], cotangent[0]

    def from_z(k):
        return [(i, ((i // 2 - k) % zs) * 2 + i % 2) for i in range(ctxs)]

    def from_s(k):
        return [(i, (i - k) % seqs) for i in range(seqs)]

    def partner(k):
        return [(i, i ^ k) for i in range(ctxs)]

    def along(axis, parts, pairs):
        return [lax.ppermute(part, axis, pair) for part, pair in zip(parts, pairs)]

    hops_z = [from_z(k) for k in range(1, zs)]
    hops_s = [from_s(k) for k in range(1, seqs)]
    hops_g = [partner(k) for k in range(1, group)]

    def spread_ctx(local):
        mine = [local] + along("ctx", [local] * (zs - 1), hops_z)
        return mine + along("ctx", mine, [partner(1)] * zs)

    def swap_ctx(blocks):
        return lax.all_to_all(blocks, "ctx", split_axis=0, concat_axis=0, tiled=True)

    packed = pack_call(
        scalars,
        group,
        heads,
        lanes,
        w_qkv,
        w_fc1,
        w_fc2,
        (ln_gain, ln_bias, b_out, b_fc2, b_qkv, b_fc1),
        segments,
    )
    got = swap_ctx(packed)
    wide = padded(total) + SMALL
    chunks = -(-width // wide)
    w_out_wide = jnp.pad(w_out, ((0, 0), (0, chunks * wide - width)))
    joint = jnp.concatenate(
        [got[:, :, :wide].reshape(rows, wide)]
        + [w_out_wide[:, j * wide : (j + 1) * wide] for j in range(chunks)]
    )
    joint = [joint] + along("seq", [joint] * (seqs - 1), hops_s)
    fc_here = got[:, :, wide:].reshape(rows, 2 * cut)
    w_fc = [fc_here] + along("seq", [fc_here] * (seqs - 1), hops_s)
    x_all = spread_ctx(x_here)
    dy_all = spread_ctx(dy_here)

    tables = tables_call(scalars, joint[0], rows, share, piece)
    gain, shift, bias_out, bias_qkv, bias_fc1, *out_parts = spread_out_call(
        scalars, joint, rows, share, width, group, heads, lanes, cut
    )
    out_parts = out_parts[:1] + along("ctx", out_parts[1:], hops_g)

    block = min(256, seq_len)
    h, xhat, attn, lse, kept, turned, w_qkv_c = attend_call(
        scalars, block, heads, rows, x_all, gain, shift, joint, bias_qkv, tables
    )
    w_fc_c, slope, act, out_mine, w_out_c, out_theirs = forward_call(
        scalars, rows, piece, h, w_fc, bias_fc1, attn, out_parts
    )
    out_theirs = along("ctx", [out_theirs], [partner(1)])[0]
    out_keep, *out_sends = middle_call(scalars, piece, out_mine, out_theirs)
    out_parts = along("ctx", out_sends, hops_z)
    block_out = x_here.astype(f32) + out_keep + bias_out
    for part in out_parts:
        block_out = block_out + part.astype(f32)
    block_out = block_out.astype(bf16)

    dy, dfc, dattn, sum_fc1 = backward_call(scalars, dy_all, w_fc_c, w_out_c, slope)
    grad_fc1 = rows_dot(h, dfc).astype(bf16)
    grad_fc2 = rows_dot(dy, act).astype(bf16)
    fc_parts = split_fc_call(scalars, seqs, grad_fc1, grad_fc2)
    fc_parts = fc_parts[:1] + along("seq", fc_parts[1:], hops_s)
    grad_out = rows_dot(attn, dy).astype(bf16)
    blocks = grad_out.reshape(heads, group, share, width)
    halves = [lax.dynamic_index_in_dim(blocks, sub ^ k, 1, keepdims=False) for k in range(1, group)]
    halves = along("ctx", halves, hops_g)
    dqkv, sum_qkv = attend_back_call(
        scalars, block, heads, kept, turned, dattn, lse, tables, (fc_parts[0],)
    )
    dh_mine, sum_gain, sum_shift, dh_theirs = input_grad_call(
        scalars, piece, dfc, w_fc_c, dqkv, w_qkv_c, xhat
    )
    dh_theirs = along("ctx", [dh_theirs], [partner(1)])[0]
    grad_qkv = rows_dot(h, dqkv).astype(bf16)
    qkv_parts = split_qkv_call(
        scalars,
        seqs,
        share,
        group,
        heads,
        lanes,
        grad_qkv,
        grad_out,
        halves,
        (sum_gain, sum_shift, dy_here, sum_qkv, sum_fc1),
    )
    qkv_parts = qkv_parts[:1] + along("seq", qkv_parts[1:], hops_s)
    dh_keep, *dh_sends = middle_call(scalars, piece, dh_mine, dh_theirs)
    dh_parts = along("ctx", dh_sends, hops_z)

    fc_sum = sum_fc_call(scalars, fc_parts)
    fc_home = swap_ctx(fc_sum.reshape(ctxs, share, 2 * cut))
    out_wout, qkv_sum = sum_qkv_call(scalars, share, width, rows, qkv_parts)
    qkv_home = swap_ctx(qkv_sum.reshape(ctxs, share, wide))
    grad_in = finish_call(scalars, x_here, dy_here, gain, dh_keep, dh_parts)
    out_wfc1, out_wfc2 = home_fc_call(scalars, fc_home)
    out_wqkv, *small = home_qkv_call(scalars, group, heads, lanes, width, qkv_home)
    small = [value.reshape(-1) for value in small]
    return (
        block_out[None],
        grad_in[None],
        small[0],
        small[1],
        out_wqkv,
        small[3],
        out_wout,
        small[2],
        out_wfc1,
        small[4],
        out_wfc2,
        small[5],
    )


def solution(mesh):
    both = ("seq", "ctx")
    tokens, flat, matrix = P("seq", "ctx", None), P(both), P(both, None)
    in_specs = (tokens, tokens, P("seq", "ctx"), flat, flat) + (matrix, flat) * 4
    out_specs = (tokens, tokens, flat, flat) + (matrix, flat) * 4
    return jax.shard_map(body, mesh=mesh, in_specs=in_specs, out_specs=out_specs, check_vma=False)
```

time: 271 us -> 265 us (0.978)
  waiting for transfers between devices: 86.5 us -> 118 us
  other arithmetic: 13.8 us -> 0.94 us
  Pallas kernels: 67.9 us -> 55.5 us
  local copies, waits for them, and re-layouts: 22.3 us -> 10.9 us
  matrix products: 10.4 us -> 4.36 us
  starting transfers between devices: 67.8 us -> 73.2 us
    ppermute x36, waiting for transfers between devices: 62.5 us -> 118 us  [along(): return [lax.ppermute(part, axis, pair) for part, pair in zip(parts, pairs)]]
    all_to_all x3, waiting for transfers between devices: 24 us -> 0.01 us  [swap_ctx(): lax.all_to_all(blocks, 'ctx', split_axis=0, concat_axis=0, tiled=True)]
    pallas_call x15 -> x17, Pallas kernels: 67.9 us -> 55.5 us  [call(): pl.pallas_call(wrapped, in_specs=[pl.BlockSpec(memory_space=pltpu.SMEM)]...]
    dot_general x4, matrix products: 10.4 us -> 4.36 us  [rows_dot(): lax.dot_general(left, right, (((0,), (0,)), ((), ())), preferred_element_...]
    ppermute x36, starting transfers between devices: 50.8 us -> 56.7 us  [along(): return [lax.ppermute(part, axis, pair) for part, pair in zip(parts, pairs)]]
    concatenate x3 -> x0, local copies, waits for them, and re-layouts: 5.24 us -> none  [the longest x1 1.75 us: body(): jnp.concatenate([sin_t, empty, zero] * heads, axis=1)]
    select_n x3 -> x0, other arithmetic: 4.61 us -> none  [the longest x2 4.54 us: body(): first = jnp.where(seg >= name, begin, first)]
    unnamed x87 -> x44, local copies, waits for them, and re-layouts: 9.37 us -> 9.11 us
  transfers between devices with their start and end apart: 39 -> 39, of which waited for: 12 -> 15; matrix products, arithmetic and copies ran while one was open for 10% -> 1% of each run, Pallas kernels for 16% -> 13%
where the time goes in v1:
time: 265 us; the launch traced here: 264 us
  waiting for transfers between devices  118 us (45%)
  starting transfers between devices  73.2 us (28%)
  Pallas kernels  55.5 us (21%)
  local copies, waits for them, and re-layouts  10.9 us (4%)
  matrix products  4.36 us (2%)
    ppermute x36, waiting for transfers between devices, along(): return [lax.ppermute(part, axis, pair) for part, pair in zip(parts, pairs)]  118 us
    ppermute x36, starting transfers between devices, along(): return [lax.ppermute(part, axis, pair) for part, pair in zip(parts, pairs)]  56.7 us
    pallas_call x17, Pallas kernels, call(): pl.pallas_call(wrapped, in_specs=[pl.BlockSpec(memory_space=pltpu.SMEM)]...  55.5 us
    all_to_all x3, starting transfers between devices, swap_ctx(): lax.all_to_all(blocks, 'ctx', split_axis=0, concat_axis=0, tiled=True)  16.5 us
    unnamed x44, local copies, waits for them, and re-layouts  9.11 us
  transfers between devices with their start and end apart: 39, of which 15 were waited for; matrix products, arithmetic and copies ran while one was open for 1% of the time, Pallas kernels for 13%

profile of v1, /device:TPU:0, one launch (start us, length us, event | category | flops | bytes accessed | tf_op | source)
XLA Modules:
  0.0 263.8 jit_solution(15749509376280854434)
XLA Ops:
  1.3 2.3 shard_map.220
  3.6 6.5 %all-to-all-start = ((bf16[8,32,1536]{2,1,0:T(8,128)(2,1)}), bf16[8,32,1536]{2,1,0:T(8,128)(2,1)S(1)}, u32[]{:S(2)}, u32[]{:S(2)}) async-start(bf16[8,32,1536]{2,1,0:T(8,128)(2,1)} %shard_map.220), calls=%async_computation | async-start | bytes 1572864 | tf_op jit(solution)/shard_map/all_to_all | solution.py:931
  10.1 3.8 %collective-permute-start.3 = (bf16[128,1024]{1,0:T(8,128)(2,1)S(1)}, bf16[128,1024]{1,0:T(8,128)(2,1)S(1)}, u32[]{:S(2)}, u32[]{:S(2)}) collective-permute-start(bf16[128,1024]{1,0:T(8,128)(2,1)S(1)} %bitcast.42), channel_id=1, source_target_pairs={{0,6},{1,7},{2,0},{3,1},{4,2},{5,3},{6,4},{7,5},{8,14},{9,15},{10,... | collective-permute-start | bytes 786440 | tf_op jit(solution)/shard_map/ppermute | solution.py:920
  14.0 1.1 collective-permute-start.5
  15.1 2.7 %collective-permute-start.18 = (bf16[128,1024]{1,0:T(8,128)(2,1)S(1)}, bf16[128,1024]{1,0:T(8,128)(2,1)S(1)}, u32[]{:S(2)}, u32[]{:S(2)}) collective-permute-start(bf16[128,1024]{1,0:T(8,128)(2,1)S(1)} %bitcast.34), channel_id=1, source_target_pairs={{0,6},{1,7},{2,0},{3,1},{4,2},{5,3},{6,4},{7,5},{8,14},{9,15},{10,... | collective-permute-start | bytes 786440 | tf_op jit(solution)/shard_map/ppermute | solution.py:920
  17.8 14.4 %collective-permute-done.3.refs_8_ = bf16[128,1024]{1,0:T(8,128)(2,1)S(1)} collective-permute-done((bf16[128,1024]{1,0:T(8,128)(2,1)S(1)}, bf16[128,1024]{1,0:T(8,128)(2,1)S(1)}, u32[]{:S(2)}, u32[]{:S(2)}) %collective-permute-start.3) | collective-permute-done | bytes 262176 | tf_op jit(solution)/shard_map/ppermute | solution.py:920
  32.1 15.9 %collective-permute-start.19 = (bf16[128,1024]{1,0:T(8,128)(2,1)S(1)}, bf16[128,1024]{1,0:T(8,128)(2,1)S(1)}, u32[]{:S(2)}, u32[]{:S(2)}) collective-permute-start(bf16[128,1024]{1,0:T(8,128)(2,1)S(1)} %bitcast.35), channel_id=1, source_target_pairs={{0,4},{1,5},{2,6},{3,7},{4,0},{5,1},{6,2},{7,3},{8,12},{9,13},{10,... | collective-permute-start | bytes 786440 | tf_op jit(solution)/shard_map/ppermute | solution.py:920
  48.1 11.6 %collective-permute-done.4.refs_9_ = bf16[128,1024]{1,0:T(8,128)(2,1)S(1)} collective-permute-done((bf16[128,1024]{1,0:T(8,128)(2,1)S(1)}, bf16[128,1024]{1,0:T(8,128)(2,1)S(1)}, u32[]{:S(2)}, u32[]{:S(2)}) %collective-permute-start.4) | collective-permute-done | bytes 262176 | tf_op jit(solution)/shard_map/ppermute | solution.py:920
  61.3 2.4 collective-permute-start
  64.3 11.8 %collective-permute-done.19.refs_6_ = bf16[128,1024]{1,0:T(8,128)(2,1)S(1)} collective-permute-done((bf16[128,1024]{1,0:T(8,128)(2,1)S(1)}, bf16[128,1024]{1,0:T(8,128)(2,1)S(1)}, u32[]{:S(2)}, u32[]{:S(2)}) %collective-permute-start.19) | collective-permute-done | bytes 262176 | tf_op jit(solution)/shard_map/ppermute | solution.py:920
  76.1 1.5 collective-permute-start.2
  78.6 1.5 collective-permute-start.10
  80.8 1.5 collective-permute-start.11
  83.0 4.6 %collective-permute-done.2.refs_4_.refs_18_ = bf16[320,512]{1,0:T(8,128)(2,1)S(1)} collective-permute-done((bf16[320,512]{1,0:T(8,128)(2,1)S(1)}, bf16[320,512]{1,0:T(8,128)(2,1)S(1)}, u32[]{:S(2)}, u32[]{:S(2)}) %collective-permute-start.2) | collective-permute-done | bytes 327712 | tf_op jit(solution)/shard_map/ppermute | solution.py:920
  87.6 1.9 shard_map.221
  92.4 6.6 %collective-permute-done.10.refs_5_ = bf16[256,1024]{1,0:T(8,128)(2,1)} collective-permute-done((bf16[256,1024]{1,0:T(8,128)(2,1)S(1)}, bf16[256,1024]{1,0:T(8,128)(2,1)}, u32[]{:S(2)}, u32[]{:S(2)}) %collective-permute-start.10) | collective-permute-done | bytes 524320 | tf_op jit(solution)/shard_map/ppermute | solution.py:920
  104.2 8.6 %shard_map.223 = (bf16[1024,1024]{1,0:T(8,128)(2,1)S(1)}, bf16[1024,1024]{1,0:T(8,128)(2,1)S(1)}, bf16[1024,128]{1,0:T(8,128)(2,1)S(1)}, f32[2,1024]{1,0:T(2,128...) custom-call(s32[5]{0:T(128)S(1)} %copy-done.4, ...), custom_call_target="tpu_custom_call" | custom-call | flops 1610612736 | bytes 3584000 | tf_op jit(solution)/shard_map/pallas_call | solution.py:58
  112.9 7.7 %shard_map.224 = (bf16[1024,1024]{1,0:T(8,128)(2,1)S(1)}, bf16[1024,512]{1,0:T(8,128)(2,1)S(1)}, bf16[1024,512]{1,0:T(8,128)(2,1)S(1)}, bf16[512,1024]{1,0:T(8,1...) custom-call(s32[5]{0:T(128)S(1)} %copy-done.4, bf16[1024,1024]{1,0:T(8,128)(2,1)S(1)} %get-tuple-element.78.refs_1_, ...), custom_call_target="tpu_custom_call" | custom-call | flops 2147483648 | bytes 4734976 | tf_op jit(solution)/shard_map/pallas_call | solution.py:58
  120.6 4.1 %shard_map.226 = (bf16[1024,1024]{1,0:T(8,128)(2,1)S(1)}, bf16[1024,512]{1,0:T(8,128)(2,1)S(1)}, bf16[1024,128]{1,0:T(8,128)(2,1)S(1)}, f32[1,512]{1,0:T(1,128)S(1)}) custom-call(s32[5]{0:T(128)S(1)} %copy-done.4, bf16[1024,1024]{1,0:T(8,128)(2,1)S(1)} %get-tuple-element.90.refs_1_.refs_2_, bf16[128,1024]{1,0:T(8,128)(2,1)S(1)} %get-tuple-element.91.refs_2_, ...), custom_call_target="tpu_custom_call" | custom-call | flops 1073741824 | bytes 5505024 | tf_op jit(solution)/shard_map/pallas_call | solution.py:58
  124.8 1.3 convolution_convert_fusion.1.refs_1_
  126.6 1.3 convolution_convert_fusion.refs_2_
  127.9 2.0 shard_map.227
  129.8 6.3 %shard_map.228 = (bf16[1024,384]{1,0:T(8,128)(2,1)S(1)}, f32[1,384]{1,0:T(1,128)S(1)}) custom-call(s32[5]{0:T(128)S(1)} %copy-done.4, bf16[1024,384]{1,0:T(8,128)(2,1)S(1)} %get-tuple-element.94.refs_1_, bf16[256,1024]{1,0:T(8,128)(2,1)S(1)} %get-tuple-element.95.refs_2_, bf16[1024,128]{1,0:T(8,128)(2,1)S(1)} %get-tuple-element.96.refs_3_, ...), custom_call_target="tpu_custom_call" | custom-call | flops 1342177280 | bytes 1703936 | tf_op jit(solution)/shard_map/pallas_call | solution.py:58
  136.1 4.4 %shard_map.229 = (bf16[512,1024]{1,0:T(8,128)(2,1)S(1)}, f32[1,1024]{1,0:T(1,128)S(1)}, f32[1,1024]{1,0:T(1,128)S(1)}, bf16[512,1024]{1,0:T(8,128)(2,1)}) custom-call(s32[5]{0:T(128)S(1)} %copy-done.4, bf16[1024,512]{1,0:T(8,128)(2,1)S(1)} %get-tuple-element.93.refs_1_, bf16[1024,1024]{1,0:T(8,128)(2,1)S(1)} %get-tuple-element.90.refs_1_.refs_2_, ...), custom_call_target="tpu_custom_call" | custom-call | flops 1073741824 | bytes 6815744 | tf_op jit(solution)/shard_map/pallas_call | solution.py:58
  141.2 1.3 convolution_convert_fusion.2.refs_1_
  142.5 1.2 collective-permute-done.29.refs_3_
  143.7 1.4 shard_map.232
  145.1 7.2 %collective-permute-start.30 = (bf16[320,512]{1,0:T(8,128)(2,1)S(1)}, bf16[320,512]{1,0:T(8,128)(2,1)S(1)}, u32[]{:S(2)}, u32[]{:S(2)}) collective-permute-start(bf16[320,512]{1,0:T(8,128)(2,1)S(1)} %get-tuple-element.115), channel_id=1, source_target_pairs={{0,24},{8,0},{16,8},{24,16},{1,25},{9,1},{17,9},{25,17},{2,26},{10... | collective-permute-start | bytes 983048 | tf_op jit(solution)/shard_map/ppermute | solution.py:920
  153.0 7.5 %collective-permute-done.30.refs_2_ = bf16[320,512]{1,0:T(8,128)(2,1)S(1)} collective-permute-done((bf16[320,512]{1,0:T(8,128)(2,1)S(1)}, bf16[320,512]{1,0:T(8,128)(2,1)S(1)}, u32[]{:S(2)}, u32[]{:S(2)}) %collective-permute-start.30) | collective-permute-done | bytes 327712 | tf_op jit(solution)/shard_map/ppermute | solution.py:920
  160.5 3.4 %collective-permute-start.33 = (bf16[256,1024]{1,0:T(8,128)(2,1)}, bf16[256,1024]{1,0:T(8,128)(2,1)S(1)}, u32[]{:S(2)}, u32[]{:S(2)}) collective-permute-start(bf16[256,1024]{1,0:T(8,128)(2,1)} %get-tuple-element.125), channel_id=1, source_target_pairs={{0,24},{8,0},{16,8},{24,16},{1,25},{9,1},{17,9},{25,17},{2,26},{10... | collective-permute-start | bytes 1572872 | tf_op jit(solution)/shard_map/ppermute | solution.py:920
  163.8 5.2 %collective-permute-done.31.refs_3_ = bf16[320,512]{1,0:T(8,128)(2,1)S(1)} collective-permute-done((bf16[320,512]{1,0:T(8,128)(2,1)S(1)}, bf16[320,512]{1,0:T(8,128)(2,1)S(1)}, u32[]{:S(2)}, u32[]{:S(2)}) %collective-permute-start.31) | collective-permute-done | bytes 327712 | tf_op jit(solution)/shard_map/ppermute | solution.py:920
  170.0 2.7 %shard_map.233 = (f32[32,1024]{1,0:T(8,128)}, bf16[256,512]{1,0:T(8,128)(2,1)}) custom-call(s32[5]{0:T(128)S(1)} %copy-done.4, bf16[320,512]{1,0:T(8,128)(2,1)S(1)} %get-tuple-element.114.refs_1_, bf16[320,512]{1,0:T(8,128)(2,1)S(1)} %collective-permute-done.30.refs_2_, bf16[320,512]{1,0:T(8,128)(2,1)S(1)} %collective-permute-done.31.refs_3_, ...), custom_call_target="tpu_custom_call" | custom-call | bytes 1310720 | tf_op jit(solution)/shard_map/pallas_call | solution.py:58
  172.7 5.9 %all-to-all-start.1 = ((bf16[8,32,512]{2,1,0:T(8,128)(2,1)}), bf16[8,32,512]{2,1,0:T(8,128)(2,1)S(1)}, u32[]{:S(2)}, u32[]{:S(2)}) async-start(bf16[8,32,512]{2,1,0:T(8,128)(2,1)} %bitcast.12), calls=%async_computation.1 | async-start | bytes 524288 | tf_op jit(solution)/shard_map/all_to_all | solution.py:931
  178.9 14.8 %collective-permute-done.34.refs_3_ = bf16[256,1024]{1,0:T(8,128)(2,1)} collective-permute-done((bf16[256,1024]{1,0:T(8,128)(2,1)}, bf16[256,1024]{1,0:T(8,128)(2,1)}, u32[]{:S(2)}, u32[]{:S(2)}) %collective-permute-start.34) | collective-permute-done | bytes 524320 | tf_op jit(solution)/shard_map/ppermute | solution.py:920
  193.7 2.7 %shard_map.235 = bf16[256,1024]{1,0:T(8,128)(2,1)} custom-call(s32[5]{0:T(128)S(1)} %copy-done.4, bf16[256,1024]{1,0:T(8,128)(2,1)S(1)} %get-tuple-element.100.refs_8_.refs_1_, bf16[256,1024]{1,0:T(8,128)(2,1)S(1)} %collective-permute-done.33.refs_2_, bf16[256,1024]{1,0:T(8,128)(2,1)} %collective-permute-done.34.refs_3_, ...), custom_call_target="tpu_custom_call" | custom-call | bytes 2097152 | tf_op jit(solution)/shard_map/pallas_call | solution.py:58
  196.4 4.2 %all-to-all-start.2 = ((bf16[8,32,1024]{2,1,0:T(8,128)(2,1)}), bf16[8,32,1024]{2,1,0:T(8,128)(2,1)}, u32[]{:S(2)}, u32[]{:S(2)}) async-start(bf16[8,32,1024]{2,1,0:T(8,128)(2,1)} %bitcast.17), calls=%async_computation.2 | async-start | bytes 1048576 | tf_op jit(solution)/shard_map/all_to_all | solution.py:931
  200.6 1.9 shard_map.230
  202.5 3.8 %collective-permute-start.26 = (bf16[128,1024]{1,0:T(8,128)(2,1)S(1)}, bf16[128,1024]{1,0:T(8,128)(2,1)S(1)}, u32[]{:S(2)}, u32[]{:S(2)}) collective-permute-start(bf16[128,1024]{1,0:T(8,128)(2,1)S(1)} %get-tuple-element.107), channel_id=1, source_target_pairs={{0,6},{1,7},{2,0},{3,1},{4,2},{5,3},{6,4},{7,5},{8,14},{9,15},{10,... | collective-permute-start | bytes 786440 | tf_op jit(solution)/shard_map/ppermute | solution.py:920
  206.3 1.9 shard_map.225
  209.4 3.3 %collective-permute-start.28 = (bf16[128,1024]{1,0:T(8,128)(2,1)S(1)}, bf16[128,1024]{1,0:T(8,128)(2,1)S(1)}, u32[]{:S(2)}, u32[]{:S(2)}) collective-permute-start(bf16[128,1024]{1,0:T(8,128)(2,1)S(1)} %get-tuple-element.109), channel_id=1, source_target_pairs={{0,2},{1,3},{2,4},{3,5},{4,6},{5,7},{6,0},{7,1},{8,10},{9,11},{10,... | collective-permute-start | bytes 786440 | tf_op jit(solution)/shard_map/ppermute | solution.py:920
  212.7 5.0 %collective-permute-done.26.refs_5_ = bf16[128,1024]{1,0:T(8,128)(2,1)S(1)} collective-permute-done((bf16[128,1024]{1,0:T(8,128)(2,1)S(1)}, bf16[128,1024]{1,0:T(8,128)(2,1)S(1)}, u32[]{:S(2)}, u32[]{:S(2)}) %collective-permute-start.26) | collective-permute-done | bytes 262176 | tf_op jit(solution)/shard_map/ppermute | solution.py:920
  218.4 2.5 collective-permute-start.15
  220.9 1.9 shard_map.234
  222.7 27.5 %collective-permute-done.27.refs_6_ = bf16[128,1024]{1,0:T(8,128)(2,1)S(1)} collective-permute-done((bf16[128,1024]{1,0:T(8,128)(2,1)S(1)}, bf16[128,1024]{1,0:T(8,128)(2,1)S(1)}, u32[]{:S(2)}, u32[]{:S(2)}) %collective-permute-start.27) | collective-permute-done | bytes 262176 | tf_op jit(solution)/shard_map/ppermute | solution.py:920
  251.0 2.7 %shard_map.231 = f32[128,1024]{1,0:T(8,128)} custom-call(s32[5]{0:T(128)} %stack.17.refs_0_, bf16[128,1024]{1,0:T(8,128)(2,1)} %bitcast.41, bf16[128,1024]{1,0:T(8,128)(2,1)} %bitcast.33, f32[1,1024]{1,0:T(1,128)} %copy-done.5, f32[128,1024]{1,0:T(8,128)} %copy-done.3, bf16[128,1024]{1,0:T(8,128)(2,1)} %copy-done.18, bf16[128,1024]{1,0:T(8,128)(2,1)} %copy-done.19, ...), custom_call_target="tpu_custom_call" | custom-call | bytes 1867776 | tf_op jit(solution)/shard_map/pallas_call | solution.py:58
  253.8 2.0 collective-permute-done.16
  255.8 5.0 %collective-permute-done.15 = bf16[128,1024]{1,0:T(8,128)(2,1)S(1)} collective-permute-done((bf16[128,1024]{1,0:T(8,128)(2,1)S(1)}, bf16[128,1024]{1,0:T(8,128)(2,1)S(1)}, u32[]{:S(2)}, u32[]{:S(2)}) %collective-permute-start.15) | collective-permute-done | bytes 262176 | tf_op jit(solution)/shard_map/ppermute | solution.py:920
  261.7 2.1 shard_map.236
  (102 shorter events, 19.9 us)
Async XLA Ops:
  0.6 9.5 %copy-start.1 = (bf16[1,128,1024]{2,1,0:T(8,128)(2,1)S(1)}, bf16[1,128,1024]{2,1,0:T(8,128)(2,1)}, u32[]{:S(2)}) copy-start(bf16[1,128,1024]{2,1,0:T(8,128)(2,1)} %param.13) | copy-start | bytes 786436
  0.7 14.4 %copy-start = (bf16[1,128,1024]{2,1,0:T(8,128)(2,1)S(1)}, bf16[1,128,1024]{2,1,0:T(8,128)(2,1)}, u32[]{:S(2)}) copy-start(bf16[1,128,1024]{2,1,0:T(8,128)(2,1)} %param.14) | copy-start | bytes 786436
  0.7 47.4 %copy-start.21 = (bf16[32,1024]{1,0:T(8,128)(2,1)S(1)}, bf16[32,1024]{1,0:T(8,128)(2,1)}, u32[]{:S(2)}) copy-start(bf16[32,1024]{1,0:T(8,128)(2,1)} %param.20) | copy-start | bytes 196612
  3.6 83.9 %copy-start.4 = (s32[5]{0:T(128)S(1)}, s32[5]{0:T(128)}, u32[]{:S(2)}) copy-start(s32[5]{0:T(128)} %stack.17.refs_0_) | copy-start | bytes 64
  3.6 44.5 %all-to-all-start = ((bf16[8,32,1536]{2,1,0:T(8,128)(2,1)}), bf16[8,32,1536]{2,1,0:T(8,128)(2,1)S(1)}, u32[]{:S(2)}, u32[]{:S(2)}) async-start(bf16[8,32,1536]{2,1,0:T(8,128)(2,1)} %shard_map.220), calls=%async_computation | async-start | bytes 1572864 | tf_op jit(solution)/shard_map/all_to_all | solution.py:931
  10.1 22.0 %collective-permute-start.3 = (bf16[128,1024]{1,0:T(8,128)(2,1)S(1)}, bf16[128,1024]{1,0:T(8,128)(2,1)S(1)}, u32[]{:S(2)}, u32[]{:S(2)}) collective-permute-start(bf16[128,1024]{1,0:T(8,128)(2,1)S(1)} %bitcast.42), channel_id=1, source_target_pairs={{0,6},{1,7},{2,0},{3,1},{4,2},{5,3},{6,4},{7,5},{8,14},{9,15},{10,... | collective-permute-start | bytes 786440 | tf_op jit(solution)/shard_map/ppermute | solution.py:920
  13.9 45.8 %collective-permute-start.4 = (bf16[128,1024]{1,0:T(8,128)(2,1)S(1)}, bf16[128,1024]{1,0:T(8,128)(2,1)S(1)}, u32[]{:S(2)}, u32[]{:S(2)}) collective-permute-start(bf16[128,1024]{1,0:T(8,128)(2,1)S(1)} %bitcast.43), channel_id=1, source_target_pairs={{0,4},{1,5},{2,6},{3,7},{4,0},{5,1},{6,2},{7,3},{8,12},{9,13},{10,... | collective-permute-start | bytes 786440 | tf_op jit(solution)/shard_map/ppermute | solution.py:920
  14.0 45.8 %collective-permute-start.5 = (bf16[128,1024]{1,0:T(8,128)(2,1)S(1)}, bf16[128,1024]{1,0:T(8,128)(2,1)S(1)}, u32[]{:S(2)}, u32[]{:S(2)}) collective-permute-start(bf16[128,1024]{1,0:T(8,128)(2,1)S(1)} %bitcast.44), channel_id=1, source_target_pairs={{0,2},{1,3},{2,4},{3,5},{4,6},{5,7},{6,0},{7,1},{8,10},{9,11},{10,... | collective-permute-start | bytes 786440 | tf_op jit(solution)/shard_map/ppermute | solution.py:920
  15.1 45.5 %collective-permute-start.6 = (bf16[128,1024]{1,0:T(8,128)(2,1)S(1)}, bf16[128,1024]{1,0:T(8,128)(2,1)S(1)}, u32[]{:S(2)}, u32[]{:S(2)}) collective-permute-start(bf16[128,1024]{1,0:T(8,128)(2,1)S(1)} %bitcast.45), channel_id=1, source_target_pairs={{0,1},{1,0},{2,3},{3,2},{4,5},{5,4},{6,7},{7,6},{8,9},{9,8},{10,11... | collective-permute-start | bytes 786440 | tf_op jit(solution)/shard_map/ppermute | solution.py:920
  15.1 48.7 %collective-permute-start.18 = (bf16[128,1024]{1,0:T(8,128)(2,1)S(1)}, bf16[128,1024]{1,0:T(8,128)(2,1)S(1)}, u32[]{:S(2)}, u32[]{:S(2)}) collective-permute-start(bf16[128,1024]{1,0:T(8,128)(2,1)S(1)} %bitcast.34), channel_id=1, source_target_pairs={{0,6},{1,7},{2,0},{3,1},{4,2},{5,3},{6,4},{7,5},{8,14},{9,15},{10,... | collective-permute-start | bytes 786440 | tf_op jit(solution)/shard_map/ppermute | solution.py:920
  32.1 43.9 %collective-permute-start.19 = (bf16[128,1024]{1,0:T(8,128)(2,1)S(1)}, bf16[128,1024]{1,0:T(8,128)(2,1)S(1)}, u32[]{:S(2)}, u32[]{:S(2)}) collective-permute-start(bf16[128,1024]{1,0:T(8,128)(2,1)S(1)} %bitcast.35), channel_id=1, source_target_pairs={{0,4},{1,5},{2,6},{3,7},{4,0},{5,1},{6,2},{7,3},{8,12},{9,13},{10,... | collective-permute-start | bytes 786440 | tf_op jit(solution)/shard_map/ppermute | solution.py:920
  48.1 12.5 %copy-start.16 = (bf16[8,32,1536]{2,1,0:T(8,128)(2,1)}, bf16[8,32,1536]{2,1,0:T(8,128)(2,1)S(1)}, u32[]{:S(2)}) copy-start(bf16[8,32,1536]{2,1,0:T(8,128)(2,1)S(1)} %all-to-all-done) | copy-start | bytes 2359300
  59.8 18.9 %collective-permute-start.20 = (bf16[128,1024]{1,0:T(8,128)(2,1)S(1)}, bf16[128,1024]{1,0:T(8,128)(2,1)}, u32[]{:S(2)}, u32[]{:S(2)}) collective-permute-start(bf16[128,1024]{1,0:T(8,128)(2,1)S(1)} %bitcast.36), channel_id=1, source_target_pairs={{0,2},{1,3},{2,4},{3,5},{4,6},{5,7},{6,0},{7,1},{8,10},{9,11},{10,... | collective-permute-start | bytes 786440 | tf_op jit(solution)/shard_map/ppermute | solution.py:920
  59.8 20.3 %collective-permute-start.7 = (bf16[128,1024]{1,0:T(8,128)(2,1)S(1)}, bf16[128,1024]{1,0:T(8,128)(2,1)S(1)}, u32[]{:S(2)}, u32[]{:S(2)}) collective-permute-start(bf16[128,1024]{1,0:T(8,128)(2,1)S(1)} %collective-permute-done.3.refs_8_), channel_id=1, source_target_pairs={{0,1},{1,0},{2,3},{3,2},{4,5},{5,4},{6,7},{7,6},{8,9},{9,8},{10,11... | collective-permute-start | bytes 786440 | tf_op jit(solution)/shard_map/ppermute | solution.py:920
  61.3 21.1 %collective-permute-start = (bf16[320,512]{1,0:T(8,128)(2,1)S(1)}, bf16[320,512]{1,0:T(8,128)(2,1)S(1)}, u32[]{:S(2)}, u32[]{:S(2)}) collective-permute-start(bf16[320,512]{1,0:T(8,128)(2,1)S(1)} %pad_maximum_fusion.refs_1_.refs_15_), channel_id=1, source_target_pairs={{0,24},{8,0},{16,8},{24,16},{1,25},{9,1},{17,9},{25,17},{2,26},{10... | collective-permute-start | bytes 983048 | tf_op jit(solution)/shard_map/ppermute | solution.py:920
  63.8 18.6 %collective-permute-start.1 = (bf16[320,512]{1,0:T(8,128)(2,1)S(1)}, bf16[320,512]{1,0:T(8,128)(2,1)S(1)}, u32[]{:S(2)}, u32[]{:S(2)}) collective-permute-start(bf16[320,512]{1,0:T(8,128)(2,1)S(1)} %pad_maximum_fusion.refs_1_.refs_15_), channel_id=1, source_target_pairs={{0,16},{8,24},{16,0},{24,8},{1,17},{9,25},{17,1},{25,9},{2,18},{10... | collective-permute-start | bytes 983048 | tf_op jit(solution)/shard_map/ppermute | solution.py:920
  76.1 11.5 %collective-permute-start.2 = (bf16[320,512]{1,0:T(8,128)(2,1)S(1)}, bf16[320,512]{1,0:T(8,128)(2,1)S(1)}, u32[]{:S(2)}, u32[]{:S(2)}) collective-permute-start(bf16[320,512]{1,0:T(8,128)(2,1)S(1)} %pad_maximum_fusion.refs_1_.refs_15_), channel_id=1, source_target_pairs={{0,8},{8,16},{16,24},{24,0},{1,9},{9,17},{17,25},{25,1},{2,10},{10... | collective-permute-start | bytes 983048 | tf_op jit(solution)/shard_map/ppermute | solution.py:920
  78.6 20.3 %collective-permute-start.10 = (bf16[256,1024]{1,0:T(8,128)(2,1)S(1)}, bf16[256,1024]{1,0:T(8,128)(2,1)}, u32[]{:S(2)}, u32[]{:S(2)}) collective-permute-start(bf16[256,1024]{1,0:T(8,128)(2,1)S(1)} %bitcast.47), channel_id=1, source_target_pairs={{0,24},{8,0},{16,8},{24,16},{1,25},{9,1},{17,9},{25,17},{2,26},{10... | collective-permute-start | bytes 1572872 | tf_op jit(solution)/shard_map/ppermute | solution.py:920
  80.8 18.1 %collective-permute-start.11 = (bf16[256,1024]{1,0:T(8,128)(2,1)S(1)}, bf16[256,1024]{1,0:T(8,128)(2,1)}, u32[]{:S(2)}, u32[]{:S(2)}) collective-permute-start(bf16[256,1024]{1,0:T(8,128)(2,1)S(1)} %bitcast.48), channel_id=1, source_target_pairs={{0,16},{8,24},{16,0},{24,8},{1,17},{9,25},{17,1},{25,9},{2,18},{10... | collective-permute-start | bytes 1572872 | tf_op jit(solution)/shard_map/ppermute | solution.py:920
  82.4 7.1 %collective-permute-start.8 = (bf16[128,1024]{1,0:T(8,128)(2,1)}, bf16[128,1024]{1,0:T(8,128)(2,1)S(1)}, u32[]{:S(2)}, u32[]{:S(2)}) collective-permute-start(bf16[128,1024]{1,0:T(8,128)(2,1)} %copy-done.6), channel_id=1, source_target_pairs={{0,1},{1,0},{2,3},{3,2},{4,5},{5,4},{6,7},{7,6},{8,9},{9,8},{10,11... | collective-permute-start | bytes 786440 | tf_op jit(solution)/shard_map/ppermute | solution.py:920
  82.4 30.5 %collective-permute-start.12 = (bf16[256,1024]{1,0:T(8,128)(2,1)S(1)}, bf16[256,1024]{1,0:T(8,128)(2,1)}, u32[]{:S(2)}, u32[]{:S(2)}) collective-permute-start(bf16[256,1024]{1,0:T(8,128)(2,1)S(1)} %bitcast.49), channel_id=1, source_target_pairs={{0,8},{8,16},{16,24},{24,0},{1,9},{9,17},{17,25},{25,1},{2,10},{10... | collective-permute-start | bytes 1572872 | tf_op jit(solution)/shard_map/ppermute | solution.py:920
  87.6 4.0 %collective-permute-start.9 = (bf16[128,1024]{1,0:T(8,128)(2,1)}, bf16[128,1024]{1,0:T(8,128)(2,1)}, u32[]{:S(2)}, u32[]{:S(2)}) collective-permute-start(bf16[128,1024]{1,0:T(8,128)(2,1)} %copy-done.8), channel_id=1, source_target_pairs={{0,1},{1,0},{2,3},{3,2},{4,5},{5,4},{6,7},{7,6},{8,9},{9,8},{10,11... | collective-permute-start | bytes 786440 | tf_op jit(solution)/shard_map/ppermute | solution.py:920
  89.4 23.4 %copy-start.5 = (f32[1,1024]{1,0:T(1,128)}, f32[1,1024]{1,0:T(1,128)S(1)}, u32[]{:S(2)}) copy-start(f32[1,1024]{1,0:T(1,128)S(1)} %get-tuple-element.72.refs_1_.refs_3_) | copy-start | bytes 12292
  90.2 1.8 collective-permute-start.13
  91.6 29.0 %collective-permute-start.21 = (bf16[128,1024]{1,0:T(8,128)(2,1)S(1)}, bf16[128,1024]{1,0:T(8,128)(2,1)S(1)}, u32[]{:S(2)}, u32[]{:S(2)}) collective-permute-start(bf16[128,1024]{1,0:T(8,128)(2,1)S(1)} %bitcast.37), channel_id=1, source_target_pairs={{0,1},{1,0},{2,3},{3,2},{4,5},{5,4},{6,7},{7,6},{8,9},{9,8},{10,11... | collective-permute-start | bytes 786440 | tf_op jit(solution)/shard_map/ppermute | solution.py:920
  92.0 28.6 %collective-permute-start.22 = (bf16[128,1024]{1,0:T(8,128)(2,1)S(1)}, bf16[128,1024]{1,0:T(8,128)(2,1)S(1)}, u32[]{:S(2)}, u32[]{:S(2)}) collective-permute-start(bf16[128,1024]{1,0:T(8,128)(2,1)S(1)} %collective-permute-done.18.refs_5_), channel_id=1, source_target_pairs={{0,1},{1,0},{2,3},{3,2},{4,5},{5,4},{6,7},{7,6},{8,9},{9,8},{10,11... | collective-permute-start | bytes 786440 | tf_op jit(solution)/shard_map/ppermute | solution.py:920
  99.0 21.6 %collective-permute-start.23 = (bf16[128,1024]{1,0:T(8,128)(2,1)S(1)}, bf16[128,1024]{1,0:T(8,128)(2,1)S(1)}, u32[]{:S(2)}, u32[]{:S(2)}) collective-permute-start(bf16[128,1024]{1,0:T(8,128)(2,1)S(1)} %collective-permute-done.19.refs_6_), channel_id=1, source_target_pairs={{0,1},{1,0},{2,3},{3,2},{4,5},{5,4},{6,7},{7,6},{8,9},{9,8},{10,11... | collective-permute-start | bytes 786440 | tf_op jit(solution)/shard_map/ppermute | solution.py:920
  99.0 21.6 %collective-permute-start.24 = (bf16[128,1024]{1,0:T(8,128)(2,1)}, bf16[128,1024]{1,0:T(8,128)(2,1)S(1)}, u32[]{:S(2)}, u32[]{:S(2)}) collective-permute-start(bf16[128,1024]{1,0:T(8,128)(2,1)} %collective-permute-done.20.refs_7_), channel_id=1, source_target_pairs={{0,1},{1,0},{2,3},{3,2},{4,5},{5,4},{6,7},{7,6},{8,9},{9,8},{10,11... | collective-permute-start | bytes 786440 | tf_op jit(solution)/shard_map/ppermute | solution.py:920
  140.5 60.0 %collective-permute-start.25 = (bf16[512,1024]{1,0:T(8,128)(2,1)}, bf16[512,1024]{1,0:T(8,128)(2,1)}, u32[]{:S(2)}, u32[]{:S(2)}) collective-permute-start(bf16[512,1024]{1,0:T(8,128)(2,1)} %get-tuple-element.105), channel_id=1, source_target_pairs={{0,1},{1,0},{2,3},{3,2},{4,5},{5,4},{6,7},{7,6},{8,9},{9,8},{10,11... | collective-permute-start | bytes 3145736 | tf_op jit(solution)/shard_map/ppermute | solution.py:920
  140.6 3.0 %collective-permute-start.29 = (bf16[2,32,1024]{2,1,0:T(8,128)(2,1)S(1)}, bf16[2,32,1024]{2,1,0:T(8,128)(2,1)S(1)}, u32[]{:S(2)}, u32[]{:S(2)}) collective-permute-start(bf16[2,32,1024]{2,1,0:T(8,128)(2,1)S(1)} %dynamic-slice_bitcast_fusion), channel_id=1, source_target_pairs={{0,1},{1,0},{2,3},{3,2},{4,5},{5,4},{6,7},{7,6},{8,9},{9,8},{10,11... | collective-permute-start | bytes 393224 | tf_op jit(solution)/shard_map/ppermute | solution.py:920
  145.1 15.4 %collective-permute-start.30 = (bf16[320,512]{1,0:T(8,128)(2,1)S(1)}, bf16[320,512]{1,0:T(8,128)(2,1)S(1)}, u32[]{:S(2)}, u32[]{:S(2)}) collective-permute-start(bf16[320,512]{1,0:T(8,128)(2,1)S(1)} %get-tuple-element.115), channel_id=1, source_target_pairs={{0,24},{8,0},{16,8},{24,16},{1,25},{9,1},{17,9},{25,17},{2,26},{10... | collective-permute-start | bytes 983048 | tf_op jit(solution)/shard_map/ppermute | solution.py:920
  152.3 16.7 %collective-permute-start.31 = (bf16[320,512]{1,0:T(8,128)(2,1)S(1)}, bf16[320,512]{1,0:T(8,128)(2,1)S(1)}, u32[]{:S(2)}, u32[]{:S(2)}) collective-permute-start(bf16[320,512]{1,0:T(8,128)(2,1)S(1)} %get-tuple-element.116), channel_id=1, source_target_pairs={{0,16},{8,24},{16,0},{24,8},{1,17},{9,25},{17,1},{25,9},{2,18},{10... | collective-permute-start | bytes 983048 | tf_op jit(solution)/shard_map/ppermute | solution.py:920
  152.8 16.7 %collective-permute-start.32 = (bf16[320,512]{1,0:T(8,128)(2,1)S(1)}, bf16[320,512]{1,0:T(8,128)(2,1)S(1)}, u32[]{:S(2)}, u32[]{:S(2)}) collective-permute-start(bf16[320,512]{1,0:T(8,128)(2,1)S(1)} %get-tuple-element.117), channel_id=1, source_target_pairs={{0,8},{8,16},{16,24},{24,0},{1,9},{9,17},{17,25},{25,1},{2,10},{10... | collective-permute-start | bytes 983048 | tf_op jit(solution)/shard_map/ppermute | solution.py:920
  153.0 53.3 %collective-permute-start.14 = (bf16[512,1024]{1,0:T(8,128)(2,1)}, bf16[512,1024]{1,0:T(8,128)(2,1)}, u32[]{:S(2)}, u32[]{:S(2)}) collective-permute-start(bf16[512,1024]{1,0:T(8,128)(2,1)} %get-tuple-element.84), channel_id=1, source_target_pairs={{0,1},{1,0},{2,3},{3,2},{4,5},{5,4},{6,7},{7,6},{8,9},{9,8},{10,11... | collective-permute-start | bytes 3145736 | tf_op jit(solution)/shard_map/ppermute | solution.py:920
  160.5 18.4 %collective-permute-start.33 = (bf16[256,1024]{1,0:T(8,128)(2,1)}, bf16[256,1024]{1,0:T(8,128)(2,1)S(1)}, u32[]{:S(2)}, u32[]{:S(2)}) collective-permute-start(bf16[256,1024]{1,0:T(8,128)(2,1)} %get-tuple-element.125), channel_id=1, source_target_pairs={{0,24},{8,0},{16,8},{24,16},{1,25},{9,1},{17,9},{25,17},{2,26},{10... | collective-permute-start | bytes 1572872 | tf_op jit(solution)/shard_map/ppermute | solution.py:920
  169.0 24.6 %collective-permute-start.34 = (bf16[256,1024]{1,0:T(8,128)(2,1)}, bf16[256,1024]{1,0:T(8,128)(2,1)}, u32[]{:S(2)}, u32[]{:S(2)}) collective-permute-start(bf16[256,1024]{1,0:T(8,128)(2,1)} %get-tuple-element.126), channel_id=1, source_target_pairs={{0,16},{8,24},{16,0},{24,8},{1,17},{9,25},{17,1},{25,9},{2,18},{10... | collective-permute-start | bytes 1572872 | tf_op jit(solution)/shard_map/ppermute | solution.py:920
  169.6 24.1 %collective-permute-start.35 = (bf16[256,1024]{1,0:T(8,128)(2,1)}, bf16[256,1024]{1,0:T(8,128)(2,1)}, u32[]{:S(2)}, u32[]{:S(2)}) collective-permute-start(bf16[256,1024]{1,0:T(8,128)(2,1)} %get-tuple-element.127), channel_id=1, source_target_pairs={{0,8},{8,16},{16,24},{24,0},{1,9},{9,17},{17,25},{25,1},{2,10},{10... | collective-permute-start | bytes 1572872 | tf_op jit(solution)/shard_map/ppermute | solution.py:920
  172.7 23.7 %all-to-all-start.1 = ((bf16[8,32,512]{2,1,0:T(8,128)(2,1)}), bf16[8,32,512]{2,1,0:T(8,128)(2,1)S(1)}, u32[]{:S(2)}, u32[]{:S(2)}) async-start(bf16[8,32,512]{2,1,0:T(8,128)(2,1)} %bitcast.12), calls=%async_computation.1 | async-start | bytes 524288 | tf_op jit(solution)/shard_map/all_to_all | solution.py:931
  196.4 9.9 %copy-start.17 = (bf16[8,32,512]{2,1,0:T(8,128)(2,1)}, bf16[8,32,512]{2,1,0:T(8,128)(2,1)S(1)}, u32[]{:S(2)}) copy-start(bf16[8,32,512]{2,1,0:T(8,128)(2,1)S(1)} %all-to-all-done.1.refs_1_) | copy-start | bytes 786436
  196.4 65.3 %all-to-all-start.2 = ((bf16[8,32,1024]{2,1,0:T(8,128)(2,1)}), bf16[8,32,1024]{2,1,0:T(8,128)(2,1)}, u32[]{:S(2)}, u32[]{:S(2)}) async-start(bf16[8,32,1024]{2,1,0:T(8,128)(2,1)} %bitcast.17), calls=%async_computation.2 | async-start | bytes 1048576 | tf_op jit(solution)/shard_map/all_to_all | solution.py:931
  202.5 5.7 %copy-start.3 = (f32[128,1024]{1,0:T(8,128)}, f32[128,1024]{1,0:T(8,128)S(1)}, u32[]{:S(2)}) copy-start(f32[128,1024]{1,0:T(8,128)S(1)} %get-tuple-element.106.refs_4_) | copy-start | bytes 1572868
  202.5 15.1 %collective-permute-start.26 = (bf16[128,1024]{1,0:T(8,128)(2,1)S(1)}, bf16[128,1024]{1,0:T(8,128)(2,1)S(1)}, u32[]{:S(2)}, u32[]{:S(2)}) collective-permute-start(bf16[128,1024]{1,0:T(8,128)(2,1)S(1)} %get-tuple-element.107), channel_id=1, source_target_pairs={{0,6},{1,7},{2,0},{3,1},{4,2},{5,3},{6,4},{7,5},{8,14},{9,15},{10,... | collective-permute-start | bytes 786440 | tf_op jit(solution)/shard_map/ppermute | solution.py:920
  206.3 54.5 %copy-start.2 = (bf16[1,128,1024]{2,1,0:T(8,128)(2,1)S(1)}, bf16[1,128,1024]{2,1,0:T(8,128)(2,1)}, u32[]{:S(2)}) copy-start(bf16[1,128,1024]{2,1,0:T(8,128)(2,1)} %param.13) | copy-start | bytes 786436
  208.3 45.5 %collective-permute-start.17 = (bf16[128,1024]{1,0:T(8,128)(2,1)S(1)}, bf16[128,1024]{1,0:T(8,128)(2,1)S(1)}, u32[]{:S(2)}, u32[]{:S(2)}) collective-permute-start(bf16[128,1024]{1,0:T(8,128)(2,1)S(1)} %get-tuple-element.89), channel_id=1, source_target_pairs={{0,2},{1,3},{2,4},{3,5},{4,6},{5,7},{6,0},{7,1},{8,10},{9,11},{10,... | collective-permute-start | bytes 786440 | tf_op jit(solution)/shard_map/ppermute | solution.py:920
  208.3 41.9 %collective-permute-start.27 = (bf16[128,1024]{1,0:T(8,128)(2,1)S(1)}, bf16[128,1024]{1,0:T(8,128)(2,1)S(1)}, u32[]{:S(2)}, u32[]{:S(2)}) collective-permute-start(bf16[128,1024]{1,0:T(8,128)(2,1)S(1)} %get-tuple-element.108), channel_id=1, source_target_pairs={{0,4},{1,5},{2,6},{3,7},{4,0},{5,1},{6,2},{7,3},{8,12},{9,13},{10,... | collective-permute-start | bytes 786440 | tf_op jit(solution)/shard_map/ppermute | solution.py:920
  209.4 40.8 %collective-permute-start.28 = (bf16[128,1024]{1,0:T(8,128)(2,1)S(1)}, bf16[128,1024]{1,0:T(8,128)(2,1)S(1)}, u32[]{:S(2)}, u32[]{:S(2)}) collective-permute-start(bf16[128,1024]{1,0:T(8,128)(2,1)S(1)} %get-tuple-element.109), channel_id=1, source_target_pairs={{0,2},{1,3},{2,4},{3,5},{4,6},{5,7},{6,0},{7,1},{8,10},{9,11},{10,... | collective-permute-start | bytes 786440 | tf_op jit(solution)/shard_map/ppermute | solution.py:920
  212.7 43.0 %collective-permute-start.16 = (bf16[128,1024]{1,0:T(8,128)(2,1)S(1)}, bf16[128,1024]{1,0:T(8,128)(2,1)S(1)}, u32[]{:S(2)}, u32[]{:S(2)}) collective-permute-start(bf16[128,1024]{1,0:T(8,128)(2,1)S(1)} %get-tuple-element.88), channel_id=1, source_target_pairs={{0,4},{1,5},{2,6},{3,7},{4,0},{5,1},{6,2},{7,3},{8,12},{9,13},{10,... | collective-permute-start | bytes 786440 | tf_op jit(solution)/shard_map/ppermute | solution.py:920
  218.4 42.4 %collective-permute-start.15 = (bf16[128,1024]{1,0:T(8,128)(2,1)S(1)}, bf16[128,1024]{1,0:T(8,128)(2,1)S(1)}, u32[]{:S(2)}, u32[]{:S(2)}) collective-permute-start(bf16[128,1024]{1,0:T(8,128)(2,1)S(1)} %get-tuple-element.87), channel_id=1, source_target_pairs={{0,6},{1,7},{2,0},{3,1},{4,2},{5,3},{6,4},{7,5},{8,14},{9,15},{10,... | collective-permute-start | bytes 786440 | tf_op jit(solution)/shard_map/ppermute | solution.py:920
  (13 other events, 10.6 us)

commit v2 on v1

--- a/solution.py
+++ b/solution.py
@@ -92,7 +92,11 @@
     return pl.ds(pl.multiple_of(index * count, count), count)
 
 
-CORE, Z, S, SUB, LANE = range(5)
+CORE, Z, S, SUB, LANE, CTX = range(6)
+
+
+def at_c(at, k):
+    return at[CTX] ^ k
 
 
 def padded(total):
@@ -110,13 +114,14 @@
     total = 3 * heads * HEAD_DIM
     width = w_qkv.shape[1] // 3
 
-    def kernel(_, qkv_ref, fc1_ref, fc2_ref, *refs):
-        *small_refs, seg_ref, out_ref, small = refs
+    def kernel(at, qkv_ref, fc1_ref, fc2_ref, *refs):
+        small_refs, seg_ref = refs[:6], refs[6]
+        outs, (out_ref, small, sem) = refs[7 : 7 + count], refs[7 + count :]
         small[...] = jnp.zeros_like(small)
-        for at, ref in enumerate(small_refs):
-            small[at : at + 1, : ref.shape[0]] = ref[...].astype(f32).reshape(1, -1)
-        at = len(small_refs)
-        small[at : at + 1, : seg_ref.shape[1]] = seg_ref[...].astype(f32)
+        for row, ref in enumerate(small_refs):
+            small[row : row + 1, : ref.shape[0]] = ref[...].astype(f32).reshape(1, -1)
+        last = len(small_refs)
+        small[last : last + 1, : seg_ref.shape[1]] = seg_ref[...].astype(f32)
         rounded = small[...].astype(bf16)
         for to in range(count):
             for part in range(3):
@@ -128,15 +133,58 @@
             out_ref[to, :, base - SMALL : base] = rounded
             out_ref[to, :, base : base + cut] = fc1_ref[:, to * cut : (to + 1) * cut]
             out_ref[to, :, base + cut :] = fc2_ref[:, to * cut : (to + 1) * cut]
-
-    return call(
-        kernel,
-        [shape((count, share, padded(total) + SMALL + 2 * cut))],
-        [pltpu.VMEM((share, SMALL), f32)],
+        wait_all(start_all([(out_ref.at[at_c(at, k)], ref) for k, ref in enumerate(outs)], sem))
+
+    return call(
+        kernel,
+        [],
+        [
+            pltpu.VMEM((count, share, padded(total) + SMALL + 2 * cut), bf16),
+            pltpu.VMEM((share, SMALL), f32),
+            sems(count),
+        ],
         scalars,
         (w_qkv, w_fc1, w_fc2, *vectors, seg),
+        far_outs=[shape((share, padded(total) + SMALL + 2 * cut))] * count,
         room=0,
-    )[0]
+    )
+
+
+def collect_call(scalars, pieces, w_out, wide):
+    count = len(pieces)
+    share, lanes = pieces[0].shape
+    width = w_out.shape[1]
+    chunks = -(-width // wide)
+    rows = count * share
+
+    def kernel(at, *refs):
+        far_refs, w_out_ref, (joint_ref, fc_ref, sem) = refs[:count], refs[count], refs[count + 1 :]
+        pairs = []
+        for k, ref in enumerate(far_refs):
+            here = rows_at(at_c(at, k), share)
+            pairs += [
+                (ref.at[:, :wide], joint_ref.at[here, :]),
+                (ref.at[:, wide:], fc_ref.at[here, :]),
+            ]
+        for j in range(chunks):
+            upto = min(width - j * wide, wide)
+            begin = rows + j * share
+            pairs.append(
+                (
+                    w_out_ref.at[:, j * wide : j * wide + upto],
+                    joint_ref.at[begin : begin + share, :upto],
+                )
+            )
+        wait_all(start_all(pairs, sem))
+
+    return call(
+        kernel,
+        [shape((rows + chunks * share, wide)), shape((rows, lanes - wide))],
+        [sems(2 * count + chunks)],
+        scalars,
+        (),
+        far=(*pieces, w_out),
+    )
 
 
 def spread_out_call(scalars, pieces, rows, share, width, group, heads, lanes, cut):
@@ -633,27 +681,32 @@
     )
 
 
-def sum_fc_call(scalars, pieces):
+def sum_fc_call(scalars, share, pieces):
     rows, lanes = pieces[0].shape
     count = len(pieces)
     tiles = 2
+    ctxs = rows // share
     tile = rows // tiles
 
     def kernel(at, *refs):
-        far_refs, (out_ref, got, made, sem, sem_out) = refs[:count], refs[count:]
+        far_refs, outs, (got, made, sem, sem_out) = (
+            refs[:count],
+            refs[count : count + ctxs],
+            refs[count + ctxs :],
+        )
         starts = [slice(t * tile, (t + 1) * tile) for t in range(tiles)]
         copies = start_all(
             [(ref.at[here, :], got.at[k, here, :]) for here in starts for k, ref in enumerate(far_refs)],
             sem,
         )
-        outs = []
         for t, here in enumerate(starts):
             wait_all(copies[t * count : (t + 1) * count])
             made[here, :] = sum(got[k, here, :].astype(f32) for k in range(count)).astype(bf16)
-            out = pltpu.make_async_copy(made.at[here, :], out_ref.at[here, :], sem_out.at[t])
-            out.start()
-            outs.append(out)
-        wait_all(outs)
+        wait_all(
+            start_all(
+                [(made.at[rows_at(at_c(at, k), share), :], ref) for k, ref in enumerate(outs)], sem_out
+            )
+        )
 
     return call(
         kernel,
@@ -662,13 +715,13 @@
             pltpu.VMEM((count, rows, lanes), bf16),
             pltpu.VMEM((rows, lanes), bf16),
             sems(tiles * count),
-            sems(tiles),
+            sems(ctxs),
         ],
         scalars,
         (),
         far=pieces,
-        far_outs=[shape((rows, lanes))],
-    )[0]
+        far_outs=[shape((share, lanes))] * ctxs,
+    )
 
 
 def small_rows(share):
@@ -773,10 +826,8 @@
     ctxs = rows // share
 
     def kernel(at, *refs):
-        far_refs, (w_out_ref, out_ref, sums, got, made, sem, sem_out) = (
-            refs[: len(pieces)],
-            refs[len(pieces) :],
-        )
+        far_refs, w_out_ref, refs = refs[: len(pieces)], refs[len(pieces)], refs[len(pieces) + 1 :]
+        outs, (sums, got, made, sem, sem_out) = refs[:ctxs], refs[ctxs:]
         wait_all(start_all([(ref, got.at[k]) for k, ref in enumerate(far_refs)], sem))
         sums[...] = sum(got[k].astype(f32) for k in range(len(pieces)))
         for j in range(chunks):
@@ -793,7 +844,11 @@
                 sums[base : base + kinds, lanes - SMALL :] = high
                 sums[base + kinds : base + 2 * kinds, lanes - SMALL :] = value - high
         made[...] = sums[:rows, :].astype(bf16)
-        wait_all(start_all([(made, out_ref)], sem_out))
+        wait_all(
+            start_all(
+                [(made.at[rows_at(at_c(at, k), share), :], ref) for k, ref in enumerate(outs)], sem_out
+            )
+        )
 
     return call(
         kernel,
@@ -803,35 +858,51 @@
             pltpu.VMEM((len(pieces), *pieces[0].shape), bf16),
             pltpu.VMEM((rows, lanes), bf16),
             sems(len(pieces)),
-            sems(1),
+            sems(ctxs),
         ],
         scalars,
         (),
         far=pieces,
-        far_outs=[shape((rows, lanes))],
-    )
-
-
-def home_fc_call(scalars, got):
-    ctxs, share, double = got.shape
+        far_outs=[shape((share, lanes))] * ctxs,
+    )
+
+
+def home_fc_call(scalars, pieces, after):
+    ctxs = len(pieces)
+    share, double = pieces[0].shape
     cut = double // 2
 
-    def kernel(at, got_ref, one_ref, two_ref):
+    def kernel(at, *refs):
+        far_refs, (one_ref, two_ref, got, sem) = refs[:ctxs], refs[ctxs:]
+        wait_all(start_all([(ref, got.at[at_c(at, k)]) for k, ref in enumerate(far_refs)], sem))
         for ctx in range(ctxs):
             cols = slice(ctx * cut, (ctx + 1) * cut)
-            one_ref[:, cols] = got_ref[ctx, :, :cut].astype(f32)
-            two_ref[:, cols] = got_ref[ctx, :, cut:].astype(f32)
-
-    return call(kernel, [shape((share, ctxs * cut), f32)] * 2, [], scalars, (got,), room=0)
-
-
-def home_qkv_call(scalars, group, heads, lanes, width, got):
-    ctxs, share, wide = got.shape
+            one_ref[:, cols] = got[ctx, :, :cut].astype(f32)
+            two_ref[:, cols] = got[ctx, :, cut:].astype(f32)
+
+    return call(
+        kernel,
+        [shape((share, ctxs * cut), f32)] * 2,
+        [pltpu.VMEM((ctxs, share, double), bf16), sems(ctxs)],
+        scalars,
+        (),
+        far=pieces,
+        after=after,
+        room=4,
+    )
+
+
+def home_qkv_call(scalars, group, heads, lanes, width, pieces, after):
+    ctxs = len(pieces)
+    share, wide = pieces[0].shape
     kinds, parts = small_rows(share)
     sizes = (share, share, share, 3 * share, 4 * share, share)
     kind_of = (0, 1, 2, 3, 4, 2)
 
-    def kernel(at, got_ref, out_ref, *small_refs):
+    def kernel(at, *refs):
+        far_refs, out_ref, refs = refs[:ctxs], refs[ctxs], refs[ctxs + 1 :]
+        *small_refs, got_ref, sem = refs
+        wait_all(start_all([(ref, got_ref.at[at_c(at, k)]) for k, ref in enumerate(far_refs)], sem))
         for ctx in range(ctxs):
             for part in range(3):
                 for i in range(heads):
@@ -850,21 +921,27 @@
     return call(
         kernel,
         [shape((share, 3 * width), f32)] + [shape((1, n), f32) for n in sizes],
-        [],
-        scalars,
-        (got,),
-        room=0,
+        [pltpu.VMEM((ctxs, share, wide), bf16), sems(ctxs)],
+        scalars,
+        (),
+        far=pieces,
+        after=after,
+        room=4,
     )
 
 
 def finish_call(scalars, x, dy, gain, keep, parts):
+    count = len(parts)
+
     def kernel(at, x_ref, dy_ref, gain_ref, keep_ref, *refs):
-        *part_refs, out_ref = refs
-        dh = keep_ref[...] + sum(ref[...].astype(f32) for ref in part_refs)
+        far_refs, (out_ref, got, sem) = refs[:count], refs[count:]
+        copies = start_all([(ref, got.at[k]) for k, ref in enumerate(far_refs)], sem)
         here = x_ref[...].astype(f32)
         centred = here - jnp.mean(here, axis=1, keepdims=True)
         rstd = lax.rsqrt(jnp.mean(centred * centred, axis=1, keepdims=True) + norm_eps)
         xhat = centred * rstd
+        wait_all(copies)
+        dh = keep_ref[...] + sum(got[k].astype(f32) for k in range(count))
         scaled = dh * gain_ref[...]
         out_ref[...] = dy_ref[...].astype(f32) + rstd * (
             scaled
@@ -872,7 +949,15 @@
             - xhat * jnp.mean(scaled * xhat, axis=1, keepdims=True)
         )
 
-    return call(kernel, [shape(x.shape, f32)], [], scalars, (x, dy, gain, keep, *parts), room=0)[0]
+    return call(
+        kernel,
+        [shape(x.shape, f32)],
+        [pltpu.VMEM((count, *x.shape), bf16), sems(count)],
+        scalars,
+        (x, dy, gain, keep),
+        far=parts,
+        room=6,
+    )[0]
 
 
 def body(
@@ -903,7 +988,7 @@
     rows = ctxs * share
     zs = ctxs // 2
     sub, lane = c % group, c // group
-    scalars = jnp.stack([c % 2, c // 2, s, sub, lane]).astype(jnp.int32)
+    scalars = jnp.stack([c % 2, c // 2, s, sub, lane, c]).astype(jnp.int32)
     total = 3 * heads * HEAD_DIM
     x_here, dy_here = block_in[0], cotangent[0]
 
@@ -917,18 +1002,19 @@
         return [(i, i ^ k) for i in range(ctxs)]
 
     def along(axis, parts, pairs):
-        return [lax.ppermute(part, axis, pair) for part, pair in zip(parts, pairs)]
+        out = []
+        for part, pair in zip(parts, pairs):
+            out.append(lax.ppermute(part, axis, pair))
+        return out
 
     hops_z = [from_z(k) for k in range(1, zs)]
     hops_s = [from_s(k) for k in range(1, seqs)]
+    hops_c = [partner(k) for k in range(1, ctxs)]
     hops_g = [partner(k) for k in range(1, group)]
 
     def spread_ctx(local):
         mine = [local] + along("ctx", [local] * (zs - 1), hops_z)
         return mine + along("ctx", mine, [partner(1)] * zs)
-
-    def swap_ctx(blocks):
-        return lax.all_to_all(blocks, "ctx", split_axis=0, concat_axis=0, tiled=True)
 
     packed = pack_call(
         scalars,
@@ -941,16 +1027,10 @@
         (ln_gain, ln_bias, b_out, b_fc2, b_qkv, b_fc1),
         segments,
     )
-    got = swap_ctx(packed)
     wide = padded(total) + SMALL
-    chunks = -(-width // wide)
-    w_out_wide = jnp.pad(w_out, ((0, 0), (0, chunks * wide - width)))
-    joint = jnp.concatenate(
-        [got[:, :, :wide].reshape(rows, wide)]
-        + [w_out_wide[:, j * wide : (j + 1) * wide] for j in range(chunks)]
-    )
+    got = packed[:1] + along("ctx", packed[1:], hops_c)
+    joint, fc_here = collect_call(scalars, got, w_out, wide)
     joint = [joint] + along("seq", [joint] * (seqs - 1), hops_s)
-    fc_here = got[:, :, wide:].reshape(rows, 2 * cut)
     w_fc = [fc_here] + along("seq", [fc_here] * (seqs - 1), hops_s)
     x_all = spread_ctx(x_here)
     dy_all = spread_ctx(dy_here)
@@ -1009,13 +1089,15 @@
     dh_keep, *dh_sends = middle_call(scalars, piece, dh_mine, dh_theirs)
     dh_parts = along("ctx", dh_sends, hops_z)
 
-    fc_sum = sum_fc_call(scalars, fc_parts)
-    fc_home = swap_ctx(fc_sum.reshape(ctxs, share, 2 * cut))
-    out_wout, qkv_sum = sum_qkv_call(scalars, share, width, rows, qkv_parts)
-    qkv_home = swap_ctx(qkv_sum.reshape(ctxs, share, wide))
+    fc_home = sum_fc_call(scalars, share, fc_parts)
+    fc_home = fc_home[:1] + along("ctx", fc_home[1:], hops_c)
+    out_wout, *qkv_home = sum_qkv_call(scalars, share, width, rows, qkv_parts)
+    qkv_home = qkv_home[:1] + along("ctx", qkv_home[1:], hops_c)
     grad_in = finish_call(scalars, x_here, dy_here, gain, dh_keep, dh_parts)
-    out_wfc1, out_wfc2 = home_fc_call(scalars, fc_home)
-    out_wqkv, *small = home_qkv_call(scalars, group, heads, lanes, width, qkv_home)
+    out_wfc1, out_wfc2 = home_fc_call(scalars, fc_home, (grad_in,))
+    out_wqkv, *small = home_qkv_call(
+        scalars, group, heads, lanes, width, qkv_home, (out_wfc1,)
+    )
     small = [value.reshape(-1) for value in small]
     return (
         block_out[None],

time: 265 us -> 272 us (1.026)
  starting transfers between devices: 73.2 us -> 130 us
  waiting for transfers between devices: 118 us -> 70.9 us
  Pallas kernels: 55.5 us -> 49.9 us
    ppermute x36 -> x57, starting transfers between devices: 56.7 us -> 130 us  [along(): out.append(lax.ppermute(part, axis, pair))]
    ppermute x36 -> x57, waiting for transfers between devices: 118 us -> 70.9 us  [along(): out.append(lax.ppermute(part, axis, pair))]
    all_to_all x3 -> x0, starting transfers between devices: 16.5 us -> none  [swap_ctx(): lax.all_to_all(blocks, 'ctx', split_axis=0, concat_axis=0, tiled=True)]
    pallas_call x17 -> x18, Pallas kernels: 55.5 us -> 49.9 us  [call(): pl.pallas_call(wrapped, in_specs=[pl.BlockSpec(memory_space=pltpu.SMEM)]...]
    unnamed x44 -> x42, local copies, waits for them, and re-layouts: 9.11 us -> 12.8 us
  transfers between devices with their start and end apart: 39 -> 57, of which waited for: 15 -> 15; matrix products, arithmetic and copies ran while one was open for 1% -> 2% of each run, Pallas kernels for 13% -> 17%
where the time goes in v2:
time: 272 us; the launch traced here: 271 us
  starting transfers between devices  130 us (48%)
  waiting for transfers between devices  70.9 us (26%)
  Pallas kernels  49.9 us (18%)
  local copies, waits for them, and re-layouts  13.4 us (5%)
  matrix products  4.37 us (2%)
    ppermute x57, starting transfers between devices, along(): out.append(lax.ppermute(part, axis, pair))  130 us
    ppermute x57, waiting for transfers between devices, along(): out.append(lax.ppermute(part, axis, pair))  70.9 us
    pallas_call x18, Pallas kernels, call(): pl.pallas_call(wrapped, in_specs=[pl.BlockSpec(memory_space=pltpu.SMEM)]...  49.9 us
    unnamed x42, local copies, waits for them, and re-layouts  12.8 us
  transfers between devices with their start and end apart: 57, of which 15 were waited for; matrix products, arithmetic and copies ran while one was open for 2% of the time, Pallas kernels for 17%

profile of v2, /device:TPU:0, one launch (start us, length us, event | category | flops | bytes accessed | tf_op | source)
XLA Modules:
  0.0 270.9 jit_solution(2445772214438399834)
XLA Ops:
  1.3 2.3 shard_map.220
  4.1 2.6 collective-permute-start.1
  6.8 2.8 %collective-permute-start.3 = (bf16[32,1536]{1,0:T(8,128)(2,1)}, bf16[32,1536]{1,0:T(8,128)(2,1)S(1)}, u32[]{:S(2)}, u32[]{:S(2)}) collective-permute-start(bf16[32,1536]{1,0:T(8,128)(2,1)} %get-tuple-element.101), channel_id=1, source_target_pairs={{0,4},{1,5},{2,6},{3,7},{4,0},{5,1},{6,2},{7,3},{8,12},{9,13},{10,... | collective-permute-start | bytes 294920 | tf_op jit(solution)/shard_map/ppermute | solution.py:1007
  9.6 3.6 %collective-permute-start.10 = (bf16[128,1024]{1,0:T(8,128)(2,1)}, bf16[128,1024]{1,0:T(8,128)(2,1)S(1)}, u32[]{:S(2)}, u32[]{:S(2)}) collective-permute-start(bf16[128,1024]{1,0:T(8,128)(2,1)} %bitcast.39), channel_id=1, source_target_pairs={{0,6},{1,7},{2,0},{3,1},{4,2},{5,3},{6,4},{7,5},{8,14},{9,15},{10,... | collective-permute-start | bytes 786440 | tf_op jit(solution)/shard_map/ppermute | solution.py:1007
  13.2 1.5 collective-permute-start.5
  15.4 2.0 collective-permute-start.6
  17.9 2.0 collective-permute-done.4.refs_6_
  19.8 17.8 %collective-permute-start.12 = (bf16[128,1024]{1,0:T(8,128)(2,1)}, bf16[128,1024]{1,0:T(8,128)(2,1)}, u32[]{:S(2)}, u32[]{:S(2)}) collective-permute-start(bf16[128,1024]{1,0:T(8,128)(2,1)} %bitcast.41), channel_id=1, source_target_pairs={{0,2},{1,3},{2,4},{3,5},{4,6},{5,7},{6,0},{7,1},{8,10},{9,11},{10,... | collective-permute-start | bytes 786440 | tf_op jit(solution)/shard_map/ppermute | solution.py:1007
  42.4 2.5 collective-permute-start.7
  44.9 6.3 %collective-permute-done.11.refs_9_ = bf16[128,1024]{1,0:T(8,128)(2,1)S(1)} collective-permute-done((bf16[128,1024]{1,0:T(8,128)(2,1)}, bf16[128,1024]{1,0:T(8,128)(2,1)S(1)}, u32[]{:S(2)}, u32[]{:S(2)}) %collective-permute-start.11) | collective-permute-done | bytes 262176 | tf_op jit(solution)/shard_map/ppermute | solution.py:1007
  51.2 11.9 %collective-permute-start.27 = (bf16[128,1024]{1,0:T(8,128)(2,1)}, bf16[128,1024]{1,0:T(8,128)(2,1)S(1)}, u32[]{:S(2)}, u32[]{:S(2)}) collective-permute-start(bf16[128,1024]{1,0:T(8,128)(2,1)} %bitcast.32), channel_id=1, source_target_pairs={{0,2},{1,3},{2,4},{3,5},{4,6},{5,7},{6,0},{7,1},{8,10},{9,11},{10,... | collective-permute-start | bytes 786440 | tf_op jit(solution)/shard_map/ppermute | solution.py:1007
  63.9 1.5 collective-permute-start.8
  65.4 1.5 collective-permute-start.9
  66.9 6.5 %collective-permute-done.26.refs_6_ = bf16[128,1024]{1,0:T(8,128)(2,1)S(1)} collective-permute-done((bf16[128,1024]{1,0:T(8,128)(2,1)}, bf16[128,1024]{1,0:T(8,128)(2,1)S(1)}, u32[]{:S(2)}, u32[]{:S(2)}) %collective-permute-start.26) | collective-permute-done | bytes 262176 | tf_op jit(solution)/shard_map/ppermute | solution.py:1007
  73.4 2.4 collective-permute-start.17
  76.4 3.2 %collective-permute-done.8.refs_3_.refs_17_ = bf16[320,512]{1,0:T(8,128)(2,1)S(1)} collective-permute-done((bf16[320,512]{1,0:T(8,128)(2,1)S(1)}, bf16[320,512]{1,0:T(8,128)(2,1)S(1)}, u32[]{:S(2)}, u32[]{:S(2)}) %collective-permute-start.8) | collective-permute-done | bytes 327712 | tf_op jit(solution)/shard_map/ppermute | solution.py:1007
  81.4 1.9 shard_map.222
  88.3 13.4 %collective-permute-done.18.refs_6_ = bf16[256,1024]{1,0:T(8,128)(2,1)} collective-permute-done((bf16[256,1024]{1,0:T(8,128)(2,1)S(1)}, bf16[256,1024]{1,0:T(8,128)(2,1)}, u32[]{:S(2)}, u32[]{:S(2)}) %collective-permute-start.18) | collective-permute-done | bytes 524320 | tf_op jit(solution)/shard_map/ppermute | solution.py:1007
  106.1 8.7 %shard_map.224 = (bf16[1024,1024]{1,0:T(8,128)(2,1)S(1)}, bf16[1024,1024]{1,0:T(8,128)(2,1)S(1)}, bf16[1024,128]{1,0:T(8,128)(2,1)S(1)}, f32[2,1024]{1,0:T(2,128...) custom-call(s32[6]{0:T(128)S(1)} %copy-done.6, ...), custom_call_target="tpu_custom_call" | custom-call | flops 1610612736 | bytes 3584000 | tf_op jit(solution)/shard_map/pallas_call | solution.py:58
  114.8 7.0 %shard_map.225 = (bf16[1024,1024]{1,0:T(8,128)(2,1)S(1)}, bf16[1024,512]{1,0:T(8,128)(2,1)S(1)}, bf16[1024,512]{1,0:T(8,128)(2,1)S(1)}, bf16[512,1024]{1,0:T(8,1...) custom-call(s32[6]{0:T(128)S(1)} %copy-done.6, ...), custom_call_target="tpu_custom_call" | custom-call | flops 2147483648 | bytes 4734976 | tf_op jit(solution)/shard_map/pallas_call | solution.py:58
  122.4 3.2 %shard_map.227 = (bf16[1024,1024]{1,0:T(8,128)(2,1)S(1)}, bf16[1024,512]{1,0:T(8,128)(2,1)S(1)}, bf16[1024,128]{1,0:T(8,128)(2,1)S(1)}, f32[1,512]{1,0:T(1,128)S(1)}) custom-call(s32[6]{0:T(128)S(1)} %copy-done.6, bf16[1024,1024]{1,0:T(8,128)(2,1)S(1)} %get-tuple-element.125.refs_1_.refs_2_, bf16[128,1024]{1,0:T(8,128)(2,1)S(1)} %get-tuple-element.126.refs_2_, ...), custom_call_target="tpu_custom_call" | custom-call | flops 1073741824 | bytes 5505024 | tf_op jit(solution)/shard_map/pallas_call | solution.py:58
  129.3 6.2 %shard_map.229 = (bf16[1024,384]{1,0:T(8,128)(2,1)S(1)}, f32[1,384]{1,0:T(1,128)S(1)}) custom-call(s32[6]{0:T(128)S(1)} %copy-done.6, bf16[1024,384]{1,0:T(8,128)(2,1)S(1)} %get-tuple-element.129.refs_1_, bf16[256,1024]{1,0:T(8,128)(2,1)S(1)} %get-tuple-element.130.refs_2_, bf16[1024,128]{1,0:T(8,128)(2,1)S(1)} %get-tuple-element.131.refs_3_, ...), custom_call_target="tpu_custom_call" | custom-call | flops 1342177280 | bytes 1703936 | tf_op jit(solution)/shard_map/pallas_call | solution.py:58
  135.6 3.8 %shard_map.230 = (bf16[512,1024]{1,0:T(8,128)(2,1)S(1)}, f32[1,1024]{1,0:T(1,128)S(1)}, f32[1,1024]{1,0:T(1,128)S(1)}, bf16[512,1024]{1,0:T(8,128)(2,1)S(1)}) custom-call(s32[6]{0:T(128)S(1)} %copy-done.6, bf16[1024,512]{1,0:T(8,128)(2,1)S(1)} %get-tuple-element.128.refs_1_, bf16[1024,1024]{1,0:T(8,128)(2,1)S(1)} %get-tuple-element.125.refs_1_.refs_2_, ...), custom_call_target="tpu_custom_call" | custom-call | flops 1073741824 | bytes 6815744 | tf_op jit(solution)/shard_map/pallas_call | solution.py:58
  142.3 1.4 shard_map.233
  143.9 1.5 collective-permute-start.38
  145.4 1.9 collective-permute-start.47
  147.2 7.1 %collective-permute-done.37.refs_2_ = bf16[320,512]{1,0:T(8,128)(2,1)S(1)} collective-permute-done((bf16[320,512]{1,0:T(8,128)(2,1)S(1)}, bf16[320,512]{1,0:T(8,128)(2,1)S(1)}, u32[]{:S(2)}, u32[]{:S(2)}) %collective-permute-start.37) | collective-permute-done | bytes 327712 | tf_op jit(solution)/shard_map/ppermute | solution.py:1007
  154.3 1.6 collective-permute-start.48
  155.9 17.2 %collective-permute-start.49 = (bf16[256,1024]{1,0:T(8,128)(2,1)S(1)}, bf16[256,1024]{1,0:T(8,128)(2,1)S(1)}, u32[]{:S(2)}, u32[]{:S(2)}) collective-permute-start(bf16[256,1024]{1,0:T(8,128)(2,1)S(1)} %get-tuple-element.163), channel_id=1, source_target_pairs={{0,8},{8,16},{16,24},{24,0},{1,9},{9,17},{17,25},{25,1},{2,10},{10... | collective-permute-start | bytes 1572872 | tf_op jit(solution)/shard_map/ppermute | solution.py:1007
  174.2 17.9 %collective-permute-done.39.refs_4_ = bf16[320,512]{1,0:T(8,128)(2,1)S(1)} collective-permute-done((bf16[320,512]{1,0:T(8,128)(2,1)S(1)}, bf16[320,512]{1,0:T(8,128)(2,1)S(1)}, u32[]{:S(2)}, u32[]{:S(2)}) %collective-permute-start.39) | collective-permute-done | bytes 327712 | tf_op jit(solution)/shard_map/ppermute | solution.py:1007
  192.1 2.5 collective-permute-start.24
  194.6 2.4 shard_map.234
  197.4 1.8 shard_map.235
  199.4 1.7 collective-permute-start.51
  203.8 1.4 collective-permute-start.54
  205.2 2.3 collective-permute-done.52.refs_4_
  207.5 3.3 %collective-permute-start.56 = (bf16[32,1024]{1,0:T(8,128)(2,1)S(1)}, bf16[32,1024]{1,0:T(8,128)(2,1)S(1)}, u32[]{:S(2)}, u32[]{:S(2)}) collective-permute-start(bf16[32,1024]{1,0:T(8,128)(2,1)S(1)} %get-tuple-element.171), channel_id=1, source_target_pairs={{0,7},{1,6},{2,5},{3,4},{4,3},{5,2},{6,1},{7,0},{8,15},{9,14},{10,... | collective-permute-start | bytes 196616 | tf_op jit(solution)/shard_map/ppermute | solution.py:1007
  211.9 2.7 collective-permute-start.22
  214.5 1.7 collective-permute-start.33
  216.2 18.5 %collective-permute-start.34 = (bf16[128,1024]{1,0:T(8,128)(2,1)S(1)}, bf16[128,1024]{1,0:T(8,128)(2,1)S(1)}, u32[]{:S(2)}, u32[]{:S(2)}) collective-permute-start(bf16[128,1024]{1,0:T(8,128)(2,1)S(1)} %get-tuple-element.143), channel_id=1, source_target_pairs={{0,4},{1,5},{2,6},{3,7},{4,0},{5,1},{6,2},{7,3},{8,12},{9,13},{10,... | collective-permute-start | bytes 786440 | tf_op jit(solution)/shard_map/ppermute | solution.py:1007
  234.7 9.0 %collective-permute-start.42 = (bf16[32,512]{1,0:T(8,128)(2,1)S(1)}, bf16[32,512]{1,0:T(8,128)(2,1)S(1)}, u32[]{:S(2)}, u32[]{:S(2)}) collective-permute-start(bf16[32,512]{1,0:T(8,128)(2,1)S(1)} %get-tuple-element.156), channel_id=1, source_target_pairs={{0,3},{1,2},{2,1},{3,0},{4,7},{5,6},{6,5},{7,4},{8,11},{9,10},{10,... | collective-permute-start | bytes 98312 | tf_op jit(solution)/shard_map/ppermute | solution.py:1007
  243.7 3.4 %collective-permute-start.43 = (bf16[32,512]{1,0:T(8,128)(2,1)S(1)}, bf16[32,512]{1,0:T(8,128)(2,1)S(1)}, u32[]{:S(2)}, u32[]{:S(2)}) collective-permute-start(bf16[32,512]{1,0:T(8,128)(2,1)S(1)} %get-tuple-element.157), channel_id=1, source_target_pairs={{0,4},{1,5},{2,6},{3,7},{4,0},{5,1},{6,2},{7,3},{8,12},{9,13},{10,... | collective-permute-start | bytes 98312 | tf_op jit(solution)/shard_map/ppermute | solution.py:1007
  247.1 4.1 %collective-permute-start.44 = (bf16[32,512]{1,0:T(8,128)(2,1)S(1)}, bf16[32,512]{1,0:T(8,128)(2,1)S(1)}, u32[]{:S(2)}, u32[]{:S(2)}) collective-permute-start(bf16[32,512]{1,0:T(8,128)(2,1)S(1)} %get-tuple-element.158), channel_id=1, source_target_pairs={{0,5},{1,4},{2,7},{3,6},{4,1},{5,0},{6,3},{7,2},{8,13},{9,12},{10,... | collective-permute-start | bytes 98312 | tf_op jit(solution)/shard_map/ppermute | solution.py:1007
  251.2 7.5 %collective-permute-done.34.refs_6_ = bf16[128,1024]{1,0:T(8,128)(2,1)S(1)} collective-permute-done((bf16[128,1024]{1,0:T(8,128)(2,1)S(1)}, bf16[128,1024]{1,0:T(8,128)(2,1)S(1)}, u32[]{:S(2)}, u32[]{:S(2)}) %collective-permute-start.34) | collective-permute-done | bytes 262176 | tf_op jit(solution)/shard_map/ppermute | solution.py:1007
  258.7 2.9 %collective-permute-start.46 = (bf16[32,512]{1,0:T(8,128)(2,1)S(1)}, bf16[32,512]{1,0:T(8,128)(2,1)S(1)}, u32[]{:S(2)}, u32[]{:S(2)}) collective-permute-start(bf16[32,512]{1,0:T(8,128)(2,1)S(1)} %get-tuple-element.160), channel_id=1, source_target_pairs={{0,7},{1,6},{2,5},{3,4},{4,3},{5,2},{6,1},{7,0},{8,15},{9,14},{10,... | collective-permute-start | bytes 98312 | tf_op jit(solution)/shard_map/ppermute | solution.py:1007
  262.4 2.0 shard_map.232.refs_9_
  265.4 2.3 shard_map.236
  268.9 1.9 shard_map.237
  (133 shorter events, 35.3 us)
Async XLA Ops:
  3.6 6.0 %collective-permute-start = (bf16[32,1536]{1,0:T(8,128)(2,1)}, bf16[32,1536]{1,0:T(8,128)(2,1)S(1)}, u32[]{:S(2)}, u32[]{:S(2)}) collective-permute-start(bf16[32,1536]{1,0:T(8,128)(2,1)} %get-tuple-element.98), channel_id=1, source_target_pairs={{0,1},{1,0},{2,3},{3,2},{4,5},{5,4},{6,7},{7,6},{8,9},{9,8},{10,11... | collective-permute-start | bytes 294920 | tf_op jit(solution)/shard_map/ppermute | solution.py:1007
  4.1 9.1 %collective-permute-start.1 = (bf16[32,1536]{1,0:T(8,128)(2,1)}, bf16[32,1536]{1,0:T(8,128)(2,1)S(1)}, u32[]{:S(2)}, u32[]{:S(2)}) collective-permute-start(bf16[32,1536]{1,0:T(8,128)(2,1)} %get-tuple-element.99), channel_id=1, source_target_pairs={{0,2},{1,3},{2,0},{3,1},{4,6},{5,7},{6,4},{7,5},{8,10},{9,11},{10,... | collective-permute-start | bytes 294920 | tf_op jit(solution)/shard_map/ppermute | solution.py:1007
  6.8 8.7 %collective-permute-start.2 = (bf16[32,1536]{1,0:T(8,128)(2,1)}, bf16[32,1536]{1,0:T(8,128)(2,1)S(1)}, u32[]{:S(2)}, u32[]{:S(2)}) collective-permute-start(bf16[32,1536]{1,0:T(8,128)(2,1)} %get-tuple-element.100), channel_id=1, source_target_pairs={{0,3},{1,2},{2,1},{3,0},{4,7},{5,6},{6,5},{7,4},{8,11},{9,10},{10,... | collective-permute-start | bytes 294920 | tf_op jit(solution)/shard_map/ppermute | solution.py:1007
  6.8 10.6 %collective-permute-start.3 = (bf16[32,1536]{1,0:T(8,128)(2,1)}, bf16[32,1536]{1,0:T(8,128)(2,1)S(1)}, u32[]{:S(2)}, u32[]{:S(2)}) collective-permute-start(bf16[32,1536]{1,0:T(8,128)(2,1)} %get-tuple-element.101), channel_id=1, source_target_pairs={{0,4},{1,5},{2,6},{3,7},{4,0},{5,1},{6,2},{7,3},{8,12},{9,13},{10,... | collective-permute-start | bytes 294920 | tf_op jit(solution)/shard_map/ppermute | solution.py:1007
  9.6 10.3 %collective-permute-start.4 = (bf16[32,1536]{1,0:T(8,128)(2,1)}, bf16[32,1536]{1,0:T(8,128)(2,1)S(1)}, u32[]{:S(2)}, u32[]{:S(2)}) collective-permute-start(bf16[32,1536]{1,0:T(8,128)(2,1)} %get-tuple-element.102), channel_id=1, source_target_pairs={{0,5},{1,4},{2,7},{3,6},{4,1},{5,0},{6,3},{7,2},{8,13},{9,12},{10,... | collective-permute-start | bytes 294920 | tf_op jit(solution)/shard_map/ppermute | solution.py:1007
  9.6 32.8 %collective-permute-start.10 = (bf16[128,1024]{1,0:T(8,128)(2,1)}, bf16[128,1024]{1,0:T(8,128)(2,1)S(1)}, u32[]{:S(2)}, u32[]{:S(2)}) collective-permute-start(bf16[128,1024]{1,0:T(8,128)(2,1)} %bitcast.39), channel_id=1, source_target_pairs={{0,6},{1,7},{2,0},{3,1},{4,2},{5,3},{6,4},{7,5},{8,14},{9,15},{10,... | collective-permute-start | bytes 786440 | tf_op jit(solution)/shard_map/ppermute | solution.py:1007
  13.2 24.4 %collective-permute-start.5 = (bf16[32,1536]{1,0:T(8,128)(2,1)}, bf16[32,1536]{1,0:T(8,128)(2,1)S(1)}, u32[]{:S(2)}, u32[]{:S(2)}) collective-permute-start(bf16[32,1536]{1,0:T(8,128)(2,1)} %get-tuple-element.103), channel_id=1, source_target_pairs={{0,6},{1,7},{2,4},{3,5},{4,2},{5,3},{6,0},{7,1},{8,14},{9,15},{10,... | collective-permute-start | bytes 294920 | tf_op jit(solution)/shard_map/ppermute | solution.py:1007
  15.4 22.2 %collective-permute-start.6 = (bf16[32,1536]{1,0:T(8,128)(2,1)}, bf16[32,1536]{1,0:T(8,128)(2,1)S(1)}, u32[]{:S(2)}, u32[]{:S(2)}) collective-permute-start(bf16[32,1536]{1,0:T(8,128)(2,1)} %get-tuple-element.104), channel_id=1, source_target_pairs={{0,7},{1,6},{2,5},{3,4},{4,3},{5,2},{6,1},{7,0},{8,15},{9,14},{10,... | collective-permute-start | bytes 294920 | tf_op jit(solution)/shard_map/ppermute | solution.py:1007
  17.4 33.7 %collective-permute-start.11 = (bf16[128,1024]{1,0:T(8,128)(2,1)}, bf16[128,1024]{1,0:T(8,128)(2,1)S(1)}, u32[]{:S(2)}, u32[]{:S(2)}) collective-permute-start(bf16[128,1024]{1,0:T(8,128)(2,1)} %bitcast.40), channel_id=1, source_target_pairs={{0,4},{1,5},{2,6},{3,7},{4,0},{5,1},{6,2},{7,3},{8,12},{9,13},{10,... | collective-permute-start | bytes 786440 | tf_op jit(solution)/shard_map/ppermute | solution.py:1007
  19.8 31.4 %collective-permute-start.12 = (bf16[128,1024]{1,0:T(8,128)(2,1)}, bf16[128,1024]{1,0:T(8,128)(2,1)}, u32[]{:S(2)}, u32[]{:S(2)}) collective-permute-start(bf16[128,1024]{1,0:T(8,128)(2,1)} %bitcast.41), channel_id=1, source_target_pairs={{0,2},{1,3},{2,4},{3,5},{4,6},{5,7},{6,0},{7,1},{8,10},{9,11},{10,... | collective-permute-start | bytes 786440 | tf_op jit(solution)/shard_map/ppermute | solution.py:1007
  37.6 25.6 %collective-permute-start.13 = (bf16[128,1024]{1,0:T(8,128)(2,1)}, bf16[128,1024]{1,0:T(8,128)(2,1)S(1)}, u32[]{:S(2)}, u32[]{:S(2)}) collective-permute-start(bf16[128,1024]{1,0:T(8,128)(2,1)} %bitcast.42), channel_id=1, source_target_pairs={{0,1},{1,0},{2,3},{3,2},{4,5},{5,4},{6,7},{7,6},{8,9},{9,8},{10,11... | collective-permute-start | bytes 786440 | tf_op jit(solution)/shard_map/ppermute | solution.py:1007
  37.6 27.8 %collective-permute-start.25 = (bf16[128,1024]{1,0:T(8,128)(2,1)}, bf16[128,1024]{1,0:T(8,128)(2,1)S(1)}, u32[]{:S(2)}, u32[]{:S(2)}) collective-permute-start(bf16[128,1024]{1,0:T(8,128)(2,1)} %bitcast.30), channel_id=1, source_target_pairs={{0,6},{1,7},{2,0},{3,1},{4,2},{5,3},{6,4},{7,5},{8,14},{9,15},{10,... | collective-permute-start | bytes 786440 | tf_op jit(solution)/shard_map/ppermute | solution.py:1007
  42.4 33.5 %collective-permute-start.7 = (bf16[320,512]{1,0:T(8,128)(2,1)S(1)}, bf16[320,512]{1,0:T(8,128)(2,1)S(1)}, u32[]{:S(2)}, u32[]{:S(2)}) collective-permute-start(bf16[320,512]{1,0:T(8,128)(2,1)S(1)} %get-tuple-element.105.refs_1_.refs_15_), channel_id=1, source_target_pairs={{0,24},{8,0},{16,8},{24,16},{1,25},{9,1},{17,9},{25,17},{2,26},{10... | collective-permute-start | bytes 983048 | tf_op jit(solution)/shard_map/ppermute | solution.py:1007
  51.2 22.2 %collective-permute-start.26 = (bf16[128,1024]{1,0:T(8,128)(2,1)}, bf16[128,1024]{1,0:T(8,128)(2,1)S(1)}, u32[]{:S(2)}, u32[]{:S(2)}) collective-permute-start(bf16[128,1024]{1,0:T(8,128)(2,1)} %bitcast.31), channel_id=1, source_target_pairs={{0,4},{1,5},{2,6},{3,7},{4,0},{5,1},{6,2},{7,3},{8,12},{9,13},{10,... | collective-permute-start | bytes 786440 | tf_op jit(solution)/shard_map/ppermute | solution.py:1007
  51.2 22.2 %collective-permute-start.27 = (bf16[128,1024]{1,0:T(8,128)(2,1)}, bf16[128,1024]{1,0:T(8,128)(2,1)S(1)}, u32[]{:S(2)}, u32[]{:S(2)}) collective-permute-start(bf16[128,1024]{1,0:T(8,128)(2,1)} %bitcast.32), channel_id=1, source_target_pairs={{0,2},{1,3},{2,4},{3,5},{4,6},{5,7},{6,0},{7,1},{8,10},{9,11},{10,... | collective-permute-start | bytes 786440 | tf_op jit(solution)/shard_map/ppermute | solution.py:1007
  63.9 15.7 %collective-permute-start.8 = (bf16[320,512]{1,0:T(8,128)(2,1)S(1)}, bf16[320,512]{1,0:T(8,128)(2,1)S(1)}, u32[]{:S(2)}, u32[]{:S(2)}) collective-permute-start(bf16[320,512]{1,0:T(8,128)(2,1)S(1)} %get-tuple-element.105.refs_1_.refs_15_), channel_id=1, source_target_pairs={{0,16},{8,24},{16,0},{24,8},{1,17},{9,25},{17,1},{25,9},{2,18},{10... | collective-permute-start | bytes 983048 | tf_op jit(solution)/shard_map/ppermute | solution.py:1007
  65.4 14.2 %collective-permute-start.9 = (bf16[320,512]{1,0:T(8,128)(2,1)S(1)}, bf16[320,512]{1,0:T(8,128)(2,1)S(1)}, u32[]{:S(2)}, u32[]{:S(2)}) collective-permute-start(bf16[320,512]{1,0:T(8,128)(2,1)S(1)} %get-tuple-element.105.refs_1_.refs_15_), channel_id=1, source_target_pairs={{0,8},{8,16},{16,24},{24,0},{1,9},{9,17},{17,25},{25,1},{2,10},{10... | collective-permute-start | bytes 983048 | tf_op jit(solution)/shard_map/ppermute | solution.py:1007
  73.4 6.1 %collective-permute-start.14 = (bf16[128,1024]{1,0:T(8,128)(2,1)S(1)}, bf16[128,1024]{1,0:T(8,128)(2,1)S(1)}, u32[]{:S(2)}, u32[]{:S(2)}) collective-permute-start(bf16[128,1024]{1,0:T(8,128)(2,1)S(1)} %collective-permute-done.10.refs_8_), channel_id=1, source_target_pairs={{0,1},{1,0},{2,3},{3,2},{4,5},{5,4},{6,7},{7,6},{8,9},{9,8},{10,11... | collective-permute-start | bytes 786440 | tf_op jit(solution)/shard_map/ppermute | solution.py:1007
  73.4 14.9 %collective-permute-start.17 = (bf16[256,1024]{1,0:T(8,128)(2,1)S(1)}, bf16[256,1024]{1,0:T(8,128)(2,1)}, u32[]{:S(2)}, u32[]{:S(2)}) collective-permute-start(bf16[256,1024]{1,0:T(8,128)(2,1)S(1)} %get-tuple-element.115.refs_4_), channel_id=1, source_target_pairs={{0,24},{8,0},{16,8},{24,16},{1,25},{9,1},{17,9},{25,17},{2,26},{10... | collective-permute-start | bytes 1572872 | tf_op jit(solution)/shard_map/ppermute | solution.py:1007
  75.9 25.8 %collective-permute-start.18 = (bf16[256,1024]{1,0:T(8,128)(2,1)S(1)}, bf16[256,1024]{1,0:T(8,128)(2,1)}, u32[]{:S(2)}, u32[]{:S(2)}) collective-permute-start(bf16[256,1024]{1,0:T(8,128)(2,1)S(1)} %get-tuple-element.115.refs_4_), channel_id=1, source_target_pairs={{0,16},{8,24},{16,0},{24,8},{1,17},{9,25},{17,1},{25,9},{2,18},{10... | collective-permute-start | bytes 1572872 | tf_op jit(solution)/shard_map/ppermute | solution.py:1007
  79.5 35.3 %collective-permute-start.19 = (bf16[256,1024]{1,0:T(8,128)(2,1)S(1)}, bf16[256,1024]{1,0:T(8,128)(2,1)}, u32[]{:S(2)}, u32[]{:S(2)}) collective-permute-start(bf16[256,1024]{1,0:T(8,128)(2,1)S(1)} %get-tuple-element.115.refs_4_), channel_id=1, source_target_pairs={{0,8},{8,16},{16,24},{24,0},{1,9},{9,17},{17,25},{25,1},{2,10},{10... | collective-permute-start | bytes 1572872 | tf_op jit(solution)/shard_map/ppermute | solution.py:1007
  86.0 36.4 %collective-permute-start.28 = (bf16[128,1024]{1,0:T(8,128)(2,1)S(1)}, bf16[128,1024]{1,0:T(8,128)(2,1)S(1)}, u32[]{:S(2)}, u32[]{:S(2)}) collective-permute-start(bf16[128,1024]{1,0:T(8,128)(2,1)S(1)} %bitcast.33), channel_id=1, source_target_pairs={{0,1},{1,0},{2,3},{3,2},{4,5},{5,4},{6,7},{7,6},{8,9},{9,8},{10,11... | collective-permute-start | bytes 786440 | tf_op jit(solution)/shard_map/ppermute | solution.py:1007
  86.8 35.6 %collective-permute-start.29 = (bf16[128,1024]{1,0:T(8,128)(2,1)S(1)}, bf16[128,1024]{1,0:T(8,128)(2,1)S(1)}, u32[]{:S(2)}, u32[]{:S(2)}) collective-permute-start(bf16[128,1024]{1,0:T(8,128)(2,1)S(1)} %collective-permute-done.25.refs_5_), channel_id=1, source_target_pairs={{0,1},{1,0},{2,3},{3,2},{4,5},{5,4},{6,7},{7,6},{8,9},{9,8},{10,11... | collective-permute-start | bytes 786440 | tf_op jit(solution)/shard_map/ppermute | solution.py:1007
  88.3 34.1 %collective-permute-start.30 = (bf16[128,1024]{1,0:T(8,128)(2,1)S(1)}, bf16[128,1024]{1,0:T(8,128)(2,1)S(1)}, u32[]{:S(2)}, u32[]{:S(2)}) collective-permute-start(bf16[128,1024]{1,0:T(8,128)(2,1)S(1)} %collective-permute-done.26.refs_6_), channel_id=1, source_target_pairs={{0,1},{1,0},{2,3},{3,2},{4,5},{5,4},{6,7},{7,6},{8,9},{9,8},{10,11... | collective-permute-start | bytes 786440 | tf_op jit(solution)/shard_map/ppermute | solution.py:1007
  101.7 20.8 %collective-permute-start.31 = (bf16[128,1024]{1,0:T(8,128)(2,1)S(1)}, bf16[128,1024]{1,0:T(8,128)(2,1)S(1)}, u32[]{:S(2)}, u32[]{:S(2)}) collective-permute-start(bf16[128,1024]{1,0:T(8,128)(2,1)S(1)} %collective-permute-done.27.refs_7_), channel_id=1, source_target_pairs={{0,1},{1,0},{2,3},{3,2},{4,5},{5,4},{6,7},{7,6},{8,9},{9,8},{10,11... | collective-permute-start | bytes 786440 | tf_op jit(solution)/shard_map/ppermute | solution.py:1007
  121.8 51.3 %collective-permute-start.21 = (bf16[512,1024]{1,0:T(8,128)(2,1)S(1)}, bf16[512,1024]{1,0:T(8,128)(2,1)S(1)}, u32[]{:S(2)}, u32[]{:S(2)}) collective-permute-start(bf16[512,1024]{1,0:T(8,128)(2,1)S(1)} %get-tuple-element.119), channel_id=1, source_target_pairs={{0,1},{1,0},{2,3},{3,2},{4,5},{5,4},{6,7},{7,6},{8,9},{9,8},{10,11... | collective-permute-start | bytes 3145736 | tf_op jit(solution)/shard_map/ppermute | solution.py:1007
  139.4 68.1 %collective-permute-start.32 = (bf16[512,1024]{1,0:T(8,128)(2,1)S(1)}, bf16[512,1024]{1,0:T(8,128)(2,1)S(1)}, u32[]{:S(2)}, u32[]{:S(2)}) collective-permute-start(bf16[512,1024]{1,0:T(8,128)(2,1)S(1)} %get-tuple-element.140), channel_id=1, source_target_pairs={{0,1},{1,0},{2,3},{3,2},{4,5},{5,4},{6,7},{7,6},{8,9},{9,8},{10,11... | collective-permute-start | bytes 3145736 | tf_op jit(solution)/shard_map/ppermute | solution.py:1007
  143.7 10.6 %collective-permute-start.37 = (bf16[320,512]{1,0:T(8,128)(2,1)S(1)}, bf16[320,512]{1,0:T(8,128)(2,1)S(1)}, u32[]{:S(2)}, u32[]{:S(2)}) collective-permute-start(bf16[320,512]{1,0:T(8,128)(2,1)S(1)} %get-tuple-element.150), channel_id=1, source_target_pairs={{0,24},{8,0},{16,8},{24,16},{1,25},{9,1},{17,9},{25,17},{2,26},{10... | collective-permute-start | bytes 983048 | tf_op jit(solution)/shard_map/ppermute | solution.py:1007
  143.9 12.0 %collective-permute-start.38 = (bf16[320,512]{1,0:T(8,128)(2,1)S(1)}, bf16[320,512]{1,0:T(8,128)(2,1)S(1)}, u32[]{:S(2)}, u32[]{:S(2)}) collective-permute-start(bf16[320,512]{1,0:T(8,128)(2,1)S(1)} %get-tuple-element.151), channel_id=1, source_target_pairs={{0,16},{8,24},{16,0},{24,8},{1,17},{9,25},{17,1},{25,9},{2,18},{10... | collective-permute-start | bytes 983048 | tf_op jit(solution)/shard_map/ppermute | solution.py:1007
  145.4 51.6 %collective-permute-start.47 = (bf16[256,1024]{1,0:T(8,128)(2,1)S(1)}, bf16[256,1024]{1,0:T(8,128)(2,1)S(1)}, u32[]{:S(2)}, u32[]{:S(2)}) collective-permute-start(bf16[256,1024]{1,0:T(8,128)(2,1)S(1)} %get-tuple-element.161), channel_id=1, source_target_pairs={{0,24},{8,0},{16,8},{24,16},{1,25},{9,1},{17,9},{25,17},{2,26},{10... | collective-permute-start | bytes 1572872 | tf_op jit(solution)/shard_map/ppermute | solution.py:1007
  154.3 42.7 %collective-permute-start.48 = (bf16[256,1024]{1,0:T(8,128)(2,1)S(1)}, bf16[256,1024]{1,0:T(8,128)(2,1)S(1)}, u32[]{:S(2)}, u32[]{:S(2)}) collective-permute-start(bf16[256,1024]{1,0:T(8,128)(2,1)S(1)} %get-tuple-element.162), channel_id=1, source_target_pairs={{0,16},{8,24},{16,0},{24,8},{1,17},{9,25},{17,1},{25,9},{2,18},{10... | collective-permute-start | bytes 1572872 | tf_op jit(solution)/shard_map/ppermute | solution.py:1007
  155.9 41.5 %collective-permute-start.49 = (bf16[256,1024]{1,0:T(8,128)(2,1)S(1)}, bf16[256,1024]{1,0:T(8,128)(2,1)S(1)}, u32[]{:S(2)}, u32[]{:S(2)}) collective-permute-start(bf16[256,1024]{1,0:T(8,128)(2,1)S(1)} %get-tuple-element.163), channel_id=1, source_target_pairs={{0,8},{8,16},{16,24},{24,0},{1,9},{9,17},{17,25},{25,1},{2,10},{10... | collective-permute-start | bytes 1572872 | tf_op jit(solution)/shard_map/ppermute | solution.py:1007
  173.1 18.9 %collective-permute-start.39 = (bf16[320,512]{1,0:T(8,128)(2,1)S(1)}, bf16[320,512]{1,0:T(8,128)(2,1)S(1)}, u32[]{:S(2)}, u32[]{:S(2)}) collective-permute-start(bf16[320,512]{1,0:T(8,128)(2,1)S(1)} %get-tuple-element.152), channel_id=1, source_target_pairs={{0,8},{8,16},{16,24},{24,0},{1,9},{9,17},{17,25},{25,1},{2,10},{10... | collective-permute-start | bytes 983048 | tf_op jit(solution)/shard_map/ppermute | solution.py:1007
  192.1 42.6 %collective-permute-start.24 = (bf16[128,1024]{1,0:T(8,128)(2,1)S(1)}, bf16[128,1024]{1,0:T(8,128)(2,1)S(1)}, u32[]{:S(2)}, u32[]{:S(2)}) collective-permute-start(bf16[128,1024]{1,0:T(8,128)(2,1)S(1)} %get-tuple-element.124), channel_id=1, source_target_pairs={{0,2},{1,3},{2,4},{3,5},{4,6},{5,7},{6,0},{7,1},{8,10},{9,11},{10,... | collective-permute-start | bytes 786440 | tf_op jit(solution)/shard_map/ppermute | solution.py:1007
  202.2 9.6 %collective-permute-start.53 = (bf16[32,1024]{1,0:T(8,128)(2,1)S(1)}, bf16[32,1024]{1,0:T(8,128)(2,1)S(1)}, u32[]{:S(2)}, u32[]{:S(2)}) collective-permute-start(bf16[32,1024]{1,0:T(8,128)(2,1)S(1)} %get-tuple-element.168), channel_id=1, source_target_pairs={{0,4},{1,5},{2,6},{3,7},{4,0},{5,1},{6,2},{7,3},{8,12},{9,13},{10,... | collective-permute-start | bytes 196616 | tf_op jit(solution)/shard_map/ppermute | solution.py:1007
  203.8 8.0 %collective-permute-start.54 = (bf16[32,1024]{1,0:T(8,128)(2,1)S(1)}, bf16[32,1024]{1,0:T(8,128)(2,1)S(1)}, u32[]{:S(2)}, u32[]{:S(2)}) collective-permute-start(bf16[32,1024]{1,0:T(8,128)(2,1)S(1)} %get-tuple-element.169), channel_id=1, source_target_pairs={{0,5},{1,4},{2,7},{3,6},{4,1},{5,0},{6,3},{7,2},{8,13},{9,12},{10,... | collective-permute-start | bytes 196616 | tf_op jit(solution)/shard_map/ppermute | solution.py:1007
  207.5 7.1 %collective-permute-start.55 = (bf16[32,1024]{1,0:T(8,128)(2,1)S(1)}, bf16[32,1024]{1,0:T(8,128)(2,1)S(1)}, u32[]{:S(2)}, u32[]{:S(2)}) collective-permute-start(bf16[32,1024]{1,0:T(8,128)(2,1)S(1)} %get-tuple-element.170), channel_id=1, source_target_pairs={{0,6},{1,7},{2,4},{3,5},{4,2},{5,3},{6,0},{7,1},{8,14},{9,15},{10,... | collective-permute-start | bytes 196616 | tf_op jit(solution)/shard_map/ppermute | solution.py:1007
  207.5 8.8 %collective-permute-start.56 = (bf16[32,1024]{1,0:T(8,128)(2,1)S(1)}, bf16[32,1024]{1,0:T(8,128)(2,1)S(1)}, u32[]{:S(2)}, u32[]{:S(2)}) collective-permute-start(bf16[32,1024]{1,0:T(8,128)(2,1)S(1)} %get-tuple-element.171), channel_id=1, source_target_pairs={{0,7},{1,6},{2,5},{3,4},{4,3},{5,2},{6,1},{7,0},{8,15},{9,14},{10,... | collective-permute-start | bytes 196616 | tf_op jit(solution)/shard_map/ppermute | solution.py:1007
  211.8 22.9 %collective-permute-start.23 = (bf16[128,1024]{1,0:T(8,128)(2,1)S(1)}, bf16[128,1024]{1,0:T(8,128)(2,1)S(1)}, u32[]{:S(2)}, u32[]{:S(2)}) collective-permute-start(bf16[128,1024]{1,0:T(8,128)(2,1)S(1)} %get-tuple-element.123), channel_id=1, source_target_pairs={{0,4},{1,5},{2,6},{3,7},{4,0},{5,1},{6,2},{7,3},{8,12},{9,13},{10,... | collective-permute-start | bytes 786440 | tf_op jit(solution)/shard_map/ppermute | solution.py:1007
  211.9 31.9 %collective-permute-start.22 = (bf16[128,1024]{1,0:T(8,128)(2,1)S(1)}, bf16[128,1024]{1,0:T(8,128)(2,1)S(1)}, u32[]{:S(2)}, u32[]{:S(2)}) collective-permute-start(bf16[128,1024]{1,0:T(8,128)(2,1)S(1)} %get-tuple-element.122), channel_id=1, source_target_pairs={{0,6},{1,7},{2,0},{3,1},{4,2},{5,3},{6,4},{7,5},{8,14},{9,15},{10,... | collective-permute-start | bytes 786440 | tf_op jit(solution)/shard_map/ppermute | solution.py:1007
  214.5 32.6 %collective-permute-start.33 = (bf16[128,1024]{1,0:T(8,128)(2,1)S(1)}, bf16[128,1024]{1,0:T(8,128)(2,1)S(1)}, u32[]{:S(2)}, u32[]{:S(2)}) collective-permute-start(bf16[128,1024]{1,0:T(8,128)(2,1)S(1)} %get-tuple-element.142), channel_id=1, source_target_pairs={{0,6},{1,7},{2,0},{3,1},{4,2},{5,3},{6,4},{7,5},{8,14},{9,15},{10,... | collective-permute-start | bytes 786440 | tf_op jit(solution)/shard_map/ppermute | solution.py:1007
  216.2 42.4 %collective-permute-start.34 = (bf16[128,1024]{1,0:T(8,128)(2,1)S(1)}, bf16[128,1024]{1,0:T(8,128)(2,1)S(1)}, u32[]{:S(2)}, u32[]{:S(2)}) collective-permute-start(bf16[128,1024]{1,0:T(8,128)(2,1)S(1)} %get-tuple-element.143), channel_id=1, source_target_pairs={{0,4},{1,5},{2,6},{3,7},{4,0},{5,1},{6,2},{7,3},{8,12},{9,13},{10,... | collective-permute-start | bytes 786440 | tf_op jit(solution)/shard_map/ppermute | solution.py:1007
  234.7 24.0 %collective-permute-start.35 = (bf16[128,1024]{1,0:T(8,128)(2,1)S(1)}, bf16[128,1024]{1,0:T(8,128)(2,1)S(1)}, u32[]{:S(2)}, u32[]{:S(2)}) collective-permute-start(bf16[128,1024]{1,0:T(8,128)(2,1)S(1)} %get-tuple-element.144), channel_id=1, source_target_pairs={{0,2},{1,3},{2,4},{3,5},{4,6},{5,7},{6,0},{7,1},{8,10},{9,11},{10,... | collective-permute-start | bytes 786440 | tf_op jit(solution)/shard_map/ppermute | solution.py:1007
  234.7 33.1 %collective-permute-start.42 = (bf16[32,512]{1,0:T(8,128)(2,1)S(1)}, bf16[32,512]{1,0:T(8,128)(2,1)S(1)}, u32[]{:S(2)}, u32[]{:S(2)}) collective-permute-start(bf16[32,512]{1,0:T(8,128)(2,1)S(1)} %get-tuple-element.156), channel_id=1, source_target_pairs={{0,3},{1,2},{2,1},{3,0},{4,7},{5,6},{6,5},{7,4},{8,11},{9,10},{10,... | collective-permute-start | bytes 98312 | tf_op jit(solution)/shard_map/ppermute | solution.py:1007
  243.7 24.1 %collective-permute-start.43 = (bf16[32,512]{1,0:T(8,128)(2,1)S(1)}, bf16[32,512]{1,0:T(8,128)(2,1)S(1)}, u32[]{:S(2)}, u32[]{:S(2)}) collective-permute-start(bf16[32,512]{1,0:T(8,128)(2,1)S(1)} %get-tuple-element.157), channel_id=1, source_target_pairs={{0,4},{1,5},{2,6},{3,7},{4,0},{5,1},{6,2},{7,3},{8,12},{9,13},{10,... | collective-permute-start | bytes 98312 | tf_op jit(solution)/shard_map/ppermute | solution.py:1007
  247.1 20.7 %collective-permute-start.44 = (bf16[32,512]{1,0:T(8,128)(2,1)S(1)}, bf16[32,512]{1,0:T(8,128)(2,1)S(1)}, u32[]{:S(2)}, u32[]{:S(2)}) collective-permute-start(bf16[32,512]{1,0:T(8,128)(2,1)S(1)} %get-tuple-element.158), channel_id=1, source_target_pairs={{0,5},{1,4},{2,7},{3,6},{4,1},{5,0},{6,3},{7,2},{8,13},{9,12},{10,... | collective-permute-start | bytes 98312 | tf_op jit(solution)/shard_map/ppermute | solution.py:1007
  258.6 9.2 %collective-permute-start.45 = (bf16[32,512]{1,0:T(8,128)(2,1)S(1)}, bf16[32,512]{1,0:T(8,128)(2,1)S(1)}, u32[]{:S(2)}, u32[]{:S(2)}) collective-permute-start(bf16[32,512]{1,0:T(8,128)(2,1)S(1)} %get-tuple-element.159), channel_id=1, source_target_pairs={{0,6},{1,7},{2,4},{3,5},{4,2},{5,3},{6,0},{7,1},{8,14},{9,15},{10,... | collective-permute-start | bytes 98312 | tf_op jit(solution)/shard_map/ppermute | solution.py:1007
  258.7 9.2 %collective-permute-start.46 = (bf16[32,512]{1,0:T(8,128)(2,1)S(1)}, bf16[32,512]{1,0:T(8,128)(2,1)S(1)}, u32[]{:S(2)}, u32[]{:S(2)}) collective-permute-start(bf16[32,512]{1,0:T(8,128)(2,1)S(1)} %get-tuple-element.160), channel_id=1, source_target_pairs={{0,7},{1,6},{2,5},{3,4},{4,3},{5,2},{6,1},{7,0},{8,15},{9,14},{10,... | collective-permute-start | bytes 98312 | tf_op jit(solution)/shard_map/ppermute | solution.py:1007
  (30 other events, 358.6 us)

commit v3 on v2

--- a/solution.py
+++ b/solution.py
@@ -48,7 +48,7 @@
     count = len(operands) + len(far)
 
     def wrapped(*refs):
-        kernel(refs[0], *refs[1 : 1 + count], *refs[1 + count + len(after) :])
+        kernel(places(scalars), *refs[:count], *refs[count + len(after) :])
 
     flops, moved = cost or (0, 0)
     moved = moved or sum(held(a) for a in [*operands, *far])
@@ -57,8 +57,7 @@
         limit = sum(held(a) for a in scratch if "sem" not in str(a.dtype)) + (room << 20)
     results = pl.pallas_call(
         wrapped,
-        in_specs=[pl.BlockSpec(memory_space=pltpu.SMEM)]
-        + [vmem] * len(operands)
+        in_specs=[vmem] * len(operands)
         + [hbm] * len(far)
         + [pl.BlockSpec(memory_space=pl.ANY)] * len(after),
         out_specs=[vmem] * len(outs) + [hbm] * len(far_outs),
@@ -66,8 +65,13 @@
         scratch_shapes=scratch,
         compiler_params=pltpu.CompilerParams(vmem_limit_bytes=limit),
         cost_estimate=pl.CostEstimate(flops=flops, bytes_accessed=moved, transcendentals=0),
-    )(scalars, *operands, *far, *after)
+    )(*operands, *far, *after)
     return list(results)
+
+
+def places(group):
+    s, c = lax.axis_index("seq"), lax.axis_index("ctx")
+    return (lax.rem(c, 2), lax.div(c, 2), s, lax.rem(c, group), lax.div(c, group), c)
 
 
 def start_all(pairs, sems):
@@ -656,13 +660,19 @@
     )
 
 
-def split_fc_call(scalars, seqs, grad_fc1, grad_fc2):
+def split_fc_call(scalars, seqs, share, group, grad_fc1, grad_fc2, grad_out):
     width, cut = grad_fc1.shape
     rows = width // seqs
-
-    def kernel(at, one_ref, two_ref, *refs):
-        *outs, sem = refs
+    heads = grad_out.shape[0] // HEAD_DIM
+
+    def kernel(at, one_ref, two_ref, out_grad_ref, *refs):
+        outs, halves, sem = refs[:seqs], refs[seqs:-1], refs[-1]
         pairs = []
+        for k, ref in enumerate(halves):
+            for i in range(heads):
+                begin = i * HEAD_DIM + (at[SUB] ^ (k + 1)) * share
+                here = pl.ds(pl.multiple_of(begin, share), share)
+                pairs.append((out_grad_ref.at[here, :], ref.at[i]))
         for k, ref in enumerate(outs):
             here = rows_at(lax.rem(at[S] + seqs - k, seqs), rows)
             pairs += [
@@ -674,10 +684,10 @@
     return call(
         kernel,
         [],
-        [sems(2 * seqs)],
-        scalars,
-        (grad_fc1, grad_fc2),
-        far_outs=[shape((rows, 2 * cut))] * seqs,
+        [sems(2 * seqs + (group - 1) * heads)],
+        scalars,
+        (grad_fc1, grad_fc2, grad_out),
+        far_outs=[shape((rows, 2 * cut))] * seqs + [shape((heads, share, width))] * (group - 1),
     )
 
 
@@ -976,7 +986,6 @@
     b_fc2,
 ):
     seqs, ctxs = lax.axis_size("seq"), lax.axis_size("ctx")
-    s, c = lax.axis_index("seq"), lax.axis_index("ctx")
     _, piece, width = block_in.shape
     seq_len = piece * ctxs
     share = w_qkv.shape[0]
@@ -987,8 +996,7 @@
     lanes = ctxs // group
     rows = ctxs * share
     zs = ctxs // 2
-    sub, lane = c % group, c // group
-    scalars = jnp.stack([c % 2, c // 2, s, sub, lane, c]).astype(jnp.int32)
+    scalars = group
     total = 3 * heads * HEAD_DIM
     x_here, dy_here = block_in[0], cotangent[0]
 
@@ -1059,11 +1067,10 @@
     dy, dfc, dattn, sum_fc1 = backward_call(scalars, dy_all, w_fc_c, w_out_c, slope)
     grad_fc1 = rows_dot(h, dfc).astype(bf16)
     grad_fc2 = rows_dot(dy, act).astype(bf16)
-    fc_parts = split_fc_call(scalars, seqs, grad_fc1, grad_fc2)
+    grad_out = rows_dot(attn, dy).astype(bf16)
+    split = split_fc_call(scalars, seqs, share, group, grad_fc1, grad_fc2, grad_out)
+    fc_parts, halves = split[:seqs], split[seqs:]
     fc_parts = fc_parts[:1] + along("seq", fc_parts[1:], hops_s)
-    grad_out = rows_dot(attn, dy).astype(bf16)
-    blocks = grad_out.reshape(heads, group, share, width)
-    halves = [lax.dynamic_index_in_dim(blocks, sub ^ k, 1, keepdims=False) for k in range(1, group)]
     halves = along("ctx", halves, hops_g)
     dqkv, sum_qkv = attend_back_call(
         scalars, block, heads, kept, turned, dattn, lse, tables, (fc_parts[0],)

time: 272 us -> 259 us (0.952)
  Pallas kernels: 49.9 us -> 38.5 us
  waiting for transfers between devices: 70.9 us -> 80.9 us
  local copies, waits for them, and re-layouts: 13.4 us -> 3.82 us
    pallas_call x18, Pallas kernels: 49.9 us -> 38.5 us  [call(): pl.pallas_call(wrapped, in_specs=[vmem] * len(operands) + [hbm] * len(far...]
    ppermute x57, waiting for transfers between devices: 70.9 us -> 80.9 us  [along(): out.append(lax.ppermute(part, axis, pair))]
    unnamed x42 -> x12, local copies, waits for them, and re-layouts: 12.8 us -> 3.82 us
  transfers between devices with their start and end apart: 57 -> 57, of which waited for: 15 -> 16; matrix products, arithmetic and copies ran while one was open for 2% -> 2% of each run, Pallas kernels for 17% -> 13%
where the time goes in v3:
time: 259 us
  starting transfers between devices  129 us (50%)
  waiting for transfers between devices  80.9 us (31%)
  Pallas kernels  38.5 us (15%)
  matrix products  4.35 us (2%)
  local copies, waits for them, and re-layouts  3.82 us (1%)
    ppermute x57, starting transfers between devices, along(): out.append(lax.ppermute(part, axis, pair))  129 us
    ppermute x57, waiting for transfers between devices, along(): out.append(lax.ppermute(part, axis, pair))  80.9 us
    pallas_call x18, Pallas kernels, call(): pl.pallas_call(wrapped, in_specs=[vmem] * len(operands) + [hbm] * len(far...  38.5 us
  transfers between devices with their start and end apart: 57, of which 16 were waited for; matrix products, arithmetic and copies ran while one was open for 2% of the time, Pallas kernels for 13%

profile of v3, /device:TPU:0, one launch (start us, length us, event | category | flops | bytes accessed | tf_op | source)
XLA Modules:
  0.0 258.9 jit_solution(17445944389633054776)
XLA Ops:
  0.7 2.3 shard_map.220
  3.6 2.6 %collective-permute-start.1 = (bf16[32,1536]{1,0:T(8,128)(2,1)}, bf16[32,1536]{1,0:T(8,128)(2,1)S(1)}, u32[]{:S(2)}, u32[]{:S(2)}) collective-permute-start(bf16[32,1536]{1,0:T(8,128)(2,1)} %get-tuple-element.100), channel_id=1, source_target_pairs={{0,2},{1,3},{2,0},{3,1},{4,6},{5,7},{6,4},{7,5},{8,10},{9,11},{10,... | collective-permute-start | bytes 294920 | tf_op jit(solution)/shard_map/ppermute | solution.py:1015
  6.3 2.8 %collective-permute-start.3 = (bf16[32,1536]{1,0:T(8,128)(2,1)}, bf16[32,1536]{1,0:T(8,128)(2,1)S(1)}, u32[]{:S(2)}, u32[]{:S(2)}) collective-permute-start(bf16[32,1536]{1,0:T(8,128)(2,1)} %get-tuple-element.102), channel_id=1, source_target_pairs={{0,4},{1,5},{2,6},{3,7},{4,0},{5,1},{6,2},{7,3},{8,12},{9,13},{10,... | collective-permute-start | bytes 294920 | tf_op jit(solution)/shard_map/ppermute | solution.py:1015
  9.0 3.6 %collective-permute-start.10 = (bf16[128,1024]{1,0:T(8,128)(2,1)}, bf16[128,1024]{1,0:T(8,128)(2,1)S(1)}, u32[]{:S(2)}, u32[]{:S(2)}) collective-permute-start(bf16[128,1024]{1,0:T(8,128)(2,1)} %bitcast.29), channel_id=1, source_target_pairs={{0,6},{1,7},{2,0},{3,1},{4,2},{5,3},{6,4},{7,5},{8,14},{9,15},{10,... | collective-permute-start | bytes 786440 | tf_op jit(solution)/shard_map/ppermute | solution.py:1015
  12.6 1.5 collective-permute-start.5
  14.9 2.0 collective-permute-start.6
  17.3 2.0 collective-permute-done.4.refs_5_
  19.3 17.8 %collective-permute-start.12 = (bf16[128,1024]{1,0:T(8,128)(2,1)}, bf16[128,1024]{1,0:T(8,128)(2,1)S(1)}, u32[]{:S(2)}, u32[]{:S(2)}) collective-permute-start(bf16[128,1024]{1,0:T(8,128)(2,1)} %bitcast.31), channel_id=1, source_target_pairs={{0,2},{1,3},{2,4},{3,5},{4,6},{5,7},{6,0},{7,1},{8,10},{9,11},{10,... | collective-permute-start | bytes 786440 | tf_op jit(solution)/shard_map/ppermute | solution.py:1015
  37.0 1.4 collective-permute-start.25
  40.6 2.5 collective-permute-start.7
  43.1 7.5 %collective-permute-done.11.refs_8_ = bf16[128,1024]{1,0:T(8,128)(2,1)S(1)} collective-permute-done((bf16[128,1024]{1,0:T(8,128)(2,1)}, bf16[128,1024]{1,0:T(8,128)(2,1)S(1)}, u32[]{:S(2)}, u32[]{:S(2)}) %collective-permute-start.11) | collective-permute-done | bytes 262176 | tf_op jit(solution)/shard_map/ppermute | solution.py:1015
  50.6 11.9 %collective-permute-start.27 = (bf16[128,1024]{1,0:T(8,128)(2,1)}, bf16[128,1024]{1,0:T(8,128)(2,1)S(1)}, u32[]{:S(2)}, u32[]{:S(2)}) collective-permute-start(bf16[128,1024]{1,0:T(8,128)(2,1)} %bitcast.23), channel_id=1, source_target_pairs={{0,2},{1,3},{2,4},{3,5},{4,6},{5,7},{6,0},{7,1},{8,10},{9,11},{10,... | collective-permute-start | bytes 786440 | tf_op jit(solution)/shard_map/ppermute | solution.py:1015
  62.6 1.5 collective-permute-start.8
  64.1 1.5 collective-permute-start.9
  65.6 7.2 %collective-permute-done.26.refs_5_ = bf16[128,1024]{1,0:T(8,128)(2,1)S(1)} collective-permute-done((bf16[128,1024]{1,0:T(8,128)(2,1)}, bf16[128,1024]{1,0:T(8,128)(2,1)S(1)}, u32[]{:S(2)}, u32[]{:S(2)}) %collective-permute-start.26) | collective-permute-done | bytes 262176 | tf_op jit(solution)/shard_map/ppermute | solution.py:1015
  72.8 2.4 collective-permute-start.17
  75.8 2.0 collective-permute-done.8.refs_2_.refs_16_
  80.9 6.8 %collective-permute-done.17.refs_4_ = bf16[256,1024]{1,0:T(8,128)(2,1)S(1)} collective-permute-done((bf16[256,1024]{1,0:T(8,128)(2,1)S(1)}, bf16[256,1024]{1,0:T(8,128)(2,1)S(1)}, u32[]{:S(2)}, u32[]{:S(2)}) %collective-permute-start.17) | collective-permute-done | bytes 524320 | tf_op jit(solution)/shard_map/ppermute | solution.py:1015
  87.7 12.9 %collective-permute-done.18.refs_5_ = bf16[256,1024]{1,0:T(8,128)(2,1)S(1)} collective-permute-done((bf16[256,1024]{1,0:T(8,128)(2,1)S(1)}, bf16[256,1024]{1,0:T(8,128)(2,1)S(1)}, u32[]{:S(2)}, u32[]{:S(2)}) %collective-permute-start.18) | collective-permute-done | bytes 524320 | tf_op jit(solution)/shard_map/ppermute | solution.py:1015
  100.6 7.2 %shard_map.224 = (bf16[1024,1024]{1,0:T(8,128)(2,1)S(1)}, bf16[1024,1024]{1,0:T(8,128)(2,1)S(1)}, bf16[1024,128]{1,0:T(8,128)(2,1)S(1)}, f32[2,1024]{1,0:T(2,128...) custom-call(f32[1,1024]{1,0:T(1,128)S(1)} %get-tuple-element.107.refs_0_.refs_2_,, ...), custom_call_target="tpu_custom_call" | custom-call | flops 1610612736 | bytes 3584000 | tf_op jit(solution)/shard_map/pallas_call | solution.py:58
  107.8 5.6 %shard_map.225 = (bf16[1024,1024]{1,0:T(8,128)(2,1)S(1)}, bf16[1024,512]{1,0:T(8,128)(2,1)S(1)}, bf16[1024,512]{1,0:T(8,128)(2,1)S(1)}, bf16[512,1024]{1,0:T(8,1...) custom-call(bf16[1024,1024]{1,0:T(8,128)(2,1)S(1)} %get-tuple-element.113.refs_0_, ...), custom_call_target="tpu_custom_call" | custom-call | flops 2147483648 | bytes 4734976 | tf_op jit(solution)/shard_map/pallas_call | solution.py:58
  114.0 2.7 %shard_map.227 = (bf16[1024,1024]{1,0:T(8,128)(2,1)S(1)}, bf16[1024,512]{1,0:T(8,128)(2,1)S(1)}, bf16[1024,128]{1,0:T(8,128)(2,1)S(1)}, f32[1,512]{1,0:T(1,128)S(1)}) custom-call(bf16[1024,1024]{1,0:T(8,128)(2,1)S(1)} %get-tuple-element.126.refs_0_.refs_1_, bf16[128,1024]{1,0:T(8,128)(2,1)S(1)} %get-tuple-element.127.refs_1_, ...), custom_call_target="tpu_custom_call" | custom-call | flops 1073741824 | bytes 5505024 | tf_op jit(solution)/shard_map/pallas_call | solution.py:58
  116.8 1.3 convolution_convert_fusion.1.refs_0_
  118.1 1.3 convolution_convert_fusion.refs_1_
  120.5 5.7 %shard_map.229 = (bf16[1024,384]{1,0:T(8,128)(2,1)S(1)}, f32[1,384]{1,0:T(1,128)S(1)}) custom-call(bf16[1024,384]{1,0:T(8,128)(2,1)S(1)} %get-tuple-element.130.refs_0_, bf16[256,1024]{1,0:T(8,128)(2,1)S(1)} %get-tuple-element.131.refs_1_, bf16[1024,128]{1,0:T(8,128)(2,1)S(1)} %get-tuple-element.132.refs_2_, f32[2,1024]{1,0:T(2,128)S(1)} %get-tuple-element.133.refs_3_, ...), custom_call_target="tpu_custom_call" | custom-call | flops 1342177280 | bytes 1703936 | tf_op jit(solution)/shard_map/pallas_call | solution.py:58
  126.2 3.3 %shard_map.230 = (bf16[512,1024]{1,0:T(8,128)(2,1)S(1)}, f32[1,1024]{1,0:T(1,128)S(1)}, f32[1,1024]{1,0:T(1,128)S(1)}, bf16[512,1024]{1,0:T(8,128)(2,1)S(1)}) custom-call(bf16[1024,512]{1,0:T(8,128)(2,1)S(1)} %get-tuple-element.129.refs_0_, bf16[1024,1024]{1,0:T(8,128)(2,1)S(1)} %get-tuple-element.126.refs_0_.refs_1_, ...), custom_call_target="tpu_custom_call" | custom-call | flops 1073741824 | bytes 6815744 | tf_op jit(solution)/shard_map/pallas_call | solution.py:58
  130.1 1.3 convolution_convert_fusion.2.refs_0_
  134.8 2.2 collective-permute-start.47
  136.9 7.1 %collective-permute-done.37.refs_1_ = bf16[320,512]{1,0:T(8,128)(2,1)S(1)} collective-permute-done((bf16[320,512]{1,0:T(8,128)(2,1)S(1)}, bf16[320,512]{1,0:T(8,128)(2,1)S(1)}, u32[]{:S(2)}, u32[]{:S(2)}) %collective-permute-start.37) | collective-permute-done | bytes 327712 | tf_op jit(solution)/shard_map/ppermute | solution.py:1015
  145.3 17.2 %collective-permute-start.49 = (bf16[256,1024]{1,0:T(8,128)(2,1)S(1)}, bf16[256,1024]{1,0:T(8,128)(2,1)S(1)}, u32[]{:S(2)}, u32[]{:S(2)}) collective-permute-start(bf16[256,1024]{1,0:T(8,128)(2,1)S(1)} %get-tuple-element.165), channel_id=1, source_target_pairs={{0,8},{8,16},{16,24},{24,0},{1,9},{9,17},{17,25},{25,1},{2,10},{10... | collective-permute-start | bytes 1572872 | tf_op jit(solution)/shard_map/ppermute | solution.py:1015
  163.0 19.0 %collective-permute-done.39.refs_3_ = bf16[320,512]{1,0:T(8,128)(2,1)S(1)} collective-permute-done((bf16[320,512]{1,0:T(8,128)(2,1)S(1)}, bf16[320,512]{1,0:T(8,128)(2,1)S(1)}, u32[]{:S(2)}, u32[]{:S(2)}) %collective-permute-start.39) | collective-permute-done | bytes 327712 | tf_op jit(solution)/shard_map/ppermute | solution.py:1015
  182.0 1.8 collective-permute-start.24
  183.8 1.9 shard_map.234
  187.6 1.7 collective-permute-start.51
  189.4 2.7 %collective-permute-done.41.refs_2_ = bf16[32,512]{1,0:T(8,128)(2,1)S(1)} collective-permute-done((bf16[32,512]{1,0:T(8,128)(2,1)S(1)}, bf16[32,512]{1,0:T(8,128)(2,1)S(1)}, u32[]{:S(2)}, u32[]{:S(2)}) %collective-permute-start.41) | collective-permute-done | bytes 32800 | tf_op jit(solution)/shard_map/ppermute | solution.py:1015
  194.5 3.2 %collective-permute-done.52.refs_3_ = bf16[32,1024]{1,0:T(8,128)(2,1)S(1)} collective-permute-done((bf16[32,1024]{1,0:T(8,128)(2,1)S(1)}, bf16[32,1024]{1,0:T(8,128)(2,1)S(1)}, u32[]{:S(2)}, u32[]{:S(2)}) %collective-permute-start.52) | collective-permute-done | bytes 65568 | tf_op jit(solution)/shard_map/ppermute | solution.py:1015
  197.7 3.5 %collective-permute-start.56 = (bf16[32,1024]{1,0:T(8,128)(2,1)S(1)}, bf16[32,1024]{1,0:T(8,128)(2,1)S(1)}, u32[]{:S(2)}, u32[]{:S(2)}) collective-permute-start(bf16[32,1024]{1,0:T(8,128)(2,1)S(1)} %get-tuple-element.173), channel_id=1, source_target_pairs={{0,7},{1,6},{2,5},{3,4},{4,3},{5,2},{6,1},{7,0},{8,15},{9,14},{10,... | collective-permute-start | bytes 196616 | tf_op jit(solution)/shard_map/ppermute | solution.py:1015
  201.7 3.0 %collective-permute-start.22 = (bf16[128,1024]{1,0:T(8,128)(2,1)S(1)}, bf16[128,1024]{1,0:T(8,128)(2,1)S(1)}, u32[]{:S(2)}, u32[]{:S(2)}) collective-permute-start(bf16[128,1024]{1,0:T(8,128)(2,1)S(1)} %get-tuple-element.123), channel_id=1, source_target_pairs={{0,6},{1,7},{2,0},{3,1},{4,2},{5,3},{6,4},{7,5},{8,14},{9,15},{10,... | collective-permute-start | bytes 786440 | tf_op jit(solution)/shard_map/ppermute | solution.py:1015
  204.7 1.4 collective-permute-start.33
  206.1 18.8 %collective-permute-start.34 = (bf16[128,1024]{1,0:T(8,128)(2,1)S(1)}, bf16[128,1024]{1,0:T(8,128)(2,1)S(1)}, u32[]{:S(2)}, u32[]{:S(2)}) collective-permute-start(bf16[128,1024]{1,0:T(8,128)(2,1)S(1)} %get-tuple-element.144), channel_id=1, source_target_pairs={{0,4},{1,5},{2,6},{3,7},{4,0},{5,1},{6,2},{7,3},{8,12},{9,13},{10,... | collective-permute-start | bytes 786440 | tf_op jit(solution)/shard_map/ppermute | solution.py:1015
  224.9 9.0 %collective-permute-start.42 = (bf16[32,512]{1,0:T(8,128)(2,1)S(1)}, bf16[32,512]{1,0:T(8,128)(2,1)S(1)}, u32[]{:S(2)}, u32[]{:S(2)}) collective-permute-start(bf16[32,512]{1,0:T(8,128)(2,1)S(1)} %get-tuple-element.158), channel_id=1, source_target_pairs={{0,3},{1,2},{2,1},{3,0},{4,7},{5,6},{6,5},{7,4},{8,11},{9,10},{10,... | collective-permute-start | bytes 98312 | tf_op jit(solution)/shard_map/ppermute | solution.py:1015
  233.9 3.4 %collective-permute-start.43 = (bf16[32,512]{1,0:T(8,128)(2,1)S(1)}, bf16[32,512]{1,0:T(8,128)(2,1)S(1)}, u32[]{:S(2)}, u32[]{:S(2)}) collective-permute-start(bf16[32,512]{1,0:T(8,128)(2,1)S(1)} %get-tuple-element.159), channel_id=1, source_target_pairs={{0,4},{1,5},{2,6},{3,7},{4,0},{5,1},{6,2},{7,3},{8,12},{9,13},{10,... | collective-permute-start | bytes 98312 | tf_op jit(solution)/shard_map/ppermute | solution.py:1015
  237.3 3.5 %collective-permute-start.44 = (bf16[32,512]{1,0:T(8,128)(2,1)S(1)}, bf16[32,512]{1,0:T(8,128)(2,1)S(1)}, u32[]{:S(2)}, u32[]{:S(2)}) collective-permute-start(bf16[32,512]{1,0:T(8,128)(2,1)S(1)} %get-tuple-element.160), channel_id=1, source_target_pairs={{0,5},{1,4},{2,7},{3,6},{4,1},{5,0},{6,3},{7,2},{8,13},{9,12},{10,... | collective-permute-start | bytes 98312 | tf_op jit(solution)/shard_map/ppermute | solution.py:1015
  240.8 7.1 %collective-permute-done.34.refs_5_ = bf16[128,1024]{1,0:T(8,128)(2,1)S(1)} collective-permute-done((bf16[128,1024]{1,0:T(8,128)(2,1)S(1)}, bf16[128,1024]{1,0:T(8,128)(2,1)S(1)}, u32[]{:S(2)}, u32[]{:S(2)}) %collective-permute-start.34) | collective-permute-done | bytes 262176 | tf_op jit(solution)/shard_map/ppermute | solution.py:1015
  247.9 3.3 %collective-permute-start.46 = (bf16[32,512]{1,0:T(8,128)(2,1)S(1)}, bf16[32,512]{1,0:T(8,128)(2,1)S(1)}, u32[]{:S(2)}, u32[]{:S(2)}) collective-permute-start(bf16[32,512]{1,0:T(8,128)(2,1)S(1)} %get-tuple-element.162), channel_id=1, source_target_pairs={{0,7},{1,6},{2,5},{3,4},{4,3},{5,2},{6,1},{7,0},{8,15},{9,14},{10,... | collective-permute-start | bytes 98312 | tf_op jit(solution)/shard_map/ppermute | solution.py:1015
  252.1 1.4 shard_map.232.refs_8_
  254.5 1.8 shard_map.236
  257.4 1.3 shard_map.237
  (101 shorter events, 22.7 us)
Async XLA Ops:
  3.0 6.0 %collective-permute-start = (bf16[32,1536]{1,0:T(8,128)(2,1)}, bf16[32,1536]{1,0:T(8,128)(2,1)S(1)}, u32[]{:S(2)}, u32[]{:S(2)}) collective-permute-start(bf16[32,1536]{1,0:T(8,128)(2,1)} %get-tuple-element.99), channel_id=1, source_target_pairs={{0,1},{1,0},{2,3},{3,2},{4,5},{5,4},{6,7},{7,6},{8,9},{9,8},{10,11... | collective-permute-start | bytes 294920 | tf_op jit(solution)/shard_map/ppermute | solution.py:1015
  3.6 9.1 %collective-permute-start.1 = (bf16[32,1536]{1,0:T(8,128)(2,1)}, bf16[32,1536]{1,0:T(8,128)(2,1)S(1)}, u32[]{:S(2)}, u32[]{:S(2)}) collective-permute-start(bf16[32,1536]{1,0:T(8,128)(2,1)} %get-tuple-element.100), channel_id=1, source_target_pairs={{0,2},{1,3},{2,0},{3,1},{4,6},{5,7},{6,4},{7,5},{8,10},{9,11},{10,... | collective-permute-start | bytes 294920 | tf_op jit(solution)/shard_map/ppermute | solution.py:1015
  6.2 8.7 %collective-permute-start.2 = (bf16[32,1536]{1,0:T(8,128)(2,1)}, bf16[32,1536]{1,0:T(8,128)(2,1)S(1)}, u32[]{:S(2)}, u32[]{:S(2)}) collective-permute-start(bf16[32,1536]{1,0:T(8,128)(2,1)} %get-tuple-element.101), channel_id=1, source_target_pairs={{0,3},{1,2},{2,1},{3,0},{4,7},{5,6},{6,5},{7,4},{8,11},{9,10},{10,... | collective-permute-start | bytes 294920 | tf_op jit(solution)/shard_map/ppermute | solution.py:1015
  6.3 10.6 %collective-permute-start.3 = (bf16[32,1536]{1,0:T(8,128)(2,1)}, bf16[32,1536]{1,0:T(8,128)(2,1)S(1)}, u32[]{:S(2)}, u32[]{:S(2)}) collective-permute-start(bf16[32,1536]{1,0:T(8,128)(2,1)} %get-tuple-element.102), channel_id=1, source_target_pairs={{0,4},{1,5},{2,6},{3,7},{4,0},{5,1},{6,2},{7,3},{8,12},{9,13},{10,... | collective-permute-start | bytes 294920 | tf_op jit(solution)/shard_map/ppermute | solution.py:1015
  9.0 10.3 %collective-permute-start.4 = (bf16[32,1536]{1,0:T(8,128)(2,1)}, bf16[32,1536]{1,0:T(8,128)(2,1)S(1)}, u32[]{:S(2)}, u32[]{:S(2)}) collective-permute-start(bf16[32,1536]{1,0:T(8,128)(2,1)} %get-tuple-element.103), channel_id=1, source_target_pairs={{0,5},{1,4},{2,7},{3,6},{4,1},{5,0},{6,3},{7,2},{8,13},{9,12},{10,... | collective-permute-start | bytes 294920 | tf_op jit(solution)/shard_map/ppermute | solution.py:1015
  9.0 31.6 %collective-permute-start.10 = (bf16[128,1024]{1,0:T(8,128)(2,1)}, bf16[128,1024]{1,0:T(8,128)(2,1)S(1)}, u32[]{:S(2)}, u32[]{:S(2)}) collective-permute-start(bf16[128,1024]{1,0:T(8,128)(2,1)} %bitcast.29), channel_id=1, source_target_pairs={{0,6},{1,7},{2,0},{3,1},{4,2},{5,3},{6,4},{7,5},{8,14},{9,15},{10,... | collective-permute-start | bytes 786440 | tf_op jit(solution)/shard_map/ppermute | solution.py:1015
  12.6 24.4 %collective-permute-start.5 = (bf16[32,1536]{1,0:T(8,128)(2,1)}, bf16[32,1536]{1,0:T(8,128)(2,1)S(1)}, u32[]{:S(2)}, u32[]{:S(2)}) collective-permute-start(bf16[32,1536]{1,0:T(8,128)(2,1)} %get-tuple-element.104), channel_id=1, source_target_pairs={{0,6},{1,7},{2,4},{3,5},{4,2},{5,3},{6,0},{7,1},{8,14},{9,15},{10,... | collective-permute-start | bytes 294920 | tf_op jit(solution)/shard_map/ppermute | solution.py:1015
  14.9 22.2 %collective-permute-start.6 = (bf16[32,1536]{1,0:T(8,128)(2,1)}, bf16[32,1536]{1,0:T(8,128)(2,1)S(1)}, u32[]{:S(2)}, u32[]{:S(2)}) collective-permute-start(bf16[32,1536]{1,0:T(8,128)(2,1)} %get-tuple-element.105), channel_id=1, source_target_pairs={{0,7},{1,6},{2,5},{3,4},{4,3},{5,2},{6,1},{7,0},{8,15},{9,14},{10,... | collective-permute-start | bytes 294920 | tf_op jit(solution)/shard_map/ppermute | solution.py:1015
  16.9 33.7 %collective-permute-start.11 = (bf16[128,1024]{1,0:T(8,128)(2,1)}, bf16[128,1024]{1,0:T(8,128)(2,1)S(1)}, u32[]{:S(2)}, u32[]{:S(2)}) collective-permute-start(bf16[128,1024]{1,0:T(8,128)(2,1)} %bitcast.30), channel_id=1, source_target_pairs={{0,4},{1,5},{2,6},{3,7},{4,0},{5,1},{6,2},{7,3},{8,12},{9,13},{10,... | collective-permute-start | bytes 786440 | tf_op jit(solution)/shard_map/ppermute | solution.py:1015
  19.3 31.4 %collective-permute-start.12 = (bf16[128,1024]{1,0:T(8,128)(2,1)}, bf16[128,1024]{1,0:T(8,128)(2,1)S(1)}, u32[]{:S(2)}, u32[]{:S(2)}) collective-permute-start(bf16[128,1024]{1,0:T(8,128)(2,1)} %bitcast.31), channel_id=1, source_target_pairs={{0,2},{1,3},{2,4},{3,5},{4,6},{5,7},{6,0},{7,1},{8,10},{9,11},{10,... | collective-permute-start | bytes 786440 | tf_op jit(solution)/shard_map/ppermute | solution.py:1015
  37.0 25.6 %collective-permute-start.13 = (bf16[128,1024]{1,0:T(8,128)(2,1)}, bf16[128,1024]{1,0:T(8,128)(2,1)S(1)}, u32[]{:S(2)}, u32[]{:S(2)}) collective-permute-start(bf16[128,1024]{1,0:T(8,128)(2,1)} %bitcast.32), channel_id=1, source_target_pairs={{0,1},{1,0},{2,3},{3,2},{4,5},{5,4},{6,7},{7,6},{8,9},{9,8},{10,11... | collective-permute-start | bytes 786440 | tf_op jit(solution)/shard_map/ppermute | solution.py:1015
  37.0 27.1 %collective-permute-start.25 = (bf16[128,1024]{1,0:T(8,128)(2,1)}, bf16[128,1024]{1,0:T(8,128)(2,1)S(1)}, u32[]{:S(2)}, u32[]{:S(2)}) collective-permute-start(bf16[128,1024]{1,0:T(8,128)(2,1)} %bitcast.21), channel_id=1, source_target_pairs={{0,6},{1,7},{2,0},{3,1},{4,2},{5,3},{6,4},{7,5},{8,14},{9,15},{10,... | collective-permute-start | bytes 786440 | tf_op jit(solution)/shard_map/ppermute | solution.py:1015
  40.6 34.7 %collective-permute-start.7 = (bf16[320,512]{1,0:T(8,128)(2,1)S(1)}, bf16[320,512]{1,0:T(8,128)(2,1)S(1)}, u32[]{:S(2)}, u32[]{:S(2)}) collective-permute-start(bf16[320,512]{1,0:T(8,128)(2,1)S(1)} %get-tuple-element.106.refs_0_.refs_14_), channel_id=1, source_target_pairs={{0,24},{8,0},{16,8},{24,16},{1,25},{9,1},{17,9},{25,17},{2,26},{10... | collective-permute-start | bytes 983048 | tf_op jit(solution)/shard_map/ppermute | solution.py:1015
  50.6 22.2 %collective-permute-start.26 = (bf16[128,1024]{1,0:T(8,128)(2,1)}, bf16[128,1024]{1,0:T(8,128)(2,1)S(1)}, u32[]{:S(2)}, u32[]{:S(2)}) collective-permute-start(bf16[128,1024]{1,0:T(8,128)(2,1)} %bitcast.22), channel_id=1, source_target_pairs={{0,4},{1,5},{2,6},{3,7},{4,0},{5,1},{6,2},{7,3},{8,12},{9,13},{10,... | collective-permute-start | bytes 786440 | tf_op jit(solution)/shard_map/ppermute | solution.py:1015
  50.6 22.2 %collective-permute-start.27 = (bf16[128,1024]{1,0:T(8,128)(2,1)}, bf16[128,1024]{1,0:T(8,128)(2,1)S(1)}, u32[]{:S(2)}, u32[]{:S(2)}) collective-permute-start(bf16[128,1024]{1,0:T(8,128)(2,1)} %bitcast.23), channel_id=1, source_target_pairs={{0,2},{1,3},{2,4},{3,5},{4,6},{5,7},{6,0},{7,1},{8,10},{9,11},{10,... | collective-permute-start | bytes 786440 | tf_op jit(solution)/shard_map/ppermute | solution.py:1015
  62.6 15.3 %collective-permute-start.8 = (bf16[320,512]{1,0:T(8,128)(2,1)S(1)}, bf16[320,512]{1,0:T(8,128)(2,1)S(1)}, u32[]{:S(2)}, u32[]{:S(2)}) collective-permute-start(bf16[320,512]{1,0:T(8,128)(2,1)S(1)} %get-tuple-element.106.refs_0_.refs_14_), channel_id=1, source_target_pairs={{0,16},{8,24},{16,0},{24,8},{1,17},{9,25},{17,1},{25,9},{2,18},{10... | collective-permute-start | bytes 983048 | tf_op jit(solution)/shard_map/ppermute | solution.py:1015
  64.1 13.7 %collective-permute-start.9 = (bf16[320,512]{1,0:T(8,128)(2,1)S(1)}, bf16[320,512]{1,0:T(8,128)(2,1)S(1)}, u32[]{:S(2)}, u32[]{:S(2)}) collective-permute-start(bf16[320,512]{1,0:T(8,128)(2,1)S(1)} %get-tuple-element.106.refs_0_.refs_14_), channel_id=1, source_target_pairs={{0,8},{8,16},{16,24},{24,0},{1,9},{9,17},{17,25},{25,1},{2,10},{10... | collective-permute-start | bytes 983048 | tf_op jit(solution)/shard_map/ppermute | solution.py:1015
  72.8 14.8 %collective-permute-start.17 = (bf16[256,1024]{1,0:T(8,128)(2,1)S(1)}, bf16[256,1024]{1,0:T(8,128)(2,1)S(1)}, u32[]{:S(2)}, u32[]{:S(2)}) collective-permute-start(bf16[256,1024]{1,0:T(8,128)(2,1)S(1)} %get-tuple-element.116.refs_3_), channel_id=1, source_target_pairs={{0,24},{8,0},{16,8},{24,16},{1,25},{9,1},{17,9},{25,17},{2,26},{10... | collective-permute-start | bytes 1572872 | tf_op jit(solution)/shard_map/ppermute | solution.py:1015
  75.3 25.3 %collective-permute-start.18 = (bf16[256,1024]{1,0:T(8,128)(2,1)S(1)}, bf16[256,1024]{1,0:T(8,128)(2,1)S(1)}, u32[]{:S(2)}, u32[]{:S(2)}) collective-permute-start(bf16[256,1024]{1,0:T(8,128)(2,1)S(1)} %get-tuple-element.116.refs_3_), channel_id=1, source_target_pairs={{0,16},{8,24},{16,0},{24,8},{1,17},{9,25},{17,1},{25,9},{2,18},{10... | collective-permute-start | bytes 1572872 | tf_op jit(solution)/shard_map/ppermute | solution.py:1015
  77.8 30.0 %collective-permute-start.19 = (bf16[256,1024]{1,0:T(8,128)(2,1)S(1)}, bf16[256,1024]{1,0:T(8,128)(2,1)S(1)}, u32[]{:S(2)}, u32[]{:S(2)}) collective-permute-start(bf16[256,1024]{1,0:T(8,128)(2,1)S(1)} %get-tuple-element.116.refs_3_), channel_id=1, source_target_pairs={{0,8},{8,16},{16,24},{24,0},{1,9},{9,17},{17,25},{25,1},{2,10},{10... | collective-permute-start | bytes 1572872 | tf_op jit(solution)/shard_map/ppermute | solution.py:1015
  79.9 34.1 %collective-permute-start.28 = (bf16[128,1024]{1,0:T(8,128)(2,1)S(1)}, bf16[128,1024]{1,0:T(8,128)(2,1)S(1)}, u32[]{:S(2)}, u32[]{:S(2)}) collective-permute-start(bf16[128,1024]{1,0:T(8,128)(2,1)S(1)} %bitcast.24), channel_id=1, source_target_pairs={{0,1},{1,0},{2,3},{3,2},{4,5},{5,4},{6,7},{7,6},{8,9},{9,8},{10,11... | collective-permute-start | bytes 786440 | tf_op jit(solution)/shard_map/ppermute | solution.py:1015
  80.7 33.3 %collective-permute-start.29 = (bf16[128,1024]{1,0:T(8,128)(2,1)S(1)}, bf16[128,1024]{1,0:T(8,128)(2,1)S(1)}, u32[]{:S(2)}, u32[]{:S(2)}) collective-permute-start(bf16[128,1024]{1,0:T(8,128)(2,1)S(1)} %collective-permute-done.25.refs_4_), channel_id=1, source_target_pairs={{0,1},{1,0},{2,3},{3,2},{4,5},{5,4},{6,7},{7,6},{8,9},{9,8},{10,11... | collective-permute-start | bytes 786440 | tf_op jit(solution)/shard_map/ppermute | solution.py:1015
  87.7 26.4 %collective-permute-start.30 = (bf16[128,1024]{1,0:T(8,128)(2,1)S(1)}, bf16[128,1024]{1,0:T(8,128)(2,1)S(1)}, u32[]{:S(2)}, u32[]{:S(2)}) collective-permute-start(bf16[128,1024]{1,0:T(8,128)(2,1)S(1)} %collective-permute-done.26.refs_5_), channel_id=1, source_target_pairs={{0,1},{1,0},{2,3},{3,2},{4,5},{5,4},{6,7},{7,6},{8,9},{9,8},{10,11... | collective-permute-start | bytes 786440 | tf_op jit(solution)/shard_map/ppermute | solution.py:1015
  100.6 13.4 %collective-permute-start.31 = (bf16[128,1024]{1,0:T(8,128)(2,1)S(1)}, bf16[128,1024]{1,0:T(8,128)(2,1)S(1)}, u32[]{:S(2)}, u32[]{:S(2)}) collective-permute-start(bf16[128,1024]{1,0:T(8,128)(2,1)S(1)} %collective-permute-done.27.refs_6_), channel_id=1, source_target_pairs={{0,1},{1,0},{2,3},{3,2},{4,5},{5,4},{6,7},{7,6},{8,9},{9,8},{10,11... | collective-permute-start | bytes 786440 | tf_op jit(solution)/shard_map/ppermute | solution.py:1015
  113.4 49.1 %collective-permute-start.21 = (bf16[512,1024]{1,0:T(8,128)(2,1)S(1)}, bf16[512,1024]{1,0:T(8,128)(2,1)S(1)}, u32[]{:S(2)}, u32[]{:S(2)}) collective-permute-start(bf16[512,1024]{1,0:T(8,128)(2,1)S(1)} %get-tuple-element.120), channel_id=1, source_target_pairs={{0,1},{1,0},{2,3},{3,2},{4,5},{5,4},{6,7},{7,6},{8,9},{9,8},{10,11... | collective-permute-start | bytes 3145736 | tf_op jit(solution)/shard_map/ppermute | solution.py:1015
  129.5 68.2 %collective-permute-start.32 = (bf16[512,1024]{1,0:T(8,128)(2,1)S(1)}, bf16[512,1024]{1,0:T(8,128)(2,1)S(1)}, u32[]{:S(2)}, u32[]{:S(2)}) collective-permute-start(bf16[512,1024]{1,0:T(8,128)(2,1)S(1)} %get-tuple-element.141), channel_id=1, source_target_pairs={{0,1},{1,0},{2,3},{3,2},{4,5},{5,4},{6,7},{7,6},{8,9},{9,8},{10,11... | collective-permute-start | bytes 3145736 | tf_op jit(solution)/shard_map/ppermute | solution.py:1015
  133.4 10.6 %collective-permute-start.37 = (bf16[320,512]{1,0:T(8,128)(2,1)S(1)}, bf16[320,512]{1,0:T(8,128)(2,1)S(1)}, u32[]{:S(2)}, u32[]{:S(2)}) collective-permute-start(bf16[320,512]{1,0:T(8,128)(2,1)S(1)} %get-tuple-element.152), channel_id=1, source_target_pairs={{0,24},{8,0},{16,8},{24,16},{1,25},{9,1},{17,9},{25,17},{2,26},{10... | collective-permute-start | bytes 983048 | tf_op jit(solution)/shard_map/ppermute | solution.py:1015
  134.0 11.3 %collective-permute-start.38 = (bf16[320,512]{1,0:T(8,128)(2,1)S(1)}, bf16[320,512]{1,0:T(8,128)(2,1)S(1)}, u32[]{:S(2)}, u32[]{:S(2)}) collective-permute-start(bf16[320,512]{1,0:T(8,128)(2,1)S(1)} %get-tuple-element.153), channel_id=1, source_target_pairs={{0,16},{8,24},{16,0},{24,8},{1,17},{9,25},{17,1},{25,9},{2,18},{10... | collective-permute-start | bytes 983048 | tf_op jit(solution)/shard_map/ppermute | solution.py:1015
  134.8 51.0 %collective-permute-start.47 = (bf16[256,1024]{1,0:T(8,128)(2,1)S(1)}, bf16[256,1024]{1,0:T(8,128)(2,1)S(1)}, u32[]{:S(2)}, u32[]{:S(2)}) collective-permute-start(bf16[256,1024]{1,0:T(8,128)(2,1)S(1)} %get-tuple-element.163), channel_id=1, source_target_pairs={{0,24},{8,0},{16,8},{24,16},{1,25},{9,1},{17,9},{25,17},{2,26},{10... | collective-permute-start | bytes 1572872 | tf_op jit(solution)/shard_map/ppermute | solution.py:1015
  144.0 41.8 %collective-permute-start.48 = (bf16[256,1024]{1,0:T(8,128)(2,1)S(1)}, bf16[256,1024]{1,0:T(8,128)(2,1)S(1)}, u32[]{:S(2)}, u32[]{:S(2)}) collective-permute-start(bf16[256,1024]{1,0:T(8,128)(2,1)S(1)} %get-tuple-element.164), channel_id=1, source_target_pairs={{0,16},{8,24},{16,0},{24,8},{1,17},{9,25},{17,1},{25,9},{2,18},{10... | collective-permute-start | bytes 1572872 | tf_op jit(solution)/shard_map/ppermute | solution.py:1015
  145.3 40.9 %collective-permute-start.49 = (bf16[256,1024]{1,0:T(8,128)(2,1)S(1)}, bf16[256,1024]{1,0:T(8,128)(2,1)S(1)}, u32[]{:S(2)}, u32[]{:S(2)}) collective-permute-start(bf16[256,1024]{1,0:T(8,128)(2,1)S(1)} %get-tuple-element.165), channel_id=1, source_target_pairs={{0,8},{8,16},{16,24},{24,0},{1,9},{9,17},{17,25},{25,1},{2,10},{10... | collective-permute-start | bytes 1572872 | tf_op jit(solution)/shard_map/ppermute | solution.py:1015
  162.5 19.5 %collective-permute-start.39 = (bf16[320,512]{1,0:T(8,128)(2,1)S(1)}, bf16[320,512]{1,0:T(8,128)(2,1)S(1)}, u32[]{:S(2)}, u32[]{:S(2)}) collective-permute-start(bf16[320,512]{1,0:T(8,128)(2,1)S(1)} %get-tuple-element.154), channel_id=1, source_target_pairs={{0,8},{8,16},{16,24},{24,0},{1,9},{9,17},{17,25},{25,1},{2,10},{10... | collective-permute-start | bytes 983048 | tf_op jit(solution)/shard_map/ppermute | solution.py:1015
  182.0 42.9 %collective-permute-start.24 = (bf16[128,1024]{1,0:T(8,128)(2,1)S(1)}, bf16[128,1024]{1,0:T(8,128)(2,1)S(1)}, u32[]{:S(2)}, u32[]{:S(2)}) collective-permute-start(bf16[128,1024]{1,0:T(8,128)(2,1)S(1)} %get-tuple-element.125), channel_id=1, source_target_pairs={{0,2},{1,3},{2,4},{3,5},{4,6},{5,7},{6,0},{7,1},{8,10},{9,11},{10,... | collective-permute-start | bytes 786440 | tf_op jit(solution)/shard_map/ppermute | solution.py:1015
  185.8 6.3 %collective-permute-start.41 = (bf16[32,512]{1,0:T(8,128)(2,1)S(1)}, bf16[32,512]{1,0:T(8,128)(2,1)S(1)}, u32[]{:S(2)}, u32[]{:S(2)}) collective-permute-start(bf16[32,512]{1,0:T(8,128)(2,1)S(1)} %get-tuple-element.157), channel_id=1, source_target_pairs={{0,2},{1,3},{2,0},{3,1},{4,6},{5,7},{6,4},{7,5},{8,10},{9,11},{10,... | collective-permute-start | bytes 98312 | tf_op jit(solution)/shard_map/ppermute | solution.py:1015
  192.1 9.5 %collective-permute-start.53 = (bf16[32,1024]{1,0:T(8,128)(2,1)S(1)}, bf16[32,1024]{1,0:T(8,128)(2,1)S(1)}, u32[]{:S(2)}, u32[]{:S(2)}) collective-permute-start(bf16[32,1024]{1,0:T(8,128)(2,1)S(1)} %get-tuple-element.170), channel_id=1, source_target_pairs={{0,4},{1,5},{2,6},{3,7},{4,0},{5,1},{6,2},{7,3},{8,12},{9,13},{10,... | collective-permute-start | bytes 196616 | tf_op jit(solution)/shard_map/ppermute | solution.py:1015
  193.5 8.3 %collective-permute-start.54 = (bf16[32,1024]{1,0:T(8,128)(2,1)S(1)}, bf16[32,1024]{1,0:T(8,128)(2,1)S(1)}, u32[]{:S(2)}, u32[]{:S(2)}) collective-permute-start(bf16[32,1024]{1,0:T(8,128)(2,1)S(1)} %get-tuple-element.171), channel_id=1, source_target_pairs={{0,5},{1,4},{2,7},{3,6},{4,1},{5,0},{6,3},{7,2},{8,13},{9,12},{10,... | collective-permute-start | bytes 196616 | tf_op jit(solution)/shard_map/ppermute | solution.py:1015
  197.7 7.0 %collective-permute-start.55 = (bf16[32,1024]{1,0:T(8,128)(2,1)S(1)}, bf16[32,1024]{1,0:T(8,128)(2,1)S(1)}, u32[]{:S(2)}, u32[]{:S(2)}) collective-permute-start(bf16[32,1024]{1,0:T(8,128)(2,1)S(1)} %get-tuple-element.172), channel_id=1, source_target_pairs={{0,6},{1,7},{2,4},{3,5},{4,2},{5,3},{6,0},{7,1},{8,14},{9,15},{10,... | collective-permute-start | bytes 196616 | tf_op jit(solution)/shard_map/ppermute | solution.py:1015
  197.7 8.4 %collective-permute-start.56 = (bf16[32,1024]{1,0:T(8,128)(2,1)S(1)}, bf16[32,1024]{1,0:T(8,128)(2,1)S(1)}, u32[]{:S(2)}, u32[]{:S(2)}) collective-permute-start(bf16[32,1024]{1,0:T(8,128)(2,1)S(1)} %get-tuple-element.173), channel_id=1, source_target_pairs={{0,7},{1,6},{2,5},{3,4},{4,3},{5,2},{6,1},{7,0},{8,15},{9,14},{10,... | collective-permute-start | bytes 196616 | tf_op jit(solution)/shard_map/ppermute | solution.py:1015
  201.6 23.3 %collective-permute-start.23 = (bf16[128,1024]{1,0:T(8,128)(2,1)S(1)}, bf16[128,1024]{1,0:T(8,128)(2,1)S(1)}, u32[]{:S(2)}, u32[]{:S(2)}) collective-permute-start(bf16[128,1024]{1,0:T(8,128)(2,1)S(1)} %get-tuple-element.124), channel_id=1, source_target_pairs={{0,4},{1,5},{2,6},{3,7},{4,0},{5,1},{6,2},{7,3},{8,12},{9,13},{10,... | collective-permute-start | bytes 786440 | tf_op jit(solution)/shard_map/ppermute | solution.py:1015
  201.7 32.2 %collective-permute-start.22 = (bf16[128,1024]{1,0:T(8,128)(2,1)S(1)}, bf16[128,1024]{1,0:T(8,128)(2,1)S(1)}, u32[]{:S(2)}, u32[]{:S(2)}) collective-permute-start(bf16[128,1024]{1,0:T(8,128)(2,1)S(1)} %get-tuple-element.123), channel_id=1, source_target_pairs={{0,6},{1,7},{2,0},{3,1},{4,2},{5,3},{6,4},{7,5},{8,14},{9,15},{10,... | collective-permute-start | bytes 786440 | tf_op jit(solution)/shard_map/ppermute | solution.py:1015
  204.7 32.6 %collective-permute-start.33 = (bf16[128,1024]{1,0:T(8,128)(2,1)S(1)}, bf16[128,1024]{1,0:T(8,128)(2,1)S(1)}, u32[]{:S(2)}, u32[]{:S(2)}) collective-permute-start(bf16[128,1024]{1,0:T(8,128)(2,1)S(1)} %get-tuple-element.143), channel_id=1, source_target_pairs={{0,6},{1,7},{2,0},{3,1},{4,2},{5,3},{6,4},{7,5},{8,14},{9,15},{10,... | collective-permute-start | bytes 786440 | tf_op jit(solution)/shard_map/ppermute | solution.py:1015
  206.1 41.8 %collective-permute-start.34 = (bf16[128,1024]{1,0:T(8,128)(2,1)S(1)}, bf16[128,1024]{1,0:T(8,128)(2,1)S(1)}, u32[]{:S(2)}, u32[]{:S(2)}) collective-permute-start(bf16[128,1024]{1,0:T(8,128)(2,1)S(1)} %get-tuple-element.144), channel_id=1, source_target_pairs={{0,4},{1,5},{2,6},{3,7},{4,0},{5,1},{6,2},{7,3},{8,12},{9,13},{10,... | collective-permute-start | bytes 786440 | tf_op jit(solution)/shard_map/ppermute | solution.py:1015
  224.9 23.0 %collective-permute-start.35 = (bf16[128,1024]{1,0:T(8,128)(2,1)S(1)}, bf16[128,1024]{1,0:T(8,128)(2,1)S(1)}, u32[]{:S(2)}, u32[]{:S(2)}) collective-permute-start(bf16[128,1024]{1,0:T(8,128)(2,1)S(1)} %get-tuple-element.145), channel_id=1, source_target_pairs={{0,2},{1,3},{2,4},{3,5},{4,6},{5,7},{6,0},{7,1},{8,10},{9,11},{10,... | collective-permute-start | bytes 786440 | tf_op jit(solution)/shard_map/ppermute | solution.py:1015
  224.9 31.4 %collective-permute-start.42 = (bf16[32,512]{1,0:T(8,128)(2,1)S(1)}, bf16[32,512]{1,0:T(8,128)(2,1)S(1)}, u32[]{:S(2)}, u32[]{:S(2)}) collective-permute-start(bf16[32,512]{1,0:T(8,128)(2,1)S(1)} %get-tuple-element.158), channel_id=1, source_target_pairs={{0,3},{1,2},{2,1},{3,0},{4,7},{5,6},{6,5},{7,4},{8,11},{9,10},{10,... | collective-permute-start | bytes 98312 | tf_op jit(solution)/shard_map/ppermute | solution.py:1015
  233.9 22.4 %collective-permute-start.43 = (bf16[32,512]{1,0:T(8,128)(2,1)S(1)}, bf16[32,512]{1,0:T(8,128)(2,1)S(1)}, u32[]{:S(2)}, u32[]{:S(2)}) collective-permute-start(bf16[32,512]{1,0:T(8,128)(2,1)S(1)} %get-tuple-element.159), channel_id=1, source_target_pairs={{0,4},{1,5},{2,6},{3,7},{4,0},{5,1},{6,2},{7,3},{8,12},{9,13},{10,... | collective-permute-start | bytes 98312 | tf_op jit(solution)/shard_map/ppermute | solution.py:1015
  237.3 19.0 %collective-permute-start.44 = (bf16[32,512]{1,0:T(8,128)(2,1)S(1)}, bf16[32,512]{1,0:T(8,128)(2,1)S(1)}, u32[]{:S(2)}, u32[]{:S(2)}) collective-permute-start(bf16[32,512]{1,0:T(8,128)(2,1)S(1)} %get-tuple-element.160), channel_id=1, source_target_pairs={{0,5},{1,4},{2,7},{3,6},{4,1},{5,0},{6,3},{7,2},{8,13},{9,12},{10,... | collective-permute-start | bytes 98312 | tf_op jit(solution)/shard_map/ppermute | solution.py:1015
  247.9 8.5 %collective-permute-start.45 = (bf16[32,512]{1,0:T(8,128)(2,1)S(1)}, bf16[32,512]{1,0:T(8,128)(2,1)S(1)}, u32[]{:S(2)}, u32[]{:S(2)}) collective-permute-start(bf16[32,512]{1,0:T(8,128)(2,1)S(1)} %get-tuple-element.161), channel_id=1, source_target_pairs={{0,6},{1,7},{2,4},{3,5},{4,2},{5,3},{6,0},{7,1},{8,14},{9,15},{10,... | collective-permute-start | bytes 98312 | tf_op jit(solution)/shard_map/ppermute | solution.py:1015
  247.9 8.5 %collective-permute-start.46 = (bf16[32,512]{1,0:T(8,128)(2,1)S(1)}, bf16[32,512]{1,0:T(8,128)(2,1)S(1)}, u32[]{:S(2)}, u32[]{:S(2)}) collective-permute-start(bf16[32,512]{1,0:T(8,128)(2,1)S(1)} %get-tuple-element.162), channel_id=1, source_target_pairs={{0,7},{1,6},{2,5},{3,4},{4,3},{5,2},{6,1},{7,0},{8,15},{9,14},{10,... | collective-permute-start | bytes 98312 | tf_op jit(solution)/shard_map/ppermute | solution.py:1015
  (15 other events, 213.7 us)

commit v4 on v3

--- a/solution.py
+++ b/solution.py
@@ -152,6 +152,14 @@
         far_outs=[shape((share, padded(total) + SMALL + 2 * cut))] * count,
         room=0,
     )
+
+
+def stash_call(scalars, own, w_out):
+    def kernel(at, own_ref, w_out_ref, near_ref, near_out_ref):
+        near_ref[...] = own_ref[...]
+        near_out_ref[...] = w_out_ref[...]
+
+    return call(kernel, [shape(own.shape), shape(w_out.shape)], [], scalars, (own, w_out))
 
 
 def collect_call(scalars, pieces, w_out, wide):
@@ -883,7 +891,8 @@
     cut = double // 2
 
     def kernel(at, *refs):
-        far_refs, (one_ref, two_ref, got, sem) = refs[:ctxs], refs[ctxs:]
+        far_refs, (one_ref, two_ref, done_ref, got, sem) = refs[:ctxs], refs[ctxs:]
+        done_ref[...] = jnp.zeros_like(done_ref)
         wait_all(start_all([(ref, got.at[at_c(at, k)]) for k, ref in enumerate(far_refs)], sem))
         for ctx in range(ctxs):
             cols = slice(ctx * cut, (ctx + 1) * cut)
@@ -892,7 +901,7 @@
 
     return call(
         kernel,
-        [shape((share, ctxs * cut), f32)] * 2,
+        [shape((share, ctxs * cut), f32)] * 2 + [shape((1, 128), f32)],
         [pltpu.VMEM((ctxs, share, double), bf16), sems(ctxs)],
         scalars,
         (),
@@ -940,11 +949,31 @@
     )
 
 
+def emit_call(scalars, x, bias, keep, parts):
+    count = len(parts)
+
+    def kernel(at, x_ref, bias_ref, keep_ref, *refs):
+        far_refs, (out_ref, got, sem) = refs[:count], refs[count:]
+        wait_all(start_all([(ref, got.at[k]) for k, ref in enumerate(far_refs)], sem))
+        value = x_ref[...].astype(f32) + keep_ref[...] + bias_ref[...]
+        out_ref[...] = (value + sum(got[k].astype(f32) for k in range(count))).astype(bf16)
+
+    return call(
+        kernel,
+        [shape(x.shape)],
+        [pltpu.VMEM((count, *x.shape), bf16), sems(count)],
+        scalars,
+        (x, bias, keep),
+        far=parts,
+    )[0]
+
+
 def finish_call(scalars, x, dy, gain, keep, parts):
     count = len(parts)
 
     def kernel(at, x_ref, dy_ref, gain_ref, keep_ref, *refs):
-        far_refs, (out_ref, got, sem) = refs[:count], refs[count:]
+        far_refs, (out_ref, done_ref, got, sem) = refs[:count], refs[count:]
+        done_ref[...] = jnp.zeros_like(done_ref)
         copies = start_all([(ref, got.at[k]) for k, ref in enumerate(far_refs)], sem)
         here = x_ref[...].astype(f32)
         centred = here - jnp.mean(here, axis=1, keepdims=True)
@@ -961,13 +990,13 @@
 
     return call(
         kernel,
-        [shape(x.shape, f32)],
+        [shape(x.shape, f32), shape((1, 128), f32)],
         [pltpu.VMEM((count, *x.shape), bf16), sems(count)],
         scalars,
         (x, dy, gain, keep),
         far=parts,
         room=6,
-    )[0]
+    )
 
 
 def body(
@@ -1036,8 +1065,9 @@
         segments,
     )
     wide = padded(total) + SMALL
-    got = packed[:1] + along("ctx", packed[1:], hops_c)
-    joint, fc_here = collect_call(scalars, got, w_out, wide)
+    near, near_out = stash_call(scalars, packed[0], w_out)
+    got = [near] + along("ctx", packed[1:], hops_c)
+    joint, fc_here = collect_call(scalars, got, near_out, wide)
     joint = [joint] + along("seq", [joint] * (seqs - 1), hops_s)
     w_fc = [fc_here] + along("seq", [fc_here] * (seqs - 1), hops_s)
     x_all = spread_ctx(x_here)
@@ -1059,10 +1089,7 @@
     out_theirs = along("ctx", [out_theirs], [partner(1)])[0]
     out_keep, *out_sends = middle_call(scalars, piece, out_mine, out_theirs)
     out_parts = along("ctx", out_sends, hops_z)
-    block_out = x_here.astype(f32) + out_keep + bias_out
-    for part in out_parts:
-        block_out = block_out + part.astype(f32)
-    block_out = block_out.astype(bf16)
+    block_out = emit_call(scalars, x_here, bias_out, out_keep, out_parts)
 
     dy, dfc, dattn, sum_fc1 = backward_call(scalars, dy_all, w_fc_c, w_out_c, slope)
     grad_fc1 = rows_dot(h, dfc).astype(bf16)
@@ -1100,10 +1127,10 @@
     fc_home = fc_home[:1] + along("ctx", fc_home[1:], hops_c)
     out_wout, *qkv_home = sum_qkv_call(scalars, share, width, rows, qkv_parts)
     qkv_home = qkv_home[:1] + along("ctx", qkv_home[1:], hops_c)
-    grad_in = finish_call(scalars, x_here, dy_here, gain, dh_keep, dh_parts)
-    out_wfc1, out_wfc2 = home_fc_call(scalars, fc_home, (grad_in,))
+    grad_in, finished = finish_call(scalars, x_here, dy_here, gain, dh_keep, dh_parts)
+    out_wfc1, out_wfc2, finished = home_fc_call(scalars, fc_home, (finished,))
     out_wqkv, *small = home_qkv_call(
-        scalars, group, heads, lanes, width, qkv_home, (out_wfc1,)
+        scalars, group, heads, lanes, width, qkv_home, (finished,)
     )
     small = [value.reshape(-1) for value in small]
     return (

time: 259 us -> 258 us (level)
  waiting for transfers between devices: 80.9 us -> 93.3 us
  starting transfers between devices: 129 us -> 117 us
    ppermute x57, waiting for transfers between devices: 80.9 us -> 93.3 us  [along(): out.append(lax.ppermute(part, axis, pair))]
    ppermute x57, starting transfers between devices: 129 us -> 117 us  [along(): out.append(lax.ppermute(part, axis, pair))]
    pallas_call x18 -> x20, Pallas kernels: 38.5 us -> 39.6 us  [call(): pl.pallas_call(wrapped, in_specs=[vmem] * len(operands) + [hbm] * len(far...]
  transfers between devices with their start and end apart: 57 -> 57, of which waited for: 16 -> 16; matrix products, arithmetic and copies ran while one was open for 2% -> 2% of each run, Pallas kernels for 13% -> 14%
where the time goes in v4:
time: 258 us
  starting transfers between devices  117 us (45%)
  waiting for transfers between devices  93.3 us (36%)
  Pallas kernels  39.6 us (15%)
  matrix products  4.36 us (2%)
    ppermute x57, starting transfers between devices, along(): out.append(lax.ppermute(part, axis, pair))  117 us
    ppermute x57, waiting for transfers between devices, along(): out.append(lax.ppermute(part, axis, pair))  93.3 us
    pallas_call x20, Pallas kernels, call(): pl.pallas_call(wrapped, in_specs=[vmem] * len(operands) + [hbm] * len(far...  39.6 us
  transfers between devices with their start and end apart: 57, of which 16 were waited for; matrix products, arithmetic and copies ran while one was open for 2% of the time, Pallas kernels for 14%

profile of v4, /device:TPU:0, one launch (start us, length us, event | category | flops | bytes accessed | tf_op | source)
XLA Modules:
  0.0 257.5 jit_solution(14408837821069501742)
XLA Ops:
  0.7 2.3 shard_map.220
  3.6 2.6 %collective-permute-start.1 = (bf16[32,1536]{1,0:T(8,128)(2,1)}, bf16[32,1536]{1,0:T(8,128)(2,1)S(1)}, u32[]{:S(2)}, u32[]{:S(2)}) collective-permute-start(bf16[32,1536]{1,0:T(8,128)(2,1)} %get-tuple-element.106), channel_id=1, source_target_pairs={{0,2},{1,3},{2,0},{3,1},{4,6},{5,7},{6,4},{7,5},{8,10},{9,11},{10,... | collective-permute-start | bytes 294920 | tf_op jit(solution)/shard_map/ppermute | solution.py:1044
  6.3 2.8 %collective-permute-start.3 = (bf16[32,1536]{1,0:T(8,128)(2,1)}, bf16[32,1536]{1,0:T(8,128)(2,1)S(1)}, u32[]{:S(2)}, u32[]{:S(2)}) collective-permute-start(bf16[32,1536]{1,0:T(8,128)(2,1)} %get-tuple-element.108), channel_id=1, source_target_pairs={{0,4},{1,5},{2,6},{3,7},{4,0},{5,1},{6,2},{7,3},{8,12},{9,13},{10,... | collective-permute-start | bytes 294920 | tf_op jit(solution)/shard_map/ppermute | solution.py:1044
  9.0 3.6 %collective-permute-start.10 = (bf16[128,1024]{1,0:T(8,128)(2,1)}, bf16[128,1024]{1,0:T(8,128)(2,1)S(1)}, u32[]{:S(2)}, u32[]{:S(2)}) collective-permute-start(bf16[128,1024]{1,0:T(8,128)(2,1)} %bitcast.25), channel_id=1, source_target_pairs={{0,6},{1,7},{2,0},{3,1},{4,2},{5,3},{6,4},{7,5},{8,14},{9,15},{10,... | collective-permute-start | bytes 786440 | tf_op jit(solution)/shard_map/ppermute | solution.py:1044
  12.6 1.5 collective-permute-start.5
  14.9 2.0 collective-permute-start.6
  17.3 2.0 collective-permute-done.4.refs_5_
  19.3 17.8 %collective-permute-start.12 = (bf16[128,1024]{1,0:T(8,128)(2,1)}, bf16[128,1024]{1,0:T(8,128)(2,1)S(1)}, u32[]{:S(2)}, u32[]{:S(2)}) collective-permute-start(bf16[128,1024]{1,0:T(8,128)(2,1)} %bitcast.27), channel_id=1, source_target_pairs={{0,2},{1,3},{2,4},{3,5},{4,6},{5,7},{6,0},{7,1},{8,10},{9,11},{10,... | collective-permute-start | bytes 786440 | tf_op jit(solution)/shard_map/ppermute | solution.py:1044
  37.0 1.4 collective-permute-start.25
  40.7 2.5 collective-permute-start.7
  43.2 7.5 %collective-permute-done.11.refs_8_ = bf16[128,1024]{1,0:T(8,128)(2,1)S(1)} collective-permute-done((bf16[128,1024]{1,0:T(8,128)(2,1)}, bf16[128,1024]{1,0:T(8,128)(2,1)S(1)}, u32[]{:S(2)}, u32[]{:S(2)}) %collective-permute-start.11) | collective-permute-done | bytes 262176 | tf_op jit(solution)/shard_map/ppermute | solution.py:1044
  50.6 11.9 %collective-permute-start.27 = (bf16[128,1024]{1,0:T(8,128)(2,1)}, bf16[128,1024]{1,0:T(8,128)(2,1)S(1)}, u32[]{:S(2)}, u32[]{:S(2)}) collective-permute-start(bf16[128,1024]{1,0:T(8,128)(2,1)} %bitcast.20), channel_id=1, source_target_pairs={{0,2},{1,3},{2,4},{3,5},{4,6},{5,7},{6,0},{7,1},{8,10},{9,11},{10,... | collective-permute-start | bytes 786440 | tf_op jit(solution)/shard_map/ppermute | solution.py:1044
  62.6 1.5 collective-permute-start.8
  64.1 1.5 collective-permute-start.9
  65.6 7.2 %collective-permute-done.26.refs_5_ = bf16[128,1024]{1,0:T(8,128)(2,1)S(1)} collective-permute-done((bf16[128,1024]{1,0:T(8,128)(2,1)}, bf16[128,1024]{1,0:T(8,128)(2,1)S(1)}, u32[]{:S(2)}, u32[]{:S(2)}) %collective-permute-start.26) | collective-permute-done | bytes 262176 | tf_op jit(solution)/shard_map/ppermute | solution.py:1044
  72.8 2.4 collective-permute-start.17
  75.8 2.0 collective-permute-done.8.refs_2_.refs_16_
  80.9 6.8 %collective-permute-done.17.refs_4_ = bf16[256,1024]{1,0:T(8,128)(2,1)S(1)} collective-permute-done((bf16[256,1024]{1,0:T(8,128)(2,1)S(1)}, bf16[256,1024]{1,0:T(8,128)(2,1)S(1)}, u32[]{:S(2)}, u32[]{:S(2)}) %collective-permute-start.17) | collective-permute-done | bytes 524320 | tf_op jit(solution)/shard_map/ppermute | solution.py:1044
  87.7 12.9 %collective-permute-done.18.refs_5_ = bf16[256,1024]{1,0:T(8,128)(2,1)S(1)} collective-permute-done((bf16[256,1024]{1,0:T(8,128)(2,1)S(1)}, bf16[256,1024]{1,0:T(8,128)(2,1)S(1)}, u32[]{:S(2)}, u32[]{:S(2)}) %collective-permute-start.18) | collective-permute-done | bytes 524320 | tf_op jit(solution)/shard_map/ppermute | solution.py:1044
  100.6 7.3 %shard_map.225 = (bf16[1024,1024]{1,0:T(8,128)(2,1)S(1)}, bf16[1024,1024]{1,0:T(8,128)(2,1)S(1)}, bf16[1024,128]{1,0:T(8,128)(2,1)S(1)}, f32[2,1024]{1,0:T(2,128...) custom-call(f32[1,1024]{1,0:T(1,128)S(1)} %get-tuple-element.115.refs_0_.refs_2_,, ...), custom_call_target="tpu_custom_call" | custom-call | flops 1610612736 | bytes 3584000 | tf_op jit(solution)/shard_map/pallas_call | solution.py:58
  107.9 5.6 %shard_map.226 = (bf16[1024,1024]{1,0:T(8,128)(2,1)S(1)}, bf16[1024,512]{1,0:T(8,128)(2,1)S(1)}, bf16[1024,512]{1,0:T(8,128)(2,1)S(1)}, bf16[512,1024]{1,0:T(8,1...) custom-call(bf16[1024,1024]{1,0:T(8,128)(2,1)S(1)} %get-tuple-element.121.refs_0_, ...), custom_call_target="tpu_custom_call" | custom-call | flops 2147483648 | bytes 4734976 | tf_op jit(solution)/shard_map/pallas_call | solution.py:58
  114.1 2.7 %shard_map.229 = (bf16[1024,1024]{1,0:T(8,128)(2,1)S(1)}, bf16[1024,512]{1,0:T(8,128)(2,1)S(1)}, bf16[1024,128]{1,0:T(8,128)(2,1)S(1)}, f32[1,512]{1,0:T(1,128)S(1)}) custom-call(bf16[1024,1024]{1,0:T(8,128)(2,1)S(1)} %get-tuple-element.133.refs_0_.refs_1_, bf16[128,1024]{1,0:T(8,128)(2,1)S(1)} %get-tuple-element.134.refs_1_, ...), custom_call_target="tpu_custom_call" | custom-call | flops 1073741824 | bytes 5505024 | tf_op jit(solution)/shard_map/pallas_call | solution.py:58
  116.8 1.3 convolution_convert_fusion.1.refs_0_
  118.1 1.3 convolution_convert_fusion.refs_1_
  120.6 5.7 %shard_map.231 = (bf16[1024,384]{1,0:T(8,128)(2,1)S(1)}, f32[1,384]{1,0:T(1,128)S(1)}) custom-call(bf16[1024,384]{1,0:T(8,128)(2,1)S(1)} %get-tuple-element.137.refs_0_, bf16[256,1024]{1,0:T(8,128)(2,1)S(1)} %get-tuple-element.138.refs_1_, bf16[1024,128]{1,0:T(8,128)(2,1)S(1)} %get-tuple-element.139.refs_2_, f32[2,1024]{1,0:T(2,128)S(1)} %get-tuple-element.140.refs_3_, ...), custom_call_target="tpu_custom_call" | custom-call | flops 1342177280 | bytes 1703936 | tf_op jit(solution)/shard_map/pallas_call | solution.py:58
  126.3 3.3 %shard_map.232 = (bf16[512,1024]{1,0:T(8,128)(2,1)S(1)}, f32[1,1024]{1,0:T(1,128)S(1)}, f32[1,1024]{1,0:T(1,128)S(1)}, bf16[512,1024]{1,0:T(8,128)(2,1)S(1)}) custom-call(bf16[1024,512]{1,0:T(8,128)(2,1)S(1)} %get-tuple-element.136.refs_0_, bf16[1024,1024]{1,0:T(8,128)(2,1)S(1)} %get-tuple-element.133.refs_0_.refs_1_, ...), custom_call_target="tpu_custom_call" | custom-call | flops 1073741824 | bytes 6815744 | tf_op jit(solution)/shard_map/pallas_call | solution.py:58
  130.2 1.3 convolution_convert_fusion.2.refs_0_
  134.8 2.2 collective-permute-start.47
  137.0 7.1 %collective-permute-done.37.refs_1_ = bf16[320,512]{1,0:T(8,128)(2,1)S(1)} collective-permute-done((bf16[320,512]{1,0:T(8,128)(2,1)S(1)}, bf16[320,512]{1,0:T(8,128)(2,1)S(1)}, u32[]{:S(2)}, u32[]{:S(2)}) %collective-permute-start.37) | collective-permute-done | bytes 327712 | tf_op jit(solution)/shard_map/ppermute | solution.py:1044
  145.3 17.2 %collective-permute-start.49 = (bf16[256,1024]{1,0:T(8,128)(2,1)S(1)}, bf16[256,1024]{1,0:T(8,128)(2,1)S(1)}, u32[]{:S(2)}, u32[]{:S(2)}) collective-permute-start(bf16[256,1024]{1,0:T(8,128)(2,1)S(1)} %get-tuple-element.173), channel_id=1, source_target_pairs={{0,8},{8,16},{16,24},{24,0},{1,9},{9,17},{17,25},{25,1},{2,10},{10... | collective-permute-start | bytes 1572872 | tf_op jit(solution)/shard_map/ppermute | solution.py:1044
  163.1 19.0 %collective-permute-done.39.refs_3_ = bf16[320,512]{1,0:T(8,128)(2,1)S(1)} collective-permute-done((bf16[320,512]{1,0:T(8,128)(2,1)S(1)}, bf16[320,512]{1,0:T(8,128)(2,1)S(1)}, u32[]{:S(2)}, u32[]{:S(2)}) %collective-permute-start.39) | collective-permute-done | bytes 327712 | tf_op jit(solution)/shard_map/ppermute | solution.py:1044
  182.1 2.6 collective-permute-start.22
  184.6 1.9 shard_map.236
  186.7 1.3 shard_map.237
  188.4 1.7 collective-permute-start.51
  191.0 3.9 %collective-permute-start.53 = (bf16[32,1024]{1,0:T(8,128)(2,1)S(1)}, bf16[32,1024]{1,0:T(8,128)(2,1)S(1)}, u32[]{:S(2)}, u32[]{:S(2)}) collective-permute-start(bf16[32,1024]{1,0:T(8,128)(2,1)S(1)} %get-tuple-element.178), channel_id=1, source_target_pairs={{0,4},{1,5},{2,6},{3,7},{4,0},{5,1},{6,2},{7,3},{8,12},{9,13},{10,... | collective-permute-start | bytes 196616 | tf_op jit(solution)/shard_map/ppermute | solution.py:1044
  195.3 5.1 %collective-permute-start.55 = (bf16[32,1024]{1,0:T(8,128)(2,1)S(1)}, bf16[32,1024]{1,0:T(8,128)(2,1)S(1)}, u32[]{:S(2)}, u32[]{:S(2)}) collective-permute-start(bf16[32,1024]{1,0:T(8,128)(2,1)S(1)} %get-tuple-element.180), channel_id=1, source_target_pairs={{0,6},{1,7},{2,4},{3,5},{4,2},{5,3},{6,0},{7,1},{8,14},{9,15},{10,... | collective-permute-start | bytes 196616 | tf_op jit(solution)/shard_map/ppermute | solution.py:1044
  200.9 2.5 collective-permute-done.54.refs_5_
  203.5 1.5 collective-permute-start.24
  204.9 2.4 collective-permute-start.33
  207.3 11.0 %collective-permute-start.34 = (bf16[128,1024]{1,0:T(8,128)(2,1)S(1)}, bf16[128,1024]{1,0:T(8,128)(2,1)S(1)}, u32[]{:S(2)}, u32[]{:S(2)}) collective-permute-start(bf16[128,1024]{1,0:T(8,128)(2,1)S(1)} %get-tuple-element.151), channel_id=1, source_target_pairs={{0,4},{1,5},{2,6},{3,7},{4,0},{5,1},{6,2},{7,3},{8,12},{9,13},{10,... | collective-permute-start | bytes 786440 | tf_op jit(solution)/shard_map/ppermute | solution.py:1044
  219.5 16.3 %collective-permute-done.23.refs_4_ = bf16[128,1024]{1,0:T(8,128)(2,1)S(1)} collective-permute-done((bf16[128,1024]{1,0:T(8,128)(2,1)S(1)}, bf16[128,1024]{1,0:T(8,128)(2,1)S(1)}, u32[]{:S(2)}, u32[]{:S(2)}) %collective-permute-start.23) | collective-permute-done | bytes 262176 | tf_op jit(solution)/shard_map/ppermute | solution.py:1044
  236.9 4.4 %collective-permute-start.44 = (bf16[32,512]{1,0:T(8,128)(2,1)S(1)}, bf16[32,512]{1,0:T(8,128)(2,1)S(1)}, u32[]{:S(2)}, u32[]{:S(2)}) collective-permute-start(bf16[32,512]{1,0:T(8,128)(2,1)S(1)} %get-tuple-element.168), channel_id=1, source_target_pairs={{0,5},{1,4},{2,7},{3,6},{4,1},{5,0},{6,3},{7,2},{8,13},{9,12},{10,... | collective-permute-start | bytes 98312 | tf_op jit(solution)/shard_map/ppermute | solution.py:1044
  241.4 7.0 %collective-permute-done.34.refs_5_ = bf16[128,1024]{1,0:T(8,128)(2,1)S(1)} collective-permute-done((bf16[128,1024]{1,0:T(8,128)(2,1)S(1)}, bf16[128,1024]{1,0:T(8,128)(2,1)S(1)}, u32[]{:S(2)}, u32[]{:S(2)}) %collective-permute-start.34) | collective-permute-done | bytes 262176 | tf_op jit(solution)/shard_map/ppermute | solution.py:1044
  248.4 3.3 %collective-permute-start.46 = (bf16[32,512]{1,0:T(8,128)(2,1)S(1)}, bf16[32,512]{1,0:T(8,128)(2,1)S(1)}, u32[]{:S(2)}, u32[]{:S(2)}) collective-permute-start(bf16[32,512]{1,0:T(8,128)(2,1)S(1)} %get-tuple-element.170), channel_id=1, source_target_pairs={{0,7},{1,6},{2,5},{3,4},{4,3},{5,2},{6,1},{7,0},{8,15},{9,14},{10,... | collective-permute-start | bytes 98312 | tf_op jit(solution)/shard_map/ppermute | solution.py:1044
  251.7 1.4 shard_map.234
  254.1 1.8 shard_map.238
  256.0 1.3 shard_map.239
  (98 shorter events, 20.6 us)
Async XLA Ops:
  3.0 6.0 %collective-permute-start = (bf16[32,1536]{1,0:T(8,128)(2,1)}, bf16[32,1536]{1,0:T(8,128)(2,1)S(1)}, u32[]{:S(2)}, u32[]{:S(2)}) collective-permute-start(bf16[32,1536]{1,0:T(8,128)(2,1)} %get-tuple-element.105), channel_id=1, source_target_pairs={{0,1},{1,0},{2,3},{3,2},{4,5},{5,4},{6,7},{7,6},{8,9},{9,8},{10,11... | collective-permute-start | bytes 294920 | tf_op jit(solution)/shard_map/ppermute | solution.py:1044
  3.6 9.1 %collective-permute-start.1 = (bf16[32,1536]{1,0:T(8,128)(2,1)}, bf16[32,1536]{1,0:T(8,128)(2,1)S(1)}, u32[]{:S(2)}, u32[]{:S(2)}) collective-permute-start(bf16[32,1536]{1,0:T(8,128)(2,1)} %get-tuple-element.106), channel_id=1, source_target_pairs={{0,2},{1,3},{2,0},{3,1},{4,6},{5,7},{6,4},{7,5},{8,10},{9,11},{10,... | collective-permute-start | bytes 294920 | tf_op jit(solution)/shard_map/ppermute | solution.py:1044
  6.2 8.7 %collective-permute-start.2 = (bf16[32,1536]{1,0:T(8,128)(2,1)}, bf16[32,1536]{1,0:T(8,128)(2,1)S(1)}, u32[]{:S(2)}, u32[]{:S(2)}) collective-permute-start(bf16[32,1536]{1,0:T(8,128)(2,1)} %get-tuple-element.107), channel_id=1, source_target_pairs={{0,3},{1,2},{2,1},{3,0},{4,7},{5,6},{6,5},{7,4},{8,11},{9,10},{10,... | collective-permute-start | bytes 294920 | tf_op jit(solution)/shard_map/ppermute | solution.py:1044
  6.3 10.6 %collective-permute-start.3 = (bf16[32,1536]{1,0:T(8,128)(2,1)}, bf16[32,1536]{1,0:T(8,128)(2,1)S(1)}, u32[]{:S(2)}, u32[]{:S(2)}) collective-permute-start(bf16[32,1536]{1,0:T(8,128)(2,1)} %get-tuple-element.108), channel_id=1, source_target_pairs={{0,4},{1,5},{2,6},{3,7},{4,0},{5,1},{6,2},{7,3},{8,12},{9,13},{10,... | collective-permute-start | bytes 294920 | tf_op jit(solution)/shard_map/ppermute | solution.py:1044
  9.0 10.3 %collective-permute-start.4 = (bf16[32,1536]{1,0:T(8,128)(2,1)}, bf16[32,1536]{1,0:T(8,128)(2,1)S(1)}, u32[]{:S(2)}, u32[]{:S(2)}) collective-permute-start(bf16[32,1536]{1,0:T(8,128)(2,1)} %get-tuple-element.109), channel_id=1, source_target_pairs={{0,5},{1,4},{2,7},{3,6},{4,1},{5,0},{6,3},{7,2},{8,13},{9,12},{10,... | collective-permute-start | bytes 294920 | tf_op jit(solution)/shard_map/ppermute | solution.py:1044
  9.0 31.6 %collective-permute-start.10 = (bf16[128,1024]{1,0:T(8,128)(2,1)}, bf16[128,1024]{1,0:T(8,128)(2,1)S(1)}, u32[]{:S(2)}, u32[]{:S(2)}) collective-permute-start(bf16[128,1024]{1,0:T(8,128)(2,1)} %bitcast.25), channel_id=1, source_target_pairs={{0,6},{1,7},{2,0},{3,1},{4,2},{5,3},{6,4},{7,5},{8,14},{9,15},{10,... | collective-permute-start | bytes 786440 | tf_op jit(solution)/shard_map/ppermute | solution.py:1044
  12.6 24.4 %collective-permute-start.5 = (bf16[32,1536]{1,0:T(8,128)(2,1)}, bf16[32,1536]{1,0:T(8,128)(2,1)S(1)}, u32[]{:S(2)}, u32[]{:S(2)}) collective-permute-start(bf16[32,1536]{1,0:T(8,128)(2,1)} %get-tuple-element.110), channel_id=1, source_target_pairs={{0,6},{1,7},{2,4},{3,5},{4,2},{5,3},{6,0},{7,1},{8,14},{9,15},{10,... | collective-permute-start | bytes 294920 | tf_op jit(solution)/shard_map/ppermute | solution.py:1044
  14.9 22.2 %collective-permute-start.6 = (bf16[32,1536]{1,0:T(8,128)(2,1)}, bf16[32,1536]{1,0:T(8,128)(2,1)S(1)}, u32[]{:S(2)}, u32[]{:S(2)}) collective-permute-start(bf16[32,1536]{1,0:T(8,128)(2,1)} %get-tuple-element.111), channel_id=1, source_target_pairs={{0,7},{1,6},{2,5},{3,4},{4,3},{5,2},{6,1},{7,0},{8,15},{9,14},{10,... | collective-permute-start | bytes 294920 | tf_op jit(solution)/shard_map/ppermute | solution.py:1044
  16.9 33.7 %collective-permute-start.11 = (bf16[128,1024]{1,0:T(8,128)(2,1)}, bf16[128,1024]{1,0:T(8,128)(2,1)S(1)}, u32[]{:S(2)}, u32[]{:S(2)}) collective-permute-start(bf16[128,1024]{1,0:T(8,128)(2,1)} %bitcast.26), channel_id=1, source_target_pairs={{0,4},{1,5},{2,6},{3,7},{4,0},{5,1},{6,2},{7,3},{8,12},{9,13},{10,... | collective-permute-start | bytes 786440 | tf_op jit(solution)/shard_map/ppermute | solution.py:1044
  19.3 31.4 %collective-permute-start.12 = (bf16[128,1024]{1,0:T(8,128)(2,1)}, bf16[128,1024]{1,0:T(8,128)(2,1)S(1)}, u32[]{:S(2)}, u32[]{:S(2)}) collective-permute-start(bf16[128,1024]{1,0:T(8,128)(2,1)} %bitcast.27), channel_id=1, source_target_pairs={{0,2},{1,3},{2,4},{3,5},{4,6},{5,7},{6,0},{7,1},{8,10},{9,11},{10,... | collective-permute-start | bytes 786440 | tf_op jit(solution)/shard_map/ppermute | solution.py:1044
  37.0 25.6 %collective-permute-start.13 = (bf16[128,1024]{1,0:T(8,128)(2,1)}, bf16[128,1024]{1,0:T(8,128)(2,1)S(1)}, u32[]{:S(2)}, u32[]{:S(2)}) collective-permute-start(bf16[128,1024]{1,0:T(8,128)(2,1)} %bitcast.28), channel_id=1, source_target_pairs={{0,1},{1,0},{2,3},{3,2},{4,5},{5,4},{6,7},{7,6},{8,9},{9,8},{10,11... | collective-permute-start | bytes 786440 | tf_op jit(solution)/shard_map/ppermute | solution.py:1044
  37.0 27.1 %collective-permute-start.25 = (bf16[128,1024]{1,0:T(8,128)(2,1)}, bf16[128,1024]{1,0:T(8,128)(2,1)S(1)}, u32[]{:S(2)}, u32[]{:S(2)}) collective-permute-start(bf16[128,1024]{1,0:T(8,128)(2,1)} %bitcast.18), channel_id=1, source_target_pairs={{0,6},{1,7},{2,0},{3,1},{4,2},{5,3},{6,4},{7,5},{8,14},{9,15},{10,... | collective-permute-start | bytes 786440 | tf_op jit(solution)/shard_map/ppermute | solution.py:1044
  40.7 34.6 %collective-permute-start.7 = (bf16[320,512]{1,0:T(8,128)(2,1)S(1)}, bf16[320,512]{1,0:T(8,128)(2,1)S(1)}, u32[]{:S(2)}, u32[]{:S(2)}) collective-permute-start(bf16[320,512]{1,0:T(8,128)(2,1)S(1)} %get-tuple-element.113.refs_0_.refs_14_), channel_id=1, source_target_pairs={{0,24},{8,0},{16,8},{24,16},{1,25},{9,1},{17,9},{25,17},{2,26},{10... | collective-permute-start | bytes 983048 | tf_op jit(solution)/shard_map/ppermute | solution.py:1044
  50.6 22.2 %collective-permute-start.26 = (bf16[128,1024]{1,0:T(8,128)(2,1)}, bf16[128,1024]{1,0:T(8,128)(2,1)S(1)}, u32[]{:S(2)}, u32[]{:S(2)}) collective-permute-start(bf16[128,1024]{1,0:T(8,128)(2,1)} %bitcast.19), channel_id=1, source_target_pairs={{0,4},{1,5},{2,6},{3,7},{4,0},{5,1},{6,2},{7,3},{8,12},{9,13},{10,... | collective-permute-start | bytes 786440 | tf_op jit(solution)/shard_map/ppermute | solution.py:1044
  50.6 22.2 %collective-permute-start.27 = (bf16[128,1024]{1,0:T(8,128)(2,1)}, bf16[128,1024]{1,0:T(8,128)(2,1)S(1)}, u32[]{:S(2)}, u32[]{:S(2)}) collective-permute-start(bf16[128,1024]{1,0:T(8,128)(2,1)} %bitcast.20), channel_id=1, source_target_pairs={{0,2},{1,3},{2,4},{3,5},{4,6},{5,7},{6,0},{7,1},{8,10},{9,11},{10,... | collective-permute-start | bytes 786440 | tf_op jit(solution)/shard_map/ppermute | solution.py:1044
  62.6 15.3 %collective-permute-start.8 = (bf16[320,512]{1,0:T(8,128)(2,1)S(1)}, bf16[320,512]{1,0:T(8,128)(2,1)S(1)}, u32[]{:S(2)}, u32[]{:S(2)}) collective-permute-start(bf16[320,512]{1,0:T(8,128)(2,1)S(1)} %get-tuple-element.113.refs_0_.refs_14_), channel_id=1, source_target_pairs={{0,16},{8,24},{16,0},{24,8},{1,17},{9,25},{17,1},{25,9},{2,18},{10... | collective-permute-start | bytes 983048 | tf_op jit(solution)/shard_map/ppermute | solution.py:1044
  64.1 13.7 %collective-permute-start.9 = (bf16[320,512]{1,0:T(8,128)(2,1)S(1)}, bf16[320,512]{1,0:T(8,128)(2,1)S(1)}, u32[]{:S(2)}, u32[]{:S(2)}) collective-permute-start(bf16[320,512]{1,0:T(8,128)(2,1)S(1)} %get-tuple-element.113.refs_0_.refs_14_), channel_id=1, source_target_pairs={{0,8},{8,16},{16,24},{24,0},{1,9},{9,17},{17,25},{25,1},{2,10},{10... | collective-permute-start | bytes 983048 | tf_op jit(solution)/shard_map/ppermute | solution.py:1044
  72.8 14.8 %collective-permute-start.17 = (bf16[256,1024]{1,0:T(8,128)(2,1)S(1)}, bf16[256,1024]{1,0:T(8,128)(2,1)S(1)}, u32[]{:S(2)}, u32[]{:S(2)}) collective-permute-start(bf16[256,1024]{1,0:T(8,128)(2,1)S(1)} %get-tuple-element.124.refs_3_), channel_id=1, source_target_pairs={{0,24},{8,0},{16,8},{24,16},{1,25},{9,1},{17,9},{25,17},{2,26},{10... | collective-permute-start | bytes 1572872 | tf_op jit(solution)/shard_map/ppermute | solution.py:1044
  75.3 25.3 %collective-permute-start.18 = (bf16[256,1024]{1,0:T(8,128)(2,1)S(1)}, bf16[256,1024]{1,0:T(8,128)(2,1)S(1)}, u32[]{:S(2)}, u32[]{:S(2)}) collective-permute-start(bf16[256,1024]{1,0:T(8,128)(2,1)S(1)} %get-tuple-element.124.refs_3_), channel_id=1, source_target_pairs={{0,16},{8,24},{16,0},{24,8},{1,17},{9,25},{17,1},{25,9},{2,18},{10... | collective-permute-start | bytes 1572872 | tf_op jit(solution)/shard_map/ppermute | solution.py:1044
  77.8 30.0 %collective-permute-start.19 = (bf16[256,1024]{1,0:T(8,128)(2,1)S(1)}, bf16[256,1024]{1,0:T(8,128)(2,1)S(1)}, u32[]{:S(2)}, u32[]{:S(2)}) collective-permute-start(bf16[256,1024]{1,0:T(8,128)(2,1)S(1)} %get-tuple-element.124.refs_3_), channel_id=1, source_target_pairs={{0,8},{8,16},{16,24},{24,0},{1,9},{9,17},{17,25},{25,1},{2,10},{10... | collective-permute-start | bytes 1572872 | tf_op jit(solution)/shard_map/ppermute | solution.py:1044
  79.9 34.2 %collective-permute-start.28 = (bf16[128,1024]{1,0:T(8,128)(2,1)S(1)}, bf16[128,1024]{1,0:T(8,128)(2,1)S(1)}, u32[]{:S(2)}, u32[]{:S(2)}) collective-permute-start(bf16[128,1024]{1,0:T(8,128)(2,1)S(1)} %bitcast.21), channel_id=1, source_target_pairs={{0,1},{1,0},{2,3},{3,2},{4,5},{5,4},{6,7},{7,6},{8,9},{9,8},{10,11... | collective-permute-start | bytes 786440 | tf_op jit(solution)/shard_map/ppermute | solution.py:1044
  80.7 33.3 %collective-permute-start.29 = (bf16[128,1024]{1,0:T(8,128)(2,1)S(1)}, bf16[128,1024]{1,0:T(8,128)(2,1)S(1)}, u32[]{:S(2)}, u32[]{:S(2)}) collective-permute-start(bf16[128,1024]{1,0:T(8,128)(2,1)S(1)} %collective-permute-done.25.refs_4_), channel_id=1, source_target_pairs={{0,1},{1,0},{2,3},{3,2},{4,5},{5,4},{6,7},{7,6},{8,9},{9,8},{10,11... | collective-permute-start | bytes 786440 | tf_op jit(solution)/shard_map/ppermute | solution.py:1044
  87.7 26.4 %collective-permute-start.30 = (bf16[128,1024]{1,0:T(8,128)(2,1)S(1)}, bf16[128,1024]{1,0:T(8,128)(2,1)S(1)}, u32[]{:S(2)}, u32[]{:S(2)}) collective-permute-start(bf16[128,1024]{1,0:T(8,128)(2,1)S(1)} %collective-permute-done.26.refs_5_), channel_id=1, source_target_pairs={{0,1},{1,0},{2,3},{3,2},{4,5},{5,4},{6,7},{7,6},{8,9},{9,8},{10,11... | collective-permute-start | bytes 786440 | tf_op jit(solution)/shard_map/ppermute | solution.py:1044
  100.6 13.5 %collective-permute-start.31 = (bf16[128,1024]{1,0:T(8,128)(2,1)S(1)}, bf16[128,1024]{1,0:T(8,128)(2,1)S(1)}, u32[]{:S(2)}, u32[]{:S(2)}) collective-permute-start(bf16[128,1024]{1,0:T(8,128)(2,1)S(1)} %collective-permute-done.27.refs_6_), channel_id=1, source_target_pairs={{0,1},{1,0},{2,3},{3,2},{4,5},{5,4},{6,7},{7,6},{8,9},{9,8},{10,11... | collective-permute-start | bytes 786440 | tf_op jit(solution)/shard_map/ppermute | solution.py:1044
  113.5 49.1 %collective-permute-start.21 = (bf16[512,1024]{1,0:T(8,128)(2,1)S(1)}, bf16[512,1024]{1,0:T(8,128)(2,1)S(1)}, u32[]{:S(2)}, u32[]{:S(2)}) collective-permute-start(bf16[512,1024]{1,0:T(8,128)(2,1)S(1)} %get-tuple-element.128), channel_id=1, source_target_pairs={{0,1},{1,0},{2,3},{3,2},{4,5},{5,4},{6,7},{7,6},{8,9},{9,8},{10,11... | collective-permute-start | bytes 3145736 | tf_op jit(solution)/shard_map/ppermute | solution.py:1044
  129.6 70.8 %collective-permute-start.32 = (bf16[512,1024]{1,0:T(8,128)(2,1)S(1)}, bf16[512,1024]{1,0:T(8,128)(2,1)S(1)}, u32[]{:S(2)}, u32[]{:S(2)}) collective-permute-start(bf16[512,1024]{1,0:T(8,128)(2,1)S(1)} %get-tuple-element.148), channel_id=1, source_target_pairs={{0,1},{1,0},{2,3},{3,2},{4,5},{5,4},{6,7},{7,6},{8,9},{9,8},{10,11... | collective-permute-start | bytes 3145736 | tf_op jit(solution)/shard_map/ppermute | solution.py:1044
  133.5 10.6 %collective-permute-start.37 = (bf16[320,512]{1,0:T(8,128)(2,1)S(1)}, bf16[320,512]{1,0:T(8,128)(2,1)S(1)}, u32[]{:S(2)}, u32[]{:S(2)}) collective-permute-start(bf16[320,512]{1,0:T(8,128)(2,1)S(1)} %get-tuple-element.160), channel_id=1, source_target_pairs={{0,24},{8,0},{16,8},{24,16},{1,25},{9,1},{17,9},{25,17},{2,26},{10... | collective-permute-start | bytes 983048 | tf_op jit(solution)/shard_map/ppermute | solution.py:1044
  134.1 11.3 %collective-permute-start.38 = (bf16[320,512]{1,0:T(8,128)(2,1)S(1)}, bf16[320,512]{1,0:T(8,128)(2,1)S(1)}, u32[]{:S(2)}, u32[]{:S(2)}) collective-permute-start(bf16[320,512]{1,0:T(8,128)(2,1)S(1)} %get-tuple-element.161), channel_id=1, source_target_pairs={{0,16},{8,24},{16,0},{24,8},{1,17},{9,25},{17,1},{25,9},{2,18},{10... | collective-permute-start | bytes 983048 | tf_op jit(solution)/shard_map/ppermute | solution.py:1044
  134.8 51.7 %collective-permute-start.47 = (bf16[256,1024]{1,0:T(8,128)(2,1)S(1)}, bf16[256,1024]{1,0:T(8,128)(2,1)S(1)}, u32[]{:S(2)}, u32[]{:S(2)}) collective-permute-start(bf16[256,1024]{1,0:T(8,128)(2,1)S(1)} %get-tuple-element.171), channel_id=1, source_target_pairs={{0,24},{8,0},{16,8},{24,16},{1,25},{9,1},{17,9},{25,17},{2,26},{10... | collective-permute-start | bytes 1572872 | tf_op jit(solution)/shard_map/ppermute | solution.py:1044
  144.1 42.5 %collective-permute-start.48 = (bf16[256,1024]{1,0:T(8,128)(2,1)S(1)}, bf16[256,1024]{1,0:T(8,128)(2,1)S(1)}, u32[]{:S(2)}, u32[]{:S(2)}) collective-permute-start(bf16[256,1024]{1,0:T(8,128)(2,1)S(1)} %get-tuple-element.172), channel_id=1, source_target_pairs={{0,16},{8,24},{16,0},{24,8},{1,17},{9,25},{17,1},{25,9},{2,18},{10... | collective-permute-start | bytes 1572872 | tf_op jit(solution)/shard_map/ppermute | solution.py:1044
  145.3 41.4 %collective-permute-start.49 = (bf16[256,1024]{1,0:T(8,128)(2,1)S(1)}, bf16[256,1024]{1,0:T(8,128)(2,1)S(1)}, u32[]{:S(2)}, u32[]{:S(2)}) collective-permute-start(bf16[256,1024]{1,0:T(8,128)(2,1)S(1)} %get-tuple-element.173), channel_id=1, source_target_pairs={{0,8},{8,16},{16,24},{24,0},{1,9},{9,17},{17,25},{25,1},{2,10},{10... | collective-permute-start | bytes 1572872 | tf_op jit(solution)/shard_map/ppermute | solution.py:1044
  162.6 19.5 %collective-permute-start.39 = (bf16[320,512]{1,0:T(8,128)(2,1)S(1)}, bf16[320,512]{1,0:T(8,128)(2,1)S(1)}, u32[]{:S(2)}, u32[]{:S(2)}) collective-permute-start(bf16[320,512]{1,0:T(8,128)(2,1)S(1)} %get-tuple-element.162), channel_id=1, source_target_pairs={{0,8},{8,16},{16,24},{24,0},{1,9},{9,17},{17,25},{25,1},{2,10},{10... | collective-permute-start | bytes 983048 | tf_op jit(solution)/shard_map/ppermute | solution.py:1044
  182.1 36.2 %collective-permute-start.22 = (bf16[128,1024]{1,0:T(8,128)(2,1)S(1)}, bf16[128,1024]{1,0:T(8,128)(2,1)S(1)}, u32[]{:S(2)}, u32[]{:S(2)}) collective-permute-start(bf16[128,1024]{1,0:T(8,128)(2,1)S(1)} %get-tuple-element.130), channel_id=1, source_target_pairs={{0,6},{1,7},{2,0},{3,1},{4,2},{5,3},{6,4},{7,5},{8,14},{9,15},{10,... | collective-permute-start | bytes 786440 | tf_op jit(solution)/shard_map/ppermute | solution.py:1044
  188.4 6.5 %collective-permute-start.51 = (bf16[32,1024]{1,0:T(8,128)(2,1)S(1)}, bf16[32,1024]{1,0:T(8,128)(2,1)S(1)}, u32[]{:S(2)}, u32[]{:S(2)}) collective-permute-start(bf16[32,1024]{1,0:T(8,128)(2,1)S(1)} %get-tuple-element.176), channel_id=1, source_target_pairs={{0,2},{1,3},{2,0},{3,1},{4,6},{5,7},{6,4},{7,5},{8,10},{9,11},{10,... | collective-permute-start | bytes 196616 | tf_op jit(solution)/shard_map/ppermute | solution.py:1044
  191.0 9.8 %collective-permute-start.53 = (bf16[32,1024]{1,0:T(8,128)(2,1)S(1)}, bf16[32,1024]{1,0:T(8,128)(2,1)S(1)}, u32[]{:S(2)}, u32[]{:S(2)}) collective-permute-start(bf16[32,1024]{1,0:T(8,128)(2,1)S(1)} %get-tuple-element.178), channel_id=1, source_target_pairs={{0,4},{1,5},{2,6},{3,7},{4,0},{5,1},{6,2},{7,3},{8,12},{9,13},{10,... | collective-permute-start | bytes 196616 | tf_op jit(solution)/shard_map/ppermute | solution.py:1044
  194.9 8.5 %collective-permute-start.54 = (bf16[32,1024]{1,0:T(8,128)(2,1)S(1)}, bf16[32,1024]{1,0:T(8,128)(2,1)S(1)}, u32[]{:S(2)}, u32[]{:S(2)}) collective-permute-start(bf16[32,1024]{1,0:T(8,128)(2,1)S(1)} %get-tuple-element.179), channel_id=1, source_target_pairs={{0,5},{1,4},{2,7},{3,6},{4,1},{5,0},{6,3},{7,2},{8,13},{9,12},{10,... | collective-permute-start | bytes 196616 | tf_op jit(solution)/shard_map/ppermute | solution.py:1044
  195.3 9.6 %collective-permute-start.55 = (bf16[32,1024]{1,0:T(8,128)(2,1)S(1)}, bf16[32,1024]{1,0:T(8,128)(2,1)S(1)}, u32[]{:S(2)}, u32[]{:S(2)}) collective-permute-start(bf16[32,1024]{1,0:T(8,128)(2,1)S(1)} %get-tuple-element.180), channel_id=1, source_target_pairs={{0,6},{1,7},{2,4},{3,5},{4,2},{5,3},{6,0},{7,1},{8,14},{9,15},{10,... | collective-permute-start | bytes 196616 | tf_op jit(solution)/shard_map/ppermute | solution.py:1044
  200.4 6.9 %collective-permute-start.56 = (bf16[32,1024]{1,0:T(8,128)(2,1)S(1)}, bf16[32,1024]{1,0:T(8,128)(2,1)S(1)}, u32[]{:S(2)}, u32[]{:S(2)}) collective-permute-start(bf16[32,1024]{1,0:T(8,128)(2,1)S(1)} %get-tuple-element.181), channel_id=1, source_target_pairs={{0,7},{1,6},{2,5},{3,4},{4,3},{5,2},{6,1},{7,0},{8,15},{9,14},{10,... | collective-permute-start | bytes 196616 | tf_op jit(solution)/shard_map/ppermute | solution.py:1044
  200.8 35.0 %collective-permute-start.23 = (bf16[128,1024]{1,0:T(8,128)(2,1)S(1)}, bf16[128,1024]{1,0:T(8,128)(2,1)S(1)}, u32[]{:S(2)}, u32[]{:S(2)}) collective-permute-start(bf16[128,1024]{1,0:T(8,128)(2,1)S(1)} %get-tuple-element.131), channel_id=1, source_target_pairs={{0,4},{1,5},{2,6},{3,7},{4,0},{5,1},{6,2},{7,3},{8,12},{9,13},{10,... | collective-permute-start | bytes 786440 | tf_op jit(solution)/shard_map/ppermute | solution.py:1044
  203.5 32.3 %collective-permute-start.24 = (bf16[128,1024]{1,0:T(8,128)(2,1)S(1)}, bf16[128,1024]{1,0:T(8,128)(2,1)S(1)}, u32[]{:S(2)}, u32[]{:S(2)}) collective-permute-start(bf16[128,1024]{1,0:T(8,128)(2,1)S(1)} %get-tuple-element.132), channel_id=1, source_target_pairs={{0,2},{1,3},{2,4},{3,5},{4,6},{5,7},{6,0},{7,1},{8,10},{9,11},{10,... | collective-permute-start | bytes 786440 | tf_op jit(solution)/shard_map/ppermute | solution.py:1044
  204.9 32.0 %collective-permute-start.33 = (bf16[128,1024]{1,0:T(8,128)(2,1)S(1)}, bf16[128,1024]{1,0:T(8,128)(2,1)S(1)}, u32[]{:S(2)}, u32[]{:S(2)}) collective-permute-start(bf16[128,1024]{1,0:T(8,128)(2,1)S(1)} %get-tuple-element.150), channel_id=1, source_target_pairs={{0,6},{1,7},{2,0},{3,1},{4,2},{5,3},{6,4},{7,5},{8,14},{9,15},{10,... | collective-permute-start | bytes 786440 | tf_op jit(solution)/shard_map/ppermute | solution.py:1044
  207.3 41.1 %collective-permute-start.34 = (bf16[128,1024]{1,0:T(8,128)(2,1)S(1)}, bf16[128,1024]{1,0:T(8,128)(2,1)S(1)}, u32[]{:S(2)}, u32[]{:S(2)}) collective-permute-start(bf16[128,1024]{1,0:T(8,128)(2,1)S(1)} %get-tuple-element.151), channel_id=1, source_target_pairs={{0,4},{1,5},{2,6},{3,7},{4,0},{5,1},{6,2},{7,3},{8,12},{9,13},{10,... | collective-permute-start | bytes 786440 | tf_op jit(solution)/shard_map/ppermute | solution.py:1044
  218.3 30.1 %collective-permute-start.35 = (bf16[128,1024]{1,0:T(8,128)(2,1)S(1)}, bf16[128,1024]{1,0:T(8,128)(2,1)S(1)}, u32[]{:S(2)}, u32[]{:S(2)}) collective-permute-start(bf16[128,1024]{1,0:T(8,128)(2,1)S(1)} %get-tuple-element.152), channel_id=1, source_target_pairs={{0,2},{1,3},{2,4},{3,5},{4,6},{5,7},{6,0},{7,1},{8,10},{9,11},{10,... | collective-permute-start | bytes 786440 | tf_op jit(solution)/shard_map/ppermute | solution.py:1044
  235.8 20.2 %collective-permute-start.42 = (bf16[32,512]{1,0:T(8,128)(2,1)S(1)}, bf16[32,512]{1,0:T(8,128)(2,1)S(1)}, u32[]{:S(2)}, u32[]{:S(2)}) collective-permute-start(bf16[32,512]{1,0:T(8,128)(2,1)S(1)} %get-tuple-element.166), channel_id=1, source_target_pairs={{0,3},{1,2},{2,1},{3,0},{4,7},{5,6},{6,5},{7,4},{8,11},{9,10},{10,... | collective-permute-start | bytes 98312 | tf_op jit(solution)/shard_map/ppermute | solution.py:1044
  235.8 20.2 %collective-permute-start.43 = (bf16[32,512]{1,0:T(8,128)(2,1)S(1)}, bf16[32,512]{1,0:T(8,128)(2,1)S(1)}, u32[]{:S(2)}, u32[]{:S(2)}) collective-permute-start(bf16[32,512]{1,0:T(8,128)(2,1)S(1)} %get-tuple-element.167), channel_id=1, source_target_pairs={{0,4},{1,5},{2,6},{3,7},{4,0},{5,1},{6,2},{7,3},{8,12},{9,13},{10,... | collective-permute-start | bytes 98312 | tf_op jit(solution)/shard_map/ppermute | solution.py:1044
  236.9 19.0 %collective-permute-start.44 = (bf16[32,512]{1,0:T(8,128)(2,1)S(1)}, bf16[32,512]{1,0:T(8,128)(2,1)S(1)}, u32[]{:S(2)}, u32[]{:S(2)}) collective-permute-start(bf16[32,512]{1,0:T(8,128)(2,1)S(1)} %get-tuple-element.168), channel_id=1, source_target_pairs={{0,5},{1,4},{2,7},{3,6},{4,1},{5,0},{6,3},{7,2},{8,13},{9,12},{10,... | collective-permute-start | bytes 98312 | tf_op jit(solution)/shard_map/ppermute | solution.py:1044
  248.4 7.6 %collective-permute-start.45 = (bf16[32,512]{1,0:T(8,128)(2,1)S(1)}, bf16[32,512]{1,0:T(8,128)(2,1)S(1)}, u32[]{:S(2)}, u32[]{:S(2)}) collective-permute-start(bf16[32,512]{1,0:T(8,128)(2,1)S(1)} %get-tuple-element.169), channel_id=1, source_target_pairs={{0,6},{1,7},{2,4},{3,5},{4,2},{5,3},{6,0},{7,1},{8,14},{9,15},{10,... | collective-permute-start | bytes 98312 | tf_op jit(solution)/shard_map/ppermute | solution.py:1044
  248.4 7.6 %collective-permute-start.46 = (bf16[32,512]{1,0:T(8,128)(2,1)S(1)}, bf16[32,512]{1,0:T(8,128)(2,1)S(1)}, u32[]{:S(2)}, u32[]{:S(2)}) collective-permute-start(bf16[32,512]{1,0:T(8,128)(2,1)S(1)} %get-tuple-element.170), channel_id=1, source_target_pairs={{0,7},{1,6},{2,5},{3,4},{4,3},{5,2},{6,1},{7,0},{8,15},{9,14},{10,... | collective-permute-start | bytes 98312 | tf_op jit(solution)/shard_map/ppermute | solution.py:1044
  (13 other events, 207.2 us)
